TPU v7x, 128 devices: a whole 4x4x4 slice. The times are simulated.
128 devices in a mesh: row: 32 (over z, x, core), grp: 4 (over y).
Axes of the slice: x: 4, y: 4, z: 4, core: 2. Of those that a mesh axis runs over, the one named last changes fastest.
Arguments:
- features: bfloat16 [262144, 768], P(('row', 'grp')), may hold values from -6 to 6
- dense_edge_weights: bfloat16 [1024, 4, 256, 256], P(('row', 'grp')), may hold values from -0.125 to 0.125
- dense_cols: int32 [1024, 4], P(('row', 'grp')), may hold values from 0 to 7
- dense_ids: int32 [8], replicated, may hold values from 0 to 1023, as said below
- sparse_w: bfloat16 [262144, 1024], P(('row', 'grp')), may hold values from -0.125 to 0.125
- sparse_rows: int32 [128, 128, 8], P(('row', 'grp')), may hold values from 0 to 2047, as said below
- sparse_counts: int32 [128, 128], P(('row', 'grp')), may hold values from 1 to 8, as said below
- weight: bfloat16 [768, 768], replicated, may hold values from -0.21875 to 0.21875
- bias: float32 [768], replicated, may hold values from -3 to 3
Outputs:
- output: bfloat16 [262144, 768], P(('row', 'grp'))
Inputs may be any that keep to these rules, and one draw needn't show every extreme that they name: `dense_ids`: distinct row block ids; the first and the last row block are both among them. `sparse_rows`: local row indices of the sender. `sparse_counts`: at most 8 rows from one sender to one receiver; one receiver gets 8 rows from every sender.
All inputs are finite; a program needn't handle non-finite values.
Results may differ from a plain program's by a relative error of at most 0.0044.
Values may be sent and summed in bfloat16 or wider, within the bound.
A program may use at most 128 MiB of HBM per device.

v0:
```python
import jax
import jax.numpy as jnp
from jax import lax
from jax.sharding import PartitionSpec as P


def from_root(x, axis, root):
    mine = lax.axis_index(axis) == root
    return lax.psum(jnp.where(mine, x, jnp.zeros_like(x)), axis)


def on_device(
    features,
    dense_edge_weights,
    dense_cols,
    dense_ids,
    sparse_w,
    sparse_rows,
    sparse_counts,
    weight,
    bias,
):
    block_count = dense_edge_weights.shape[0]
    tiles_per = dense_edge_weights.shape[1]
    tile_size = dense_edge_weights.shape[2]
    feature_width = features.shape[1]
    stripe_count = dense_ids.shape[0]
    local_blocks = features.reshape(block_count, tile_size, feature_width)

    def fetch_stripe(index, dense_bands):
        global_id = dense_ids[index]
        owner = global_id // block_count
        candidate = lax.dynamic_index_in_dim(
            local_blocks, global_id % block_count, 0, keepdims=False
        )
        arrived = from_root(candidate, ("row", "grp"), owner)
        return lax.dynamic_update_index_in_dim(dense_bands, arrived, index, 0)

    empty_stripes = jnp.zeros((stripe_count, tile_size, feature_width), jnp.bfloat16)
    dense_bands = lax.fori_loop(0, stripe_count, fetch_stripe, empty_stripes)
    dense_sum = jnp.zeros((block_count, tile_size, feature_width), jnp.float32)
    for tile_index in range(tiles_per):
        picked_tiles = dense_bands[dense_cols[:, tile_index]]
        dense_sum = dense_sum + jnp.einsum(
            "eim,emh->eih",
            dense_edge_weights[:, tile_index],
            picked_tiles,
            preferred_element_type=jnp.float32,
        )
    rows_out = sparse_rows[0]
    counts_out = sparse_counts[0]
    peer_count = rows_out.shape[0]
    slot_count = rows_out.shape[1]
    outgoing = features[rows_out]
    slot_ids = jnp.arange(slot_count, dtype=jnp.int32)
    live_slots = slot_ids[None, :] < counts_out[:, None]
    outgoing = jnp.where(live_slots[:, :, None], outgoing, jnp.zeros((), outgoing.dtype))
    arrived_rows = lax.all_to_all(outgoing, ("row", "grp"), split_axis=0, concat_axis=0, tiled=True)
    incoming_rows = arrived_rows.reshape(peer_count * slot_count, feature_width)
    sparse_sum = jnp.dot(sparse_w, incoming_rows, preferred_element_type=jnp.float32)
    aggregate = (dense_sum.reshape(block_count * tile_size, feature_width) + sparse_sum).astype(
        jnp.bfloat16
    )
    result = jnp.dot(aggregate, weight, preferred_element_type=jnp.float32) + bias
    return jnp.maximum(result, 0.0).astype(jnp.bfloat16)


def solution(mesh):
    placed = (
        P(("row", "grp"), None),
        P(("row", "grp"), None, None, None),
        P(("row", "grp"), None),
        P(),
        P(("row", "grp"), None),
        P(("row", "grp"), None, None),
        P(("row", "grp"), None),
        P(),
        P(),
    )
    return jax.shard_map(
        on_device, mesh=mesh, in_specs=placed, out_specs=P(("row", "grp"), None), check_vma=False
    )
```

profile of v0, /device:TPU:1, one launch (start us, length us, event | category | flops | bytes accessed | tf_op | source)
XLA Modules:
  0.0 1288.7 jit_solution(11461242823182639601)
XLA Ops:
  8.3 6.8 gather_fusion.4
  16.5 11.9 all-to-all-start
  28.4 1201.3 %while.15 = (s32[]{:T(128)}, bf16[8,256,768]{2,1,0:T(8,128)(2,1)}, s32[8]{0:T(128)S(1)}, bf16[8,256,768]{2,1,0:T(8,128)(2,1)}, s32[]{:T(128)}, /*index=5*/s32[]{...) while((s32[]{:T(128)}, bf16[8,256,768]{2,1,0:T(8,128)(2,1)}, ...), condition=%wide.region_2.3_spmd, body=%wide.region_0.2_spmd.sunk | while | flops 393248 | bytes 3932668 | solution.py:40
  31.7 1.8 dynamic-slice_select_fusion.2
  33.5 147.3 %all-reduce.2.cloned.1.call-done = bf16[1,256,768]{2,1,0:T(8,128)(2,1)} async-done(((bf16[1,256,768]{2,1,0:T(8,128)(2,1)}), bf16[1,256,768]{2,1,0:T(8,128)(2,1)}) %all-reduce.2.cloned.1.call-update) | async-done | bytes 393232 | tf_op jit(solution)/shard_map/while/body/eval_jaxpr/psum | solution.py:9
  185.8 1.8 dynamic-slice_select_fusion.2
  187.6 143.0 %all-reduce.2.cloned.1.call-done = bf16[1,256,768]{2,1,0:T(8,128)(2,1)} async-done(((bf16[1,256,768]{2,1,0:T(8,128)(2,1)}), bf16[1,256,768]{2,1,0:T(8,128)(2,1)}) %all-reduce.2.cloned.1.call-update) | async-done | bytes 393232 | tf_op jit(solution)/shard_map/while/body/eval_jaxpr/psum | solution.py:9
  330.6 1.8 constant_dynamic-update-slice_fusion.2
  335.5 1.8 dynamic-slice_select_fusion.2
  337.3 143.0 %all-reduce.2.cloned.1.call-done = bf16[1,256,768]{2,1,0:T(8,128)(2,1)} async-done(((bf16[1,256,768]{2,1,0:T(8,128)(2,1)}), bf16[1,256,768]{2,1,0:T(8,128)(2,1)}) %all-reduce.2.cloned.1.call-update) | async-done | bytes 393232 | tf_op jit(solution)/shard_map/while/body/eval_jaxpr/psum | solution.py:9
  485.2 1.8 dynamic-slice_select_fusion.2
  487.0 142.6 %all-reduce.2.cloned.1.call-done = bf16[1,256,768]{2,1,0:T(8,128)(2,1)} async-done(((bf16[1,256,768]{2,1,0:T(8,128)(2,1)}), bf16[1,256,768]{2,1,0:T(8,128)(2,1)}) %all-reduce.2.cloned.1.call-update) | async-done | bytes 393232 | tf_op jit(solution)/shard_map/while/body/eval_jaxpr/psum | solution.py:9
  629.7 1.8 constant_dynamic-update-slice_fusion.2
  634.6 1.8 dynamic-slice_select_fusion.2
  636.4 142.7 %all-reduce.2.cloned.1.call-done = bf16[1,256,768]{2,1,0:T(8,128)(2,1)} async-done(((bf16[1,256,768]{2,1,0:T(8,128)(2,1)}), bf16[1,256,768]{2,1,0:T(8,128)(2,1)}) %all-reduce.2.cloned.1.call-update) | async-done | bytes 393232 | tf_op jit(solution)/shard_map/while/body/eval_jaxpr/psum | solution.py:9
  784.0 1.8 dynamic-slice_select_fusion.2
  785.8 142.6 %all-reduce.2.cloned.1.call-done = bf16[1,256,768]{2,1,0:T(8,128)(2,1)} async-done(((bf16[1,256,768]{2,1,0:T(8,128)(2,1)}), bf16[1,256,768]{2,1,0:T(8,128)(2,1)}) %all-reduce.2.cloned.1.call-update) | async-done | bytes 393232 | tf_op jit(solution)/shard_map/while/body/eval_jaxpr/psum | solution.py:9
  933.4 1.8 dynamic-slice_select_fusion.2
  935.2 143.0 %all-reduce.2.cloned.1.call-done = bf16[1,256,768]{2,1,0:T(8,128)(2,1)} async-done(((bf16[1,256,768]{2,1,0:T(8,128)(2,1)}), bf16[1,256,768]{2,1,0:T(8,128)(2,1)}) %all-reduce.2.cloned.1.call-update) | async-done | bytes 393232 | tf_op jit(solution)/shard_map/while/body/eval_jaxpr/psum | solution.py:9
  1083.2 1.8 dynamic-slice_select_fusion.2
  1085.0 143.0 %all-reduce.2.cloned.1.call-done = bf16[1,256,768]{2,1,0:T(8,128)(2,1)} async-done(((bf16[1,256,768]{2,1,0:T(8,128)(2,1)}), bf16[1,256,768]{2,1,0:T(8,128)(2,1)}) %all-reduce.2.cloned.1.call-update) | async-done | bytes 393232 | tf_op jit(solution)/shard_map/while/body/eval_jaxpr/psum | solution.py:9
  1229.7 4.3 gather_fusion.1
  1234.0 4.3 gather_fusion
  1238.3 6.0 fusion.5
  1244.4 4.8 fusion.7
  1249.2 4.3 gather_fusion.2
  1253.5 4.4 gather_fusion.3
  1257.9 3.3 fusion.3
  1261.3 1.9 slice-done.1
  1263.2 6.7 add_add_fusion
  1269.9 7.9 fusion
  1277.9 4.0 maximum_convert_fusion
  (57 shorter events, 18.8 us)
Async XLA Ops:
  6.5 1271.3 %copy-start = (bf16[768,768]{1,0:T(8,128)(2,1)S(1)}, bf16[768,768]{1,0:T(8,128)(2,1)}, u32[]{:S(2)}) copy-start(bf16[768,768]{1,0:T(8,128)(2,1)} %param.18) | copy-start | bytes 3538948
  15.1 13.3 %copy-start.3 = (s32[8,4]{0,1:T(4,128)S(1)}, s32[8,4]{0,1:T(4,128)}, u32[]{:S(2)}) copy-start(s32[8,4]{0,1:T(4,128)} %param.13) | copy-start | bytes 388
  15.1 13.3 %copy-start.5 = (s32[8]{0:T(128)S(1)}, s32[8]{0:T(128)}, u32[]{:S(2)}) copy-start(s32[8]{0:T(128)} %param.14) | copy-start | bytes 100
  16.5 1253.5 %all-to-all-start = ((bf16[128,8,768]{2,1,0:T(8,128)(2,1)}), bf16[128,8,768]{2,1,0:T(8,128)(2,1)}, u32[]{:S(2)}, u32[]{:S(2)}) async-start(bf16[128,8,768]{2,1,0:T(8,128)(2,1)} %bitcast_select_fusion), calls=%async_computation | async-start | bytes 3145728 | tf_op jit(solution)/shard_map/all_to_all | solution.py:58
  28.4 152.4 %all-reduce.2.cloned.1.call-start = ((), (), s32[]{:S(2)}) async-start(), calls=%async_computation.1 | async-start | bytes 786432 | tf_op jit(solution)/shard_map/while/body/eval_jaxpr/psum | solution.py:9
  182.6 148.0 %all-reduce.2.cloned.1.call-start = ((), (), s32[]{:S(2)}) async-start(), calls=%async_computation.1 | async-start | bytes 786432 | tf_op jit(solution)/shard_map/while/body/eval_jaxpr/psum | solution.py:9
  332.3 147.9 %all-reduce.2.cloned.1.call-start = ((), (), s32[]{:S(2)}) async-start(), calls=%async_computation.1 | async-start | bytes 786432 | tf_op jit(solution)/shard_map/while/body/eval_jaxpr/psum | solution.py:9
  482.0 147.6 %all-reduce.2.cloned.1.call-start = ((), (), s32[]{:S(2)}) async-start(), calls=%async_computation.1 | async-start | bytes 786432 | tf_op jit(solution)/shard_map/while/body/eval_jaxpr/psum | solution.py:9
  631.4 147.6 %all-reduce.2.cloned.1.call-start = ((), (), s32[]{:S(2)}) async-start(), calls=%async_computation.1 | async-start | bytes 786432 | tf_op jit(solution)/shard_map/while/body/eval_jaxpr/psum | solution.py:9
  780.8 147.6 %all-reduce.2.cloned.1.call-start = ((), (), s32[]{:S(2)}) async-start(), calls=%async_computation.1 | async-start | bytes 786432 | tf_op jit(solution)/shard_map/while/body/eval_jaxpr/psum | solution.py:9
  930.2 148.0 %all-reduce.2.cloned.1.call-start = ((), (), s32[]{:S(2)}) async-start(), calls=%async_computation.1 | async-start | bytes 786432 | tf_op jit(solution)/shard_map/while/body/eval_jaxpr/psum | solution.py:9
  1080.0 148.0 %all-reduce.2.cloned.1.call-start = ((), (), s32[]{:S(2)}) async-start(), calls=%async_computation.1 | async-start | bytes 786432 | tf_op jit(solution)/shard_map/while/body/eval_jaxpr/psum | solution.py:9
  1238.3 6.0 copy-start.2
  1253.5 7.8 slice-start
  1257.9 5.3 slice-start.1
  1257.9 5.3 copy-start.1
  1269.9 8.0 copy-start.4
Sparse Core Ops, SparseCore 0:
  34.0 146.8 all-reduce.1
  188.1 142.3 all-reduce.1
  337.8 142.3 all-reduce.1
  487.2 142.3 all-reduce.1
  636.6 142.3 all-reduce.1
  786.0 142.3 all-reduce.1
  935.8 142.3 all-reduce.1
  1085.5 142.3 all-reduce.1
where the time goes:
time: 1290 us
  waiting for transfers between devices  1150 us (89%)
  local copies, waits for them, and re-layouts  45.2 us (4%)
  matrix products  32.9 us (3%)
  loops' own time  20.7 us (2%)
  other arithmetic  17.2 us (1%)
  between operations  13.5 us (1%)
    psum x8, waiting for transfers between devices, from_root(): return lax.psum(jnp.where(mine, x, jnp.zeros_like(x)), axis)  1150 us
  transfers between devices with their start and end apart: 9, of which 8 were waited for; matrix products, arithmetic and copies ran while one was open for 6% of the time, Pallas kernels for 0%

commit v1 on v0

v1 whole, which is shorter than its diff:
```python
import jax
import jax.numpy as jnp
from jax import lax
from jax.sharding import PartitionSpec as P

AXES = ("row", "grp")


def on_device(
    features,
    dense_edge_weights,
    dense_cols,
    dense_ids,
    sparse_w,
    sparse_rows,
    sparse_counts,
    weight,
    bias,
):
    block_count = dense_edge_weights.shape[0]
    tiles_per = dense_edge_weights.shape[1]
    tile_size = dense_edge_weights.shape[2]
    feature_width = features.shape[1]
    stripe_count = dense_ids.shape[0]
    local_blocks = features.reshape(block_count, tile_size, feature_width)

    rows_out = sparse_rows[0]
    counts_out = sparse_counts[0]
    peer_count = rows_out.shape[0]
    slot_count = rows_out.shape[1]
    piece = tile_size // peer_count
    me = lax.axis_index(AXES)

    owners = dense_ids // block_count
    mine = owners == me
    candidates = local_blocks[dense_ids % block_count]
    candidates = jnp.where(mine[:, None, None], candidates, jnp.zeros((), candidates.dtype))
    stripe_pieces = candidates.reshape(stripe_count, peer_count, piece, feature_width)
    stripe_pieces = jnp.transpose(stripe_pieces, (1, 0, 2, 3)).reshape(
        peer_count, stripe_count * piece, feature_width
    )

    outgoing = features[rows_out]
    slot_ids = jnp.arange(slot_count, dtype=jnp.int32)
    live_slots = slot_ids[None, :] < counts_out[:, None]
    outgoing = jnp.where(live_slots[:, :, None], outgoing, jnp.zeros((), outgoing.dtype))
    payload = jnp.concatenate([outgoing, stripe_pieces], axis=1)
    arrived = lax.all_to_all(payload, AXES, split_axis=0, concat_axis=0, tiled=True)
    incoming_rows = arrived[:, :slot_count].reshape(peer_count * slot_count, feature_width)
    my_pieces = jnp.sum(arrived[:, slot_count:].astype(jnp.float32), axis=0).astype(jnp.bfloat16)
    gathered = lax.all_gather(my_pieces, AXES, axis=0, tiled=False)
    dense_bands = jnp.transpose(
        gathered.reshape(peer_count, stripe_count, piece, feature_width), (1, 0, 2, 3)
    ).reshape(stripe_count, tile_size, feature_width)

    dense_sum = jnp.zeros((block_count, tile_size, feature_width), jnp.float32)
    for tile_index in range(tiles_per):
        picked_tiles = dense_bands[dense_cols[:, tile_index]]
        dense_sum = dense_sum + jnp.einsum(
            "eim,emh->eih",
            dense_edge_weights[:, tile_index],
            picked_tiles,
            preferred_element_type=jnp.float32,
        )
    sparse_sum = jnp.dot(sparse_w, incoming_rows, preferred_element_type=jnp.float32)
    aggregate = (dense_sum.reshape(block_count * tile_size, feature_width) + sparse_sum).astype(
        jnp.bfloat16
    )
    result = jnp.dot(aggregate, weight, preferred_element_type=jnp.float32) + bias
    return jnp.maximum(result, 0.0).astype(jnp.bfloat16)


def solution(mesh):
    placed = (
        P(AXES, None),
        P(AXES, None, None, None),
        P(AXES, None),
        P(),
        P(AXES, None),
        P(AXES, None, None),
        P(AXES, None),
        P(),
        P(),
    )
    return jax.shard_map(
        on_device, mesh=mesh, in_specs=placed, out_specs=P(AXES, None), check_vma=False
    )
```

time: 1290 us -> 218 us (0.17)
  waiting for transfers between devices: 1150 us -> 62.1 us
  blocking collectives: 0 us -> 70 us
  loops' own time: 20.7 us -> 0 us
    psum x8 -> x0, waiting for transfers between devices: 1150 us -> none  [from_root(): return lax.psum(jnp.where(mine, x, jnp.zeros_like(x)), axis)]
    all_to_all x0 -> x1, blocking collectives: none -> 70 us  [on_device(): lax.all_to_all(payload, AXES, split_axis=0, concat_axis=0, tiled=True)]
    all_gather x0 -> x1, waiting for transfers between devices: none -> 62.1 us  [on_device(): gathered = lax.all_gather(my_pieces, AXES, axis=0, tiled=False)]
    another operation x1 -> x0, loops' own time: 20.7 us -> none  [on_device(): dense_bands = lax.fori_loop(0, stripe_count, fetch_stripe, empty_stripes)]
    dynamic_update_slice x8 -> x0, local copies, waits for them, and re-layouts: 14.1 us -> none  [fetch_stripe(): return lax.dynamic_update_index_in_dim(dense_bands, arrived, index, 0)]
    select_n x8 -> x1, other arithmetic: 14.2 us -> 0.81 us  [on_device(): candidates = local_blocks[dense_ids % block_count]]
    reshape x0 -> x3, local copies, waits for them, and re-layouts: none -> 13.2 us  [the longest x1 6.56 us: on_device(): dense_sum.reshape(block_count * tile_size, feature_width) + sparse_sum]
  transfers between devices with their start and end apart: 9 -> 1, of which waited for: 8 -> 1; matrix products, arithmetic and copies ran while one was open for 6% -> 0% of each run, Pallas kernels for 0% -> 0%
where the time goes in v1:
time: 218 us; the launch traced here: 217 us
  blocking collectives  70 us (32%)
  waiting for transfers between devices  62.1 us (28%)
  local copies, waits for them, and re-layouts  43.9 us (20%)
  matrix products  22.1 us (10%)
  between operations  13.5 us (6%)
  other arithmetic  5.4 us (2%)
    all_to_all x1, blocking collectives, on_device(): lax.all_to_all(payload, AXES, split_axis=0, concat_axis=0, tiled=True)  70 us
    all_gather x1, waiting for transfers between devices, on_device(): gathered = lax.all_gather(my_pieces, AXES, axis=0, tiled=False)  62.1 us
    dot_general x1, matrix products, on_device(): jnp.dot(aggregate, weight, preferred_element_type=jnp.float32) + bias  11.2 us
    dot_general x4, matrix products, on_device(): jnp.einsum('eim,emh->eih', dense_edge_weights[:, tile_index], picked_tile...  10.9 us
    gather x4, local copies, waits for them, and re-layouts, on_device(): picked_tiles = dense_bands[dense_cols[:, tile_index]]  9.67 us
    reshape x1, local copies, waits for them, and re-layouts, on_device(): dense_sum.reshape(block_count * tile_size, feature_width) + sparse_sum  6.56 us
    reshape x1, local copies, waits for them, and re-layouts, on_device(): gathered.reshape(peer_count, stripe_count, piece, feature_width)  6.08 us
    gather x2, local copies, waits for them, and re-layouts, on_device(): candidates = local_blocks[dense_ids % block_count]  6.04 us
  transfers between devices with their start and end apart: 1, of which 1 were waited for; matrix products, arithmetic and copies ran while one was open for 0% of the time, Pallas kernels for 0%

profile of v1, /device:TPU:1, one launch (start us, length us, event | category | flops | bytes accessed | tf_op | source)
XLA Modules:
  0.0 217.1 jit_solution(9380956447041158163)
XLA Ops:
  6.5 0.8 compare_select_fusion.5
  7.4 0.8 fusion.16
  8.2 0.7 iota_compare_fusion
  8.8 0.7 compare_select_fusion
  9.7 5.2 %gather_fusion = bf16[1024,768]{1,0:T(8,128)(2,1)} fusion(bf16[2048,768]{1,0:T(8,128)(2,1)S(1)} %copy-done, s32[1024]{0:T(1024)S(1)} %broadcast_clamp_fusion), kind=kCustom, calls=%fused_computation | custom fusion | bytes 3149824 | tf_op jit(solution)/shard_map/gather | solution.py:43
  15.0 2.4 %gather_fusion.1 = bf16[8,256,768]{2,1,0:T(8,128)(2,1)} fusion(bf16[8,256,768]{2,1,0:T(8,128)(2,1)S(1)} %bitcast.61, s32[1024]{0:T(1024)S(1)} %pad_clamp_fusion.4), kind=kCustom, calls=%fused_computation.1 | custom fusion | bytes 6291488 | tf_op jit(solution)/shard_map/gather | solution.py:36
  17.4 3.6 %copy.55 = bf16[8,256,768]{2,0,1:T(8,128)(2,1)S(1)} copy(bf16[8,256,768]{2,1,0:T(8,128)(2,1)} %gather_fusion.1) | data formatting | bytes 6291456 | tf_op jit(solution)/shard_map/gather | solution.py:36
  21.3 1.0 copy.56
  22.3 0.4 copy-done.6
  22.7 0.6 copy_select_fusion
  23.3 0.4 pad_maximum_fusion
  23.7 2.6 %copy.57 = bf16[128,24,768]{2,1,0:T(8,128)(2,1)S(1)} copy(bf16[128,24,768]{2,0,1:T(8,128)(2,1)S(1)} %pad_maximum_fusion) | data formatting | bytes 9437184 | tf_op jit(solution)/shard_map/concatenate | solution.py:47
  26.3 70.0 %all_to_all.5 = bf16[128,24,768]{2,1,0:T(8,128)(2,1)S(1)} all-to-all(bf16[128,24,768]{2,1,0:T(8,128)(2,1)S(1)} %copy.57), channel_id=1, replica_groups=mesh['row'=32,'grp'=4] {'row','grp'}, dimensions={0} | all-to-all | bytes 9437184 | tf_op jit(solution)/shard_map/all_to_all | solution.py:48
  96.3 2.1 copy-done.2
  98.4 1.1 slice_reduce_fusion
  99.6 62.1 %all-gather.3.cloned.1.call-done = bf16[2048,768]{1,0:T(8,128)(2,1)} async-done(((bf16[16,768]{1,0:T(8,128)(2,1)}), bf16[2048,768]{1,0:T(8,128)(2,1)}) %all-gather.3.cloned.1.call-update) | async-done | bytes 3145744 | tf_op jit(solution)/shard_map/all_gather | solution.py:51
  161.7 6.1 %reshape.76 = bf16[128,8,2,768]{3,2,1,0:T(2,128)(2,1)S(1)} reshape(bf16[2048,768]{1,0:T(8,128)(2,1)} %all-gather.3.cloned.1.call-done) | data formatting | bytes 6291456 | tf_op jit(solution)/shard_map/reshape | solution.py:53
  167.8 0.6 copy.58
  168.4 0.6 copy.59
  169.0 2.4 %gather_fusion.5 = bf16[8,256,768]{2,1,0:T(8,128)(2,1)} fusion(bf16[8,256,768]{2,1,0:T(8,128)(2,1)S(1)} %copy.59, s32[1024]{0:T(1024)S(1)} %get-tuple-element.9), kind=kCustom, calls=%fused_computation.5 | custom fusion | bytes 6291488 | tf_op jit(solution)/shard_map/gather | solution.py:58
  171.4 2.4 %gather_fusion.4 = bf16[8,256,768]{2,1,0:T(8,128)(2,1)} fusion(bf16[8,256,768]{2,1,0:T(8,128)(2,1)S(1)} %copy.59, s32[1024]{0:T(1024)S(1)} %get-tuple-element.10), kind=kCustom, calls=%fused_computation.4 | custom fusion | bytes 6291488 | tf_op jit(solution)/shard_map/gather | solution.py:58
  173.8 2.4 %gather_fusion.3 = bf16[8,256,768]{2,1,0:T(8,128)(2,1)} fusion(bf16[8,256,768]{2,1,0:T(8,128)(2,1)S(1)} %copy.59, s32[1024]{0:T(1024)S(1)} %get-tuple-element.11), kind=kCustom, calls=%fused_computation.3 | custom fusion | bytes 6291488 | tf_op jit(solution)/shard_map/gather | solution.py:58
  176.2 2.5 %gather_fusion.2 = bf16[8,256,768]{2,1,0:T(8,128)(2,1)} fusion(bf16[8,256,768]{2,1,0:T(8,128)(2,1)S(1)} %copy.59, s32[1024]{0:T(1024)S(1)} %get-tuple-element.12), kind=kCustom, calls=%fused_computation.2 | custom fusion | bytes 6291488 | tf_op jit(solution)/shard_map/gather | solution.py:58
  178.7 3.3 %fusion.6 = f32[8,768,256]{1,2,0:T(8,128)S(1)} fusion(bf16[8,256,768]{2,1,0:T(8,128)(2,1)} %gather_fusion.2, bf16[8,4,256,256]{3,2,1,0:T(8,128)(2,1)} %param.10), kind=kOutput, calls=%fused_computation.20 | convolution fusion | flops 805306368 | bytes 10485760 | tf_op jit(solution)/shard_map/eim,emh->eih/dot_general | solution.py:59
  182.0 1.1 copy-done.7
  183.1 1.0 fusion.4
  184.1 0.9 copy-done.4
  185.0 1.0 fusion.2
  186.0 0.9 copy-done.3
  186.9 5.6 %add_add_fusion = f32[8,768,256]{1,2,0:T(8,128)} fusion(f32[8,768,256]{1,2,0:T(8,128)S(1)} %fusion.2, f32[8,768,256]{1,2,0:T(8,128)S(1)} %fusion.6, f32[8,768,256]{1,2,0:T(8,128)S(1)} %fusion.4, bf16[8,256,768]{2,1,0:T(8,128)(2,1)S(1)} %copy-done.3, bf16[8,4,256,256]{3,2,1,0:T(8,128)(2,1)} %param.10), kind=kOutput, calls=%fused_computation.9 | convolution fusion | flops 810024960 | bytes 29360128 | tf_op jit(solution)/shard_map/eim,emh->eih/dot_general | solution.py:59
  192.5 6.6 %copy.67 = f32[2048,768]{0,1:T(8,128)} copy(f32[2048,768]{1,0:T(8,128)} %bitcast.62) | data formatting | bytes 12582912 | tf_op jit(solution)/shard_map/reshape | solution.py:66
  199.0 11.2 %maximum_convert_fusion = bf16[2048,768]{1,0:T(8,128)(2,1)} fusion(bf16[768,768]{1,0:T(8,128)(2,1)} %param.16, f32[768]{0:T(1024)S(1)} %copy-done.9, f32[2048,768]{0,1:T(8,128)} %copy.67, bf16[2048,1024]{1,0:T(8,128)(2,1)} %param.13, bf16[128,24,768]{2,1,0:T(8,128)(2,1)} %copy-done.2), kind=kOutput, calls=%fused_computation.8 | convolution fusion | flops 5645008896 | bytes 16387072 | tf_op jit(solution)/shard_map/dot_general | solution.py:69
  (25 shorter events, 0.5 us)
Async XLA Ops:
  6.5 3.2 %copy-start = (bf16[2048,768]{1,0:T(8,128)(2,1)S(1)}, bf16[2048,768]{1,0:T(8,128)(2,1)}, u32[]{:S(2)}) copy-start(bf16[2048,768]{1,0:T(8,128)(2,1)} %param.9) | copy-start | bytes 9437188
  6.5 155.2 %all-gather.3.cloned.1.call-start = ((), (), s32[]{:S(2)}) async-start(), calls=%async_computation.1 | async-start | bytes 3170304 | tf_op jit(solution)/shard_map/all_gather | solution.py:51
  21.3 1.4 copy-start.6
  96.3 2.1 copy-start.2
  98.4 1.1 copy-start.8
  178.7 3.3 %copy-start.5 = (bf16[8,256,768]{2,1,0:T(8,128)(2,1)S(1)}, bf16[8,256,768]{2,1,0:T(8,128)(2,1)}, u32[]{:S(2)}) copy-start(bf16[8,256,768]{2,1,0:T(8,128)(2,1)} %gather_fusion.3) | copy-start | bytes 9437188
  178.7 4.4 %copy-start.7 = (bf16[8,4,256,256]{3,2,1,0:T(8,128)(2,1)S(1)}, bf16[8,4,256,256]{3,2,1,0:T(8,128)(2,1)}, u32[]{:S(2)}) copy-start(bf16[8,4,256,256]{3,2,1,0:T(8,128)(2,1)} %param.10) | copy-start | bytes 12582916
  183.1 1.9 copy-start.4
  185.0 1.9 copy-start.3
  192.5 6.6 %copy-start.9 = (f32[768]{0:T(1024)S(1)}, f32[768]{0:T(1024)}, u32[]{:S(2)}) copy-start(f32[768]{0:T(1024)} %param.17) | copy-start | bytes 9220
  199.0 11.2 %copy-start.1 = (bf16[2048,768]{1,0:T(8,128)(2,1)S(1)}, bf16[2048,768]{1,0:T(8,128)(2,1)}, u32[]{:S(2)}) copy-start(bf16[2048,768]{1,0:T(8,128)(2,1)} %param.9) | copy-start | bytes 9437188
Sparse Core Ops, SparseCore 0:
  99.7 61.9 all-gather.2

commit v2 on v1

--- a/solution.py
+++ b/solution.py
@@ -1,9 +1,79 @@
+import functools
+
 import jax
 import jax.numpy as jnp
 from jax import lax
+from jax.experimental import pallas as pl
+from jax.experimental.pallas import tpu as pltpu
 from jax.sharding import PartitionSpec as P
 
 AXES = ("row", "grp")
+
+
+def gather_kernel(group, piece_ref, out_ref, send_sem, recv_sem, local_sem):
+    n = out_ref.shape[0]
+    me = lax.axis_index(AXES)
+
+    def where(peer):
+        return (peer // group, peer % group)
+
+    barrier = pltpu.get_barrier_semaphore()
+
+    def greet(i, carry):
+        peer = lax.rem(me + i, n)
+        pl.semaphore_signal(barrier, inc=1, device_id=where(peer), device_id_type=pl.DeviceIdType.MESH)
+        return carry
+
+    lax.fori_loop(1, n, greet, 0)
+    pl.semaphore_wait(barrier, n - 1)
+    own = pltpu.make_async_copy(piece_ref, out_ref.at[me], local_sem)
+    own.start()
+
+    def send(i, carry):
+        peer = lax.rem(me + i, n)
+        pltpu.make_async_remote_copy(
+            src_ref=piece_ref,
+            dst_ref=out_ref.at[me],
+            send_sem=send_sem.at[i],
+            recv_sem=recv_sem.at[me],
+            device_id=where(peer),
+            device_id_type=pl.DeviceIdType.MESH,
+        ).start()
+        return carry
+
+    lax.fori_loop(1, n, send, 0)
+
+    def wait(i, carry):
+        peer = lax.rem(me + i, n)
+        source = lax.rem(me + n - i, n)
+        pltpu.make_async_remote_copy(
+            src_ref=piece_ref,
+            dst_ref=out_ref.at[source],
+            send_sem=send_sem.at[i],
+            recv_sem=recv_sem.at[source],
+            device_id=where(peer),
+            device_id_type=pl.DeviceIdType.MESH,
+        ).wait()
+        return carry
+
+    lax.fori_loop(1, n, wait, 0)
+    own.wait()
+
+
+def gather_pieces(piece, n, group):
+    rows, width = piece.shape
+    return pl.pallas_call(
+        functools.partial(gather_kernel, group),
+        out_shape=jax.ShapeDtypeStruct((n, rows, width), piece.dtype),
+        in_specs=[pl.BlockSpec(memory_space=pltpu.VMEM)],
+        out_specs=pl.BlockSpec(memory_space=pltpu.VMEM),
+        scratch_shapes=[
+            pltpu.SemaphoreType.DMA((n,)),
+            pltpu.SemaphoreType.DMA((n,)),
+            pltpu.SemaphoreType.DMA,
+        ],
+        compiler_params=pltpu.CompilerParams(collective_id=0, has_side_effects=True),
+    )(piece)
 
 
 def on_device(
@@ -23,22 +93,20 @@
     feature_width = features.shape[1]
     stripe_count = dense_ids.shape[0]
     local_blocks = features.reshape(block_count, tile_size, feature_width)
+    group = lax.axis_size("grp")
 
     rows_out = sparse_rows[0]
     counts_out = sparse_counts[0]
     peer_count = rows_out.shape[0]
     slot_count = rows_out.shape[1]
-    piece = tile_size // peer_count
+    piece = stripe_count * tile_size // peer_count
     me = lax.axis_index(AXES)
 
     owners = dense_ids // block_count
     mine = owners == me
     candidates = local_blocks[dense_ids % block_count]
     candidates = jnp.where(mine[:, None, None], candidates, jnp.zeros((), candidates.dtype))
-    stripe_pieces = candidates.reshape(stripe_count, peer_count, piece, feature_width)
-    stripe_pieces = jnp.transpose(stripe_pieces, (1, 0, 2, 3)).reshape(
-        peer_count, stripe_count * piece, feature_width
-    )
+    stripe_pieces = candidates.reshape(peer_count, piece, feature_width)
 
     outgoing = features[rows_out]
     slot_ids = jnp.arange(slot_count, dtype=jnp.int32)
@@ -47,11 +115,10 @@
     payload = jnp.concatenate([outgoing, stripe_pieces], axis=1)
     arrived = lax.all_to_all(payload, AXES, split_axis=0, concat_axis=0, tiled=True)
     incoming_rows = arrived[:, :slot_count].reshape(peer_count * slot_count, feature_width)
-    my_pieces = jnp.sum(arrived[:, slot_count:].astype(jnp.float32), axis=0).astype(jnp.bfloat16)
-    gathered = lax.all_gather(my_pieces, AXES, axis=0, tiled=False)
-    dense_bands = jnp.transpose(
-        gathered.reshape(peer_count, stripe_count, piece, feature_width), (1, 0, 2, 3)
-    ).reshape(stripe_count, tile_size, feature_width)
+    my_piece = jnp.sum(arrived[:, slot_count:].astype(jnp.float32), axis=0).astype(jnp.bfloat16)
+    dense_bands = gather_pieces(my_piece, peer_count, group).reshape(
+        stripe_count, tile_size, feature_width
+    )
 
     dense_sum = jnp.zeros((block_count, tile_size, feature_width), jnp.float32)
     for tile_index in range(tiles_per):

time: 218 us -> 191 us (0.88)
  blocking collectives: 70 us -> 0 us
  Pallas kernels: 0 us -> 61.1 us
  local copies, waits for them, and re-layouts: 43.9 us -> 22.7 us
  between operations: 13.5 us -> 0.16 us
  starting transfers between devices: 0.01 us -> 11.9 us
  other arithmetic: 5.4 us -> 13.6 us
  waiting for transfers between devices: 62.1 us -> 58.3 us
    all_to_all x1 -> x0, blocking collectives: 70 us -> none  [on_device(): lax.all_to_all(payload, AXES, split_axis=0, concat_axis=0, tiled=True)]
    all_gather x1 -> x0, waiting for transfers between devices: 62.1 us -> none  [on_device(): gathered = lax.all_gather(my_pieces, AXES, axis=0, tiled=False)]
    pallas_call x0 -> x1, Pallas kernels: none -> 61.1 us  [gather_pieces(): pl.pallas_call(functools.partial(gather_kernel, group), out_shape=jax.Sha...]
    all_to_all x0 -> x1, waiting for transfers between devices: none -> 58.3 us  [on_device(): lax.all_to_all(payload, AXES, split_axis=0, concat_axis=0, tiled=True)]
    reshape x3 -> x0, local copies, waits for them, and re-layouts: 13.2 us -> none  [the longest x1 6.56 us: on_device(): dense_sum.reshape(block_count * tile_size, feature_width) + sparse_sum]
    all_to_all x0 -> x1, starting transfers between devices: none -> 11.9 us  [on_device(): lax.all_to_all(payload, AXES, split_axis=0, concat_axis=0, tiled=True)]
    dot_general x0 -> x1, matrix products: none -> 8.03 us  [on_device(): jnp.dot(sparse_w, incoming_rows, preferred_element_type=jnp.float32)]
    dot_general x1, matrix products: 11.2 us -> 3.98 us  [on_device(): jnp.dot(aggregate, weight, preferred_element_type=jnp.float32) + bias]
where the time goes in v2:
time: 191 us
  Pallas kernels  61.1 us (32%)
  waiting for transfers between devices  58.3 us (31%)
  matrix products  22.9 us (12%)
  local copies, waits for them, and re-layouts  22.7 us (12%)
  other arithmetic  13.6 us (7%)
  starting transfers between devices  11.9 us (6%)
    pallas_call x1, Pallas kernels, gather_pieces(): pl.pallas_call(functools.partial(gather_kernel, group), out_shape=jax.Sha...  61.1 us
    all_to_all x1, waiting for transfers between devices, on_device(): lax.all_to_all(payload, AXES, split_axis=0, concat_axis=0, tiled=True)  58.3 us
    all_to_all x1, starting transfers between devices, on_device(): lax.all_to_all(payload, AXES, split_axis=0, concat_axis=0, tiled=True)  11.9 us
    gather x4, local copies, waits for them, and re-layouts, on_device(): picked_tiles = dense_bands[dense_cols[:, tile_index]]  11.7 us
    dot_general x4, matrix products, on_device(): jnp.einsum('eim,emh->eih', dense_edge_weights[:, tile_index], picked_tile...  10.9 us
    dot_general x1, matrix products, on_device(): jnp.dot(sparse_w, incoming_rows, preferred_element_type=jnp.float32)  8.03 us
    gather x1, local copies, waits for them, and re-layouts, on_device(): outgoing = features[rows_out]  5.21 us
    dot_general x1, matrix products, on_device(): jnp.dot(aggregate, weight, preferred_element_type=jnp.float32) + bias  3.98 us
  transfers between devices with their start and end apart: 1, of which 1 were waited for; matrix products, arithmetic and copies ran while one was open for 0% of the time, Pallas kernels for 0%

profile of v2, /device:TPU:1, one launch (start us, length us, event | category | flops | bytes accessed | tf_op | source)
XLA Modules:
  0.0 190.7 jit_solution(6469466619630503976)
XLA Ops:
  0.0 0.8 compare_select_fusion.5
  0.8 0.8 fusion.16
  1.6 0.1 broadcast_in_dim.42
  1.7 0.1 broadcast_in_dim.43
  1.8 0.7 compare_select_fusion
  2.5 0.7 iota_compare_fusion
  3.2 0.1 copy.14
  3.3 0.1 reshape.75
  3.5 5.2 %gather_fusion = bf16[1024,768]{1,0:T(8,128)(2,1)} fusion(bf16[2048,768]{1,0:T(8,128)(2,1)S(1)} %copy-done, s32[1024]{0:T(1024)S(1)} %broadcast_clamp_fusion), kind=kCustom, calls=%fused_computation | custom fusion | bytes 3149824 | tf_op jit(solution)/shard_map/gather | solution.py:111
  8.7 2.8 %bitcast_select_fusion = bf16[128,8,768]{2,1,0:T(8,128)(2,1)} fusion(bf16[1024,768]{1,0:T(8,128)(2,1)} %gather_fusion, pred[128,8]{1,0:T(8,128)(4,1)S(1)} %iota_compare_fusion), kind=kLoop, calls=%fused_computation.14 | loop fusion | flops 786432 | bytes 3146752 | tf_op jit(solution)/shard_map/jit(_where)/select_n | solution.py:114
  11.4 2.4 %gather_fusion.1 = bf16[8,256,768]{2,1,0:T(8,128)(2,1)} fusion(bf16[8,256,768]{2,1,0:T(8,128)(2,1)S(1)} %bitcast.56, s32[1024]{0:T(1024)S(1)} %pad_clamp_fusion.4), kind=kCustom, calls=%fused_computation.1 | custom fusion | bytes 6291488 | tf_op jit(solution)/shard_map/gather | solution.py:107
  13.9 2.3 %broadcast_select_fusion = bf16[128,16,768]{2,1,0:T(8,128)(2,1)S(1)} fusion(bf16[128,16,768]{2,1,0:T(8,128)(2,1)} %bitcast.61, pred[128]{0:T(512)(128)(4,1)S(1)} %broadcast_in_dim.43), kind=kLoop, calls=%fused_computation.12 | loop fusion | flops 1572864 | bytes 6291584 | tf_op jit(solution)/shard_map/jit(_where)/select_n | solution.py:108
  16.2 0.1 copy-done.6
  16.2 2.4 %pad_maximum_fusion = bf16[128,24,768]{2,1,0:T(8,128)(2,1)} fusion(bf16[128,16,768]{2,1,0:T(8,128)(2,1)S(1)} %broadcast_select_fusion, bf16[128,8,768]{2,1,0:T(8,128)(2,1)S(1)} %copy-done.6), kind=kLoop, calls=%fused_computation.10 | loop fusion | flops 9437184 | bytes 9437184 | tf_op jit(solution)/shard_map/concatenate | solution.py:115
  18.6 11.9 %all-to-all-start = ((bf16[128,24,768]{2,1,0:T(8,128)(2,1)}), bf16[128,24,768]{2,1,0:T(8,128)(2,1)}, u32[]{:S(2)}, u32[]{:S(2)}) async-start(bf16[128,24,768]{2,1,0:T(8,128)(2,1)} %pad_maximum_fusion), calls=%async_computation | async-start | bytes 9437184 | tf_op jit(solution)/shard_map/all_to_all | solution.py:116
  30.6 58.3 %all-to-all-done = bf16[128,24,768]{2,1,0:T(8,128)(2,1)} async-done(((bf16[128,24,768]{2,1,0:T(8,128)(2,1)}), bf16[128,24,768]{2,1,0:T(8,128)(2,1)}, u32[]{:S(2)}, u32[]{:S(2)}) %all-to-all-start) | async-done | bytes 4718624 | tf_op jit(solution)/shard_map/all_to_all | solution.py:116
  89.0 3.0 %slice_reduce_fusion.piece_ref = bf16[16,768]{1,0:T(8,128)(2,1)} fusion(bf16[128,24,768]{2,1,0:T(8,128)(2,1)} %all-to-all-done), kind=kLoop, calls=%fused_computation.11 | loop fusion | flops 1560576 | bytes 3170304 | tf_op jit(solution)/shard_map/reduce_sum | solution.py:118
  92.0 61.1 %shard_map.91 = bf16[128,16,768]{2,1,0:T(8,128)(2,1)} custom-call(bf16[16,768]{1,0:T(8,128)(2,1)} %slice_reduce_fusion.piece_ref), custom_call_target="tpu_custom_call" | custom-call | tf_op jit(solution)/shard_map/pallas_call | solution.py:65
  153.1 4.4 %gather_fusion.5 = bf16[8,256,768]{2,1,0:T(8,128)(2,1)} fusion(bf16[8,256,768]{2,1,0:T(8,128)(2,1)} %bitcast.57, s32[1024]{0:T(1024)S(1)} %get-tuple-element.9), kind=kCustom, calls=%fused_computation.5 | custom fusion | bytes 6291488 | tf_op jit(solution)/shard_map/gather | solution.py:125
  157.5 2.4 %gather_fusion.4 = bf16[8,256,768]{2,1,0:T(8,128)(2,1)} fusion(bf16[8,256,768]{2,1,0:T(8,128)(2,1)S(1)} %bitcast.58, s32[1024]{0:T(1024)S(1)} %get-tuple-element.10), kind=kCustom, calls=%fused_computation.4 | custom fusion | bytes 6291488 | tf_op jit(solution)/shard_map/gather | solution.py:125
  159.9 2.4 %gather_fusion.3 = bf16[8,256,768]{2,1,0:T(8,128)(2,1)} fusion(bf16[8,256,768]{2,1,0:T(8,128)(2,1)S(1)} %bitcast.59, s32[1024]{0:T(1024)S(1)} %get-tuple-element.11), kind=kCustom, calls=%fused_computation.3 | custom fusion | bytes 6291488 | tf_op jit(solution)/shard_map/gather | solution.py:125
  162.3 2.5 %gather_fusion.2 = bf16[8,256,768]{2,1,0:T(8,128)(2,1)} fusion(bf16[8,256,768]{2,1,0:T(8,128)(2,1)S(1)} %bitcast.60, s32[1024]{0:T(1024)S(1)} %get-tuple-element.12), kind=kCustom, calls=%fused_computation.2 | custom fusion | bytes 6291488 | tf_op jit(solution)/shard_map/gather | solution.py:125
  164.8 3.3 %fusion.6 = f32[8,768,256]{1,2,0:T(8,128)S(1)} fusion(bf16[8,256,768]{2,1,0:T(8,128)(2,1)} %gather_fusion.2, bf16[8,4,256,256]{3,2,1,0:T(8,128)(2,1)} %param.10), kind=kOutput, calls=%fused_computation.20 | convolution fusion | flops 805306368 | bytes 10485760 | tf_op jit(solution)/shard_map/eim,emh->eih/dot_general | solution.py:126
  168.1 1.1 copy-done.7
  169.2 1.0 fusion.4
  170.2 0.9 copy-done.4
  171.1 1.0 fusion.2
  172.1 0.9 copy-done.3
  173.0 5.6 %add_add_fusion = f32[8,768,256]{1,2,0:T(8,128)} fusion(f32[8,768,256]{1,2,0:T(8,128)S(1)} %fusion.2, f32[8,768,256]{1,2,0:T(8,128)S(1)} %fusion.6, f32[8,768,256]{1,2,0:T(8,128)S(1)} %fusion.4, bf16[8,256,768]{2,1,0:T(8,128)(2,1)S(1)} %copy-done.3, bf16[8,4,256,256]{3,2,1,0:T(8,128)(2,1)} %param.10), kind=kOutput, calls=%fused_computation.9 | convolution fusion | flops 810024960 | bytes 29360128 | tf_op jit(solution)/shard_map/eim,emh->eih/dot_general | solution.py:126
  178.6 8.0 %fusion = bf16[2048,768]{1,0:T(8,128)(2,1)S(1)} fusion(f32[8,768,256]{1,2,0:T(8,128)} %add_add_fusion, bf16[2048,1024]{1,0:T(8,128)(2,1)} %param.13, bf16[128,24,768]{2,1,0:T(8,128)(2,1)} %all-to-all-done), kind=kOutput, calls=%fused_computation.7 | convolution fusion | flops 3224371200 | bytes 15204352 | tf_op jit(solution)/shard_map/dot_general | solution.py:132
  186.7 0.0 copy-start.1
  186.7 4.0 %maximum_convert_fusion = bf16[2048,768]{1,0:T(8,128)(2,1)} fusion(bf16[2048,768]{1,0:T(8,128)(2,1)S(1)} %fusion, bf16[768,768]{1,0:T(8,128)(2,1)S(1)} %copy-done.9, f32[768]{0:T(1024)S(1)} %copy-done.10), kind=kOutput, calls=%fused_computation.8 | convolution fusion | flops 2420637696 | bytes 7474176 | tf_op jit(solution)/shard_map/dot_general | solution.py:136
  (22 shorter events, 0.1 us)
Async XLA Ops:
  0.0 3.4 %copy-start = (bf16[2048,768]{1,0:T(8,128)(2,1)S(1)}, bf16[2048,768]{1,0:T(8,128)(2,1)}, u32[]{:S(2)}) copy-start(bf16[2048,768]{1,0:T(8,128)(2,1)} %param.9) | copy-start | bytes 9437188
  13.9 2.4 %copy-start.6 = (bf16[128,8,768]{2,1,0:T(8,128)(2,1)S(1)}, bf16[128,8,768]{2,1,0:T(8,128)(2,1)}, u32[]{:S(2)}) copy-start(bf16[128,8,768]{2,1,0:T(8,128)(2,1)} %bitcast_select_fusion) | copy-start | bytes 4718596
  18.6 11.9 %copy-start.8 = (s32[8,4]{0,1:T(4,128)S(1)}, s32[8,4]{0,1:T(4,128)}, u32[]{:S(2)}) copy-start(s32[8,4]{0,1:T(4,128)} %param.11) | copy-start | bytes 388
  18.6 70.3 %all-to-all-start = ((bf16[128,24,768]{2,1,0:T(8,128)(2,1)}), bf16[128,24,768]{2,1,0:T(8,128)(2,1)}, u32[]{:S(2)}, u32[]{:S(2)}) async-start(bf16[128,24,768]{2,1,0:T(8,128)(2,1)} %pad_maximum_fusion), calls=%async_computation | async-start | bytes 9437184 | tf_op jit(solution)/shard_map/all_to_all | solution.py:116
  153.0 4.4 %copy-start.2 = (bf16[128,16,768]{2,1,0:T(8,128)(2,1)S(1)}, bf16[128,16,768]{2,1,0:T(8,128)(2,1)}, u32[]{:S(2)}) copy-start(bf16[128,16,768]{2,1,0:T(8,128)(2,1)} %shard_map.91) | copy-start | bytes 9437188
  164.8 3.3 %copy-start.5 = (bf16[8,256,768]{2,1,0:T(8,128)(2,1)S(1)}, bf16[8,256,768]{2,1,0:T(8,128)(2,1)}, u32[]{:S(2)}) copy-start(bf16[8,256,768]{2,1,0:T(8,128)(2,1)} %gather_fusion.3) | copy-start | bytes 9437188
  164.8 4.4 %copy-start.7 = (bf16[8,4,256,256]{3,2,1,0:T(8,128)(2,1)S(1)}, bf16[8,4,256,256]{3,2,1,0:T(8,128)(2,1)}, u32[]{:S(2)}) copy-start(bf16[8,4,256,256]{3,2,1,0:T(8,128)(2,1)} %param.10) | copy-start | bytes 12582916
  169.2 1.9 copy-start.4
  171.1 1.9 copy-start.3
  178.6 8.0 %copy-start.9 = (bf16[768,768]{1,0:T(8,128)(2,1)S(1)}, bf16[768,768]{1,0:T(8,128)(2,1)}, u32[]{:S(2)}) copy-start(bf16[768,768]{1,0:T(8,128)(2,1)} %param.16) | copy-start | bytes 3538948
  178.6 8.1 %copy-start.10 = (f32[768]{0:T(1024)S(1)}, f32[768]{0:T(1024)}, u32[]{:S(2)}) copy-start(f32[768]{0:T(1024)} %param.17) | copy-start | bytes 9220
  186.7 4.0 %copy-start.1 = (bf16[2048,768]{1,0:T(8,128)(2,1)S(1)}, bf16[2048,768]{1,0:T(8,128)(2,1)}, u32[]{:S(2)}) copy-start(bf16[2048,768]{1,0:T(8,128)(2,1)} %param.9) | copy-start | bytes 9437188

commit v3 on v2

--- a/solution.py
+++ b/solution.py
@@ -76,6 +76,42 @@
     )(piece)
 
 
+def layer_kernel(tiles_per, cols_ref, w_ref, bands_ref, sw_ref, inc_ref, weight_ref, bias_ref, out_ref):
+    block = pl.program_id(0)
+    total = jnp.dot(sw_ref[...], inc_ref[...], preferred_element_type=jnp.float32)
+    for tile_index in range(tiles_per):
+        col = cols_ref[block * tiles_per + tile_index]
+        total = total + jnp.dot(w_ref[0, tile_index], bands_ref[col], preferred_element_type=jnp.float32)
+    aggregate = total.astype(jnp.bfloat16)
+    result = jnp.dot(aggregate, weight_ref[...], preferred_element_type=jnp.float32) + bias_ref[...]
+    out_ref[...] = jnp.maximum(result, 0.0).astype(out_ref.dtype)
+
+
+def fused_layer(dense_cols, dense_edge_weights, dense_bands, sparse_w, incoming_rows, weight, bias):
+    block_count, tiles_per, tile_size, _ = dense_edge_weights.shape
+    stripe_count, _, width = dense_bands.shape
+    slots = incoming_rows.shape[0]
+    out_width = weight.shape[1]
+    grid_spec = pltpu.PrefetchScalarGridSpec(
+        num_scalar_prefetch=1,
+        grid=(block_count,),
+        in_specs=[
+            pl.BlockSpec((1, tiles_per, tile_size, tile_size), lambda b, cols: (b, 0, 0, 0)),
+            pl.BlockSpec((stripe_count, tile_size, width), lambda b, cols: (0, 0, 0)),
+            pl.BlockSpec((tile_size, slots), lambda b, cols: (b, 0)),
+            pl.BlockSpec((slots, width), lambda b, cols: (0, 0)),
+            pl.BlockSpec((width, out_width), lambda b, cols: (0, 0)),
+            pl.BlockSpec((1, out_width), lambda b, cols: (0, 0)),
+        ],
+        out_specs=pl.BlockSpec((tile_size, out_width), lambda b, cols: (b, 0)),
+    )
+    return pl.pallas_call(
+        functools.partial(layer_kernel, tiles_per),
+        grid_spec=grid_spec,
+        out_shape=jax.ShapeDtypeStruct((block_count * tile_size, out_width), jnp.bfloat16),
+    )(dense_cols.reshape(-1), dense_edge_weights, dense_bands, sparse_w, incoming_rows, weight, bias.reshape(1, -1))
+
+
 def on_device(
     features,
     dense_edge_weights,
@@ -120,21 +156,7 @@
         stripe_count, tile_size, feature_width
     )
 
-    dense_sum = jnp.zeros((block_count, tile_size, feature_width), jnp.float32)
-    for tile_index in range(tiles_per):
-        picked_tiles = dense_bands[dense_cols[:, tile_index]]
-        dense_sum = dense_sum + jnp.einsum(
-            "eim,emh->eih",
-            dense_edge_weights[:, tile_index],
-            picked_tiles,
-            preferred_element_type=jnp.float32,
-        )
-    sparse_sum = jnp.dot(sparse_w, incoming_rows, preferred_element_type=jnp.float32)
-    aggregate = (dense_sum.reshape(block_count * tile_size, feature_width) + sparse_sum).astype(
-        jnp.bfloat16
-    )
-    result = jnp.dot(aggregate, weight, preferred_element_type=jnp.float32) + bias
-    return jnp.maximum(result, 0.0).astype(jnp.bfloat16)
+    return fused_layer(dense_cols, dense_edge_weights, dense_bands, sparse_w, incoming_rows, weight, bias)
 
 
 def solution(mesh):

time: 191 us -> 173 us (0.906)
  matrix products: 22.9 us -> 0 us
  Pallas kernels: 61.1 us -> 80.9 us
  local copies, waits for them, and re-layouts: 22.7 us -> 12.1 us
  other arithmetic: 13.6 us -> 11.1 us
    dot_general x6 -> x0, matrix products: 22.9 us -> none  [the longest x4 10.9 us: on_device(): jnp.einsum('eim,emh->eih', dense_edge_weights[:, tile_index], picked_tile...]
    pallas_call x0 -> x1, Pallas kernels: none -> 19.8 us  [fused_layer(): pl.pallas_call(functools.partial(layer_kernel, tiles_per), grid_spec=grid...]
    gather x4 -> x0, local copies, waits for them, and re-layouts: 11.7 us -> none  [on_device(): picked_tiles = dense_bands[dense_cols[:, tile_index]]]
    reshape x0 -> x3, local copies, waits for them, and re-layouts: none -> 3.94 us  [the longest x1 2.74 us: on_device(): arrived[:, :slot_count].reshape(peer_count * slot_count, feature_width)]
    unnamed x22 -> x9, local copies, waits for them, and re-layouts: 2.94 us -> 0.15 us
    select_n x1, other arithmetic: 2.78 us -> 0.21 us  [on_device(): jnp.where(live_slots[:, :, None], outgoing, jnp.zeros((), outgoing.dtype))]
  transfers between devices with their start and end apart: 1 -> 1, of which waited for: 1 -> 1; matrix products, arithmetic and copies ran while one was open for 0% -> 1% of each run, Pallas kernels for 0% -> 0%
where the time goes in v3:
time: 173 us
  Pallas kernels  80.9 us (47%)
  waiting for transfers between devices  57.1 us (33%)
  local copies, waits for them, and re-layouts  12.1 us (7%)
  starting transfers between devices  11.9 us (7%)
  other arithmetic  11.1 us (6%)
    pallas_call x1, Pallas kernels, gather_pieces(): pl.pallas_call(functools.partial(gather_kernel, group), out_shape=jax.Sha...  61 us
    all_to_all x1, waiting for transfers between devices, on_device(): lax.all_to_all(payload, AXES, split_axis=0, concat_axis=0, tiled=True)  57.1 us
    pallas_call x1, Pallas kernels, fused_layer(): pl.pallas_call(functools.partial(layer_kernel, tiles_per), grid_spec=grid...  19.8 us
    all_to_all x1, starting transfers between devices, on_device(): lax.all_to_all(payload, AXES, split_axis=0, concat_axis=0, tiled=True)  11.9 us
    gather x1, local copies, waits for them, and re-layouts, on_device(): outgoing = features[rows_out]  5.22 us
  transfers between devices with their start and end apart: 1, of which 1 were waited for; matrix products, arithmetic and copies ran while one was open for 1% of the time, Pallas kernels for 0%

profile of v3, /device:TPU:1, one launch (start us, length us, event | category | flops | bytes accessed | tf_op | source)
XLA Modules:
  0.0 173.1 jit_solution(10344248090980458017)
XLA Ops:
  0.0 0.0 copy-start
  0.0 0.8 compare_select_fusion.1
  0.8 0.8 fusion
  1.6 0.1 broadcast_in_dim.37
  1.7 0.1 broadcast_in_dim.38
  1.8 0.7 compare_select_fusion
  2.5 0.1 copy.12
  2.6 0.1 reshape.78
  2.7 0.7 iota_compare_fusion
  3.4 0.0 copy-done
  3.5 5.2 %gather_fusion = bf16[1024,768]{1,0:T(8,128)(2,1)} fusion(bf16[2048,768]{1,0:T(8,128)(2,1)S(1)} %copy-done, s32[1024]{0:T(1024)S(1)} %broadcast_clamp_fusion), kind=kCustom, calls=%fused_computation | custom fusion | bytes 3149824 | tf_op jit(solution)/shard_map/gather | solution.py:147
  8.7 2.4 %gather_fusion.1 = bf16[8,256,768]{2,1,0:T(8,128)(2,1)} fusion(bf16[8,256,768]{2,1,0:T(8,128)(2,1)S(1)} %bitcast.12, s32[1024]{0:T(1024)S(1)} %pad_clamp_fusion), kind=kCustom, calls=%fused_computation.1 | custom fusion | bytes 6291488 | tf_op jit(solution)/shard_map/gather | solution.py:143
  11.1 0.0 copy-start.1
  11.1 2.3 %broadcast_select_fusion = bf16[128,16,768]{2,1,0:T(8,128)(2,1)S(1)} fusion(bf16[128,16,768]{2,1,0:T(8,128)(2,1)} %bitcast.13, pred[128]{0:T(512)(128)(4,1)S(1)} %broadcast_in_dim.38), kind=kLoop, calls=%fused_computation.4 | loop fusion | flops 1572864 | bytes 6291584 | tf_op jit(solution)/shard_map/jit(_where)/select_n | solution.py:144
  13.4 0.1 copy-done.1
  13.4 0.2 bitcast_select_fusion
  13.7 2.5 %pad_maximum_fusion = bf16[128,24,768]{2,1,0:T(8,128)(2,1)} fusion(bf16[128,16,768]{2,1,0:T(8,128)(2,1)S(1)} %broadcast_select_fusion, bf16[128,8,768]{2,1,0:T(8,128)(2,1)S(1)} %bitcast_select_fusion), kind=kLoop, calls=%fused_computation.2 | loop fusion | flops 9437184 | bytes 9437184 | tf_op jit(solution)/shard_map/concatenate | solution.py:151
  16.1 0.0 copy-start.3
  16.1 0.0 copy-start.2
  16.1 11.9 %all-to-all-start = ((bf16[128,24,768]{2,1,0:T(8,128)(2,1)}), bf16[128,24,768]{2,1,0:T(8,128)(2,1)}, u32[]{:S(2)}, u32[]{:S(2)}) async-start(bf16[128,24,768]{2,1,0:T(8,128)(2,1)} %pad_maximum_fusion), calls=%async_computation | async-start | bytes 9437184 | tf_op jit(solution)/shard_map/all_to_all | solution.py:152
  28.0 0.0 copy-done.3
  28.1 0.1 copy.11
  28.1 0.6 reshape.71.cols_ref
  28.7 0.0 copy-done.2
  28.7 0.6 reshape.75.bias_ref
  29.3 57.1 %all-to-all-done = bf16[128,24,768]{2,1,0:T(8,128)(2,1)} async-done(((bf16[128,24,768]{2,1,0:T(8,128)(2,1)}), bf16[128,24,768]{2,1,0:T(8,128)(2,1)}, u32[]{:S(2)}, u32[]{:S(2)}) %all-to-all-start) | async-done | bytes 4718624 | tf_op jit(solution)/shard_map/all_to_all | solution.py:152
  86.5 3.0 %slice_reduce_fusion.piece_ref = bf16[16,768]{1,0:T(8,128)(2,1)} fusion(bf16[128,24,768]{2,1,0:T(8,128)(2,1)} %all-to-all-done), kind=kLoop, calls=%fused_computation.3 | loop fusion | flops 1560576 | bytes 3170304 | tf_op jit(solution)/shard_map/reduce_sum | solution.py:154
  89.5 61.0 %shard_map.91 = bf16[128,16,768]{2,1,0:T(8,128)(2,1)} custom-call(bf16[16,768]{1,0:T(8,128)(2,1)} %slice_reduce_fusion.piece_ref), custom_call_target="tpu_custom_call" | custom-call | tf_op jit(solution)/shard_map/pallas_call | solution.py:65
  150.5 2.7 %slice_bitcast_fusion.inc_ref = bf16[1024,768]{1,0:T(8,128)(2,1)} fusion(bf16[128,24,768]{2,1,0:T(8,128)(2,1)} %all-to-all-done), kind=kLoop, calls=%fused_computation.5 | loop fusion | bytes 3145728 | tf_op jit(solution)/shard_map/reshape | solution.py:153
  153.3 19.8 %shard_map.92 = bf16[2048,768]{1,0:T(8,128)(2,1)} custom-call(s32[32]{0:T(128)} %reshape.71.cols_ref, bf16[8,4,256,256]{3,2,1,0:T(8,128)(2,1)} %w_ref.1, bf16[8,256,768]{2,1,0:T(8,128)(2,1)} %bitcast.14, bf16[2048,1024]{1,0:T(8,128)(2,1)} %sw_ref.1, bf16[1024,768]{1,0:T(8,128)(2,1)} %slice_bitcast_fusion.inc_ref, bf16[768,768]{1,0:T(8,128)(2,1)} %weight_ref.1, ...), custom_call_target="tpu_custom_call" | custom-call | tf_op jit(solution)/shard_map/pallas_call | solution.py:108
  (2 shorter events, 0.0 us)
Async XLA Ops:
  0.0 3.5 %copy-start = (bf16[2048,768]{1,0:T(8,128)(2,1)S(1)}, bf16[2048,768]{1,0:T(8,128)(2,1)}, u32[]{:S(2)}) copy-start(bf16[2048,768]{1,0:T(8,128)(2,1)} %param.9) | copy-start | bytes 9437188
  11.1 2.4 %copy-start.1 = (bf16[1024,768]{1,0:T(8,128)(2,1)S(1)}, bf16[1024,768]{1,0:T(8,128)(2,1)}, u32[]{:S(2)}) copy-start(bf16[1024,768]{1,0:T(8,128)(2,1)} %gather_fusion) | copy-start | bytes 4718596
  16.1 11.9 %copy-start.3 = (s32[8,4]{0,1:T(4,128)S(1)}, s32[8,4]{0,1:T(4,128)}, u32[]{:S(2)}) copy-start(s32[8,4]{0,1:T(4,128)} %param.11) | copy-start | bytes 388
  16.1 12.6 %copy-start.2 = (f32[768]{0:T(1024)S(1)}, f32[768]{0:T(1024)}, u32[]{:S(2)}) copy-start(f32[768]{0:T(1024)} %param.17) | copy-start | bytes 9220
  16.1 70.3 %all-to-all-start = ((bf16[128,24,768]{2,1,0:T(8,128)(2,1)}), bf16[128,24,768]{2,1,0:T(8,128)(2,1)}, u32[]{:S(2)}, u32[]{:S(2)}) async-start(bf16[128,24,768]{2,1,0:T(8,128)(2,1)} %pad_maximum_fusion), calls=%async_computation | async-start | bytes 9437184 | tf_op jit(solution)/shard_map/all_to_all | solution.py:152

commit v4 on v3

--- a/solution.py
+++ b/solution.py
@@ -10,53 +10,73 @@
 AXES = ("row", "grp")
 
 
-def gather_kernel(group, piece_ref, out_ref, send_sem, recv_sem, local_sem):
+def gather_kernel(group, piece_ref, out_ref, send_sem, relay_sem, recv_sem, local_sem):
     n = out_ref.shape[0]
+    chips = n // 2
     me = lax.axis_index(AXES)
+    core = (me // group) % 2
+    my_chip = (me // (2 * group)) * group + me % group
+    mesh_ids = pl.DeviceIdType.MESH
 
-    def where(peer):
-        return (peer // group, peer % group)
+    def device(chip, which_core):
+        return ((chip // group) * 2 + which_core) * group + chip % group
 
+    def where(k):
+        return (k // group, k % group)
+
+    def remote(src, dst, send, recv, k):
+        return pltpu.make_async_remote_copy(
+            src_ref=src, dst_ref=dst, send_sem=send, recv_sem=recv,
+            device_id=where(k), device_id_type=mesh_ids,
+        )
+
+    partner = device(my_chip, 1 - core)
     barrier = pltpu.get_barrier_semaphore()
+    pl.semaphore_signal(barrier, inc=1, device_id=where(partner), device_id_type=mesh_ids)
 
     def greet(i, carry):
-        peer = lax.rem(me + i, n)
-        pl.semaphore_signal(barrier, inc=1, device_id=where(peer), device_id_type=pl.DeviceIdType.MESH)
+        peer = device(lax.rem(my_chip + i, chips), core)
+        pl.semaphore_signal(barrier, inc=1, device_id=where(peer), device_id_type=mesh_ids)
         return carry
 
-    lax.fori_loop(1, n, greet, 0)
-    pl.semaphore_wait(barrier, n - 1)
+    lax.fori_loop(1, chips, greet, 0)
+    pl.semaphore_wait(barrier, chips)
     own = pltpu.make_async_copy(piece_ref, out_ref.at[me], local_sem)
     own.start()
+    remote(piece_ref, out_ref.at[me], send_sem.at[0], recv_sem.at[me], partner).start()
 
     def send(i, carry):
-        peer = lax.rem(me + i, n)
-        pltpu.make_async_remote_copy(
-            src_ref=piece_ref,
-            dst_ref=out_ref.at[me],
-            send_sem=send_sem.at[i],
-            recv_sem=recv_sem.at[me],
-            device_id=where(peer),
-            device_id_type=pl.DeviceIdType.MESH,
-        ).start()
+        peer = device(lax.rem(my_chip + i, chips), core)
+        remote(piece_ref, out_ref.at[me], send_sem.at[i], recv_sem.at[me], peer).start()
         return carry
 
-    lax.fori_loop(1, n, send, 0)
+    lax.fori_loop(1, chips, send, 0)
 
-    def wait(i, carry):
-        peer = lax.rem(me + i, n)
-        source = lax.rem(me + n - i, n)
-        pltpu.make_async_remote_copy(
-            src_ref=piece_ref,
-            dst_ref=out_ref.at[source],
-            send_sem=send_sem.at[i],
-            recv_sem=recv_sem.at[source],
-            device_id=where(peer),
-            device_id_type=pl.DeviceIdType.MESH,
-        ).wait()
+    def relay(i, carry):
+        source = device(lax.rem(my_chip + chips - i, chips), core)
+        remote(piece_ref, out_ref.at[source], send_sem.at[i], recv_sem.at[source], source).wait_recv()
+        remote(out_ref.at[source], out_ref.at[source], relay_sem.at[i], recv_sem.at[source], partner).start()
         return carry
 
-    lax.fori_loop(1, n, wait, 0)
+    lax.fori_loop(1, chips, relay, 0)
+    remote(piece_ref, out_ref.at[partner], send_sem.at[0], recv_sem.at[partner], partner).wait_recv()
+
+    def take(i, carry):
+        source = device(lax.rem(my_chip + chips - i, chips), 1 - core)
+        remote(piece_ref, out_ref.at[source], send_sem.at[i], recv_sem.at[source], partner).wait_recv()
+        return carry
+
+    lax.fori_loop(1, chips, take, 0)
+    remote(piece_ref, out_ref.at[me], send_sem.at[0], recv_sem.at[me], partner).wait_send()
+
+    def drain(i, carry):
+        peer = device(lax.rem(my_chip + i, chips), core)
+        remote(piece_ref, out_ref.at[me], send_sem.at[i], recv_sem.at[me], peer).wait_send()
+        source = device(lax.rem(my_chip + chips - i, chips), core)
+        remote(out_ref.at[source], out_ref.at[source], relay_sem.at[i], recv_sem.at[source], partner).wait_send()
+        return carry
+
+    lax.fori_loop(1, chips, drain, 0)
     own.wait()
 
 
@@ -68,13 +88,13 @@
         in_specs=[pl.BlockSpec(memory_space=pltpu.VMEM)],
         out_specs=pl.BlockSpec(memory_space=pltpu.VMEM),
         scratch_shapes=[
-            pltpu.SemaphoreType.DMA((n,)),
+            pltpu.SemaphoreType.DMA((n // 2,)),
+            pltpu.SemaphoreType.DMA((n // 2,)),
             pltpu.SemaphoreType.DMA((n,)),
             pltpu.SemaphoreType.DMA,
         ],
         compiler_params=pltpu.CompilerParams(collective_id=0, has_side_effects=True),
     )(piece)
-
 
 def layer_kernel(tiles_per, cols_ref, w_ref, bands_ref, sw_ref, inc_ref, weight_ref, bias_ref, out_ref):
     block = pl.program_id(0)

time: 173 us -> 148 us (0.86)
  Pallas kernels: 80.9 us -> 55.7 us
    pallas_call x1, Pallas kernels: 61 us -> 35.9 us  [gather_pieces(): pl.pallas_call(functools.partial(gather_kernel, group), out_shape=jax.Sha...]
where the time goes in v4:
time: 148 us
  waiting for transfers between devices  57.1 us (39%)
  Pallas kernels  55.7 us (38%)
  local copies, waits for them, and re-layouts  12.1 us (8%)
  starting transfers between devices  11.9 us (8%)
  other arithmetic  11.1 us (8%)
    all_to_all x1, waiting for transfers between devices, on_device(): lax.all_to_all(payload, AXES, split_axis=0, concat_axis=0, tiled=True)  57.1 us
    pallas_call x1, Pallas kernels, gather_pieces(): pl.pallas_call(functools.partial(gather_kernel, group), out_shape=jax.Sha...  35.9 us
    pallas_call x1, Pallas kernels, fused_layer(): pl.pallas_call(functools.partial(layer_kernel, tiles_per), grid_spec=grid...  19.8 us
    all_to_all x1, starting transfers between devices, on_device(): lax.all_to_all(payload, AXES, split_axis=0, concat_axis=0, tiled=True)  11.9 us
    gather x1, local copies, waits for them, and re-layouts, on_device(): outgoing = features[rows_out]  5.22 us
    reduce_sum x1, other arithmetic, on_device(): jnp.sum(arrived[:, slot_count:].astype(jnp.float32), axis=0)  3.01 us
  transfers between devices with their start and end apart: 1, of which 1 were waited for; matrix products, arithmetic and copies ran while one was open for 1% of the time, Pallas kernels for 0%

profile of v4, /device:TPU:1, one launch (start us, length us, event | category | flops | bytes accessed | tf_op | source)
XLA Modules:
  0.0 147.9 jit_solution(6965370394769399124)
XLA Ops:
  0.0 0.0 copy-start
  0.0 0.8 compare_select_fusion.1
  0.8 0.8 fusion
  1.6 0.1 broadcast_in_dim.37
  1.7 0.1 broadcast_in_dim.38
  1.8 0.7 compare_select_fusion
  2.5 0.1 copy.12
  2.6 0.1 reshape.78
  2.7 0.7 iota_compare_fusion
  3.4 0.0 copy-done
  3.5 5.2 %gather_fusion = bf16[1024,768]{1,0:T(8,128)(2,1)} fusion(bf16[2048,768]{1,0:T(8,128)(2,1)S(1)} %copy-done, s32[1024]{0:T(1024)S(1)} %broadcast_clamp_fusion), kind=kCustom, calls=%fused_computation | custom fusion | bytes 3149824 | tf_op jit(solution)/shard_map/gather | solution.py:167
  8.7 2.4 %gather_fusion.1 = bf16[8,256,768]{2,1,0:T(8,128)(2,1)} fusion(bf16[8,256,768]{2,1,0:T(8,128)(2,1)S(1)} %bitcast.12, s32[1024]{0:T(1024)S(1)} %pad_clamp_fusion), kind=kCustom, calls=%fused_computation.1 | custom fusion | bytes 6291488 | tf_op jit(solution)/shard_map/gather | solution.py:163
  11.1 0.0 copy-start.1
  11.1 2.3 %broadcast_select_fusion = bf16[128,16,768]{2,1,0:T(8,128)(2,1)S(1)} fusion(bf16[128,16,768]{2,1,0:T(8,128)(2,1)} %bitcast.13, pred[128]{0:T(512)(128)(4,1)S(1)} %broadcast_in_dim.38), kind=kLoop, calls=%fused_computation.4 | loop fusion | flops 1572864 | bytes 6291584 | tf_op jit(solution)/shard_map/jit(_where)/select_n | solution.py:164
  13.4 0.1 copy-done.1
  13.4 0.2 bitcast_select_fusion
  13.7 2.5 %pad_maximum_fusion = bf16[128,24,768]{2,1,0:T(8,128)(2,1)} fusion(bf16[128,16,768]{2,1,0:T(8,128)(2,1)S(1)} %broadcast_select_fusion, bf16[128,8,768]{2,1,0:T(8,128)(2,1)S(1)} %bitcast_select_fusion), kind=kLoop, calls=%fused_computation.2 | loop fusion | flops 9437184 | bytes 9437184 | tf_op jit(solution)/shard_map/concatenate | solution.py:171
  16.1 0.0 copy-start.3
  16.1 0.0 copy-start.2
  16.1 11.9 %all-to-all-start = ((bf16[128,24,768]{2,1,0:T(8,128)(2,1)}), bf16[128,24,768]{2,1,0:T(8,128)(2,1)}, u32[]{:S(2)}, u32[]{:S(2)}) async-start(bf16[128,24,768]{2,1,0:T(8,128)(2,1)} %pad_maximum_fusion), calls=%async_computation | async-start | bytes 9437184 | tf_op jit(solution)/shard_map/all_to_all | solution.py:172
  28.0 0.0 copy-done.3
  28.1 0.1 copy.11
  28.1 0.6 reshape.71.cols_ref
  28.7 0.0 copy-done.2
  28.7 0.6 reshape.75.bias_ref
  29.3 57.1 %all-to-all-done = bf16[128,24,768]{2,1,0:T(8,128)(2,1)} async-done(((bf16[128,24,768]{2,1,0:T(8,128)(2,1)}), bf16[128,24,768]{2,1,0:T(8,128)(2,1)}, u32[]{:S(2)}, u32[]{:S(2)}) %all-to-all-start) | async-done | bytes 4718624 | tf_op jit(solution)/shard_map/all_to_all | solution.py:172
  86.5 3.0 %slice_reduce_fusion.piece_ref = bf16[16,768]{1,0:T(8,128)(2,1)} fusion(bf16[128,24,768]{2,1,0:T(8,128)(2,1)} %all-to-all-done), kind=kLoop, calls=%fused_computation.3 | loop fusion | flops 1560576 | bytes 3170304 | tf_op jit(solution)/shard_map/reduce_sum | solution.py:174
  89.5 35.9 %shard_map.91 = bf16[128,16,768]{2,1,0:T(8,128)(2,1)} custom-call(bf16[16,768]{1,0:T(8,128)(2,1)} %slice_reduce_fusion.piece_ref), custom_call_target="tpu_custom_call" | custom-call | tf_op jit(solution)/shard_map/pallas_call | solution.py:85
  125.4 2.7 %slice_bitcast_fusion.inc_ref = bf16[1024,768]{1,0:T(8,128)(2,1)} fusion(bf16[128,24,768]{2,1,0:T(8,128)(2,1)} %all-to-all-done), kind=kLoop, calls=%fused_computation.5 | loop fusion | bytes 3145728 | tf_op jit(solution)/shard_map/reshape | solution.py:173
  128.1 19.8 %shard_map.92 = bf16[2048,768]{1,0:T(8,128)(2,1)} custom-call(s32[32]{0:T(128)} %reshape.71.cols_ref, bf16[8,4,256,256]{3,2,1,0:T(8,128)(2,1)} %w_ref.1, bf16[8,256,768]{2,1,0:T(8,128)(2,1)} %bitcast.14, bf16[2048,1024]{1,0:T(8,128)(2,1)} %sw_ref.1, bf16[1024,768]{1,0:T(8,128)(2,1)} %slice_bitcast_fusion.inc_ref, bf16[768,768]{1,0:T(8,128)(2,1)} %weight_ref.1, ...), custom_call_target="tpu_custom_call" | custom-call | tf_op jit(solution)/shard_map/pallas_call | solution.py:128
  (2 shorter events, 0.0 us)
Async XLA Ops:
  0.0 3.5 %copy-start = (bf16[2048,768]{1,0:T(8,128)(2,1)S(1)}, bf16[2048,768]{1,0:T(8,128)(2,1)}, u32[]{:S(2)}) copy-start(bf16[2048,768]{1,0:T(8,128)(2,1)} %param.9) | copy-start | bytes 9437188
  11.1 2.4 %copy-start.1 = (bf16[1024,768]{1,0:T(8,128)(2,1)S(1)}, bf16[1024,768]{1,0:T(8,128)(2,1)}, u32[]{:S(2)}) copy-start(bf16[1024,768]{1,0:T(8,128)(2,1)} %gather_fusion) | copy-start | bytes 4718596
  16.1 11.9 %copy-start.3 = (s32[8,4]{0,1:T(4,128)S(1)}, s32[8,4]{0,1:T(4,128)}, u32[]{:S(2)}) copy-start(s32[8,4]{0,1:T(4,128)} %param.11) | copy-start | bytes 388
  16.1 12.6 %copy-start.2 = (f32[768]{0:T(1024)S(1)}, f32[768]{0:T(1024)}, u32[]{:S(2)}) copy-start(f32[768]{0:T(1024)} %param.17) | copy-start | bytes 9220
  16.1 70.3 %all-to-all-start = ((bf16[128,24,768]{2,1,0:T(8,128)(2,1)}), bf16[128,24,768]{2,1,0:T(8,128)(2,1)}, u32[]{:S(2)}, u32[]{:S(2)}) async-start(bf16[128,24,768]{2,1,0:T(8,128)(2,1)} %pad_maximum_fusion), calls=%async_computation | async-start | bytes 9437184 | tf_op jit(solution)/shard_map/all_to_all | solution.py:172

commit v5 on v4

--- a/solution.py
+++ b/solution.py
@@ -158,10 +158,7 @@
     piece = stripe_count * tile_size // peer_count
     me = lax.axis_index(AXES)
 
-    owners = dense_ids // block_count
-    mine = owners == me
     candidates = local_blocks[dense_ids % block_count]
-    candidates = jnp.where(mine[:, None, None], candidates, jnp.zeros((), candidates.dtype))
     stripe_pieces = candidates.reshape(peer_count, piece, feature_width)
 
     outgoing = features[rows_out]
@@ -171,7 +168,8 @@
     payload = jnp.concatenate([outgoing, stripe_pieces], axis=1)
     arrived = lax.all_to_all(payload, AXES, split_axis=0, concat_axis=0, tiled=True)
     incoming_rows = arrived[:, :slot_count].reshape(peer_count * slot_count, feature_width)
-    my_piece = jnp.sum(arrived[:, slot_count:].astype(jnp.float32), axis=0).astype(jnp.bfloat16)
+    my_owner = dense_ids[me * piece // tile_size] // block_count
+    my_piece = lax.dynamic_index_in_dim(arrived, my_owner, 0, keepdims=False)[slot_count:]
     dense_bands = gather_pieces(my_piece, peer_count, group).reshape(
         stripe_count, tile_size, feature_width
     )

time: 148 us -> 148 us (level)
  waiting for transfers between devices: 57.1 us -> 53.8 us
  between operations: 0.07 us -> 2.69 us
  local copies, waits for them, and re-layouts: 12.1 us -> 13.8 us
    all_to_all x1, waiting for transfers between devices: 57.1 us -> 53.8 us  [on_device(): lax.all_to_all(payload, AXES, split_axis=0, concat_axis=0, tiled=True)]
    reduce_sum x1 -> x0, other arithmetic: 3.01 us -> none  [on_device(): jnp.sum(arrived[:, slot_count:].astype(jnp.float32), axis=0)]
    select_n x1, other arithmetic: 0.21 us -> 2.78 us  [on_device(): jnp.where(live_slots[:, :, None], outgoing, jnp.zeros((), outgoing.dtype))]
    concatenate x1, other arithmetic: 2.47 us -> 4.81 us  [on_device(): payload = jnp.concatenate([outgoing, stripe_pieces], axis=1)]
    select_n x1 -> x0, other arithmetic: 2.29 us -> none  [on_device(): jnp.where(mine[:, None, None], candidates, jnp.zeros((), candidates.dtype))]
where the time goes in v5:
time: 148 us
  Pallas kernels  55.7 us (38%)
  waiting for transfers between devices  53.8 us (36%)
  local copies, waits for them, and re-layouts  13.8 us (9%)
  starting transfers between devices  11.9 us (8%)
  other arithmetic  9.85 us (7%)
  between operations  2.69 us (2%)
    all_to_all x1, waiting for transfers between devices, on_device(): lax.all_to_all(payload, AXES, split_axis=0, concat_axis=0, tiled=True)  53.8 us
    pallas_call x1, Pallas kernels, gather_pieces(): pl.pallas_call(functools.partial(gather_kernel, group), out_shape=jax.Sha...  35.9 us
    pallas_call x1, Pallas kernels, fused_layer(): pl.pallas_call(functools.partial(layer_kernel, tiles_per), grid_spec=grid...  19.8 us
    all_to_all x1, starting transfers between devices, on_device(): lax.all_to_all(payload, AXES, split_axis=0, concat_axis=0, tiled=True)  11.9 us
    gather x1, local copies, waits for them, and re-layouts, on_device(): outgoing = features[rows_out]  5.21 us
    concatenate x1, other arithmetic, on_device(): payload = jnp.concatenate([outgoing, stripe_pieces], axis=1)  4.81 us
  transfers between devices with their start and end apart: 1, of which 1 were waited for; matrix products, arithmetic and copies ran while one was open for 1% of the time, Pallas kernels for 0%

profile of v5, /device:TPU:1, one launch (start us, length us, event | category | flops | bytes accessed | tf_op | source)
XLA Modules:
  0.0 147.8 jit_solution(550430210968732057)
XLA Ops:
  0.0 0.0 copy-start
  0.0 0.8 compare_select_fusion
  0.8 0.1 copy.12
  0.9 0.1 reshape.79
  1.1 0.7 iota_compare_fusion
  1.8 0.7 compare_select_fusion.1
  2.5 0.0 copy-done
  2.5 5.2 %gather_fusion = bf16[1024,768]{1,0:T(8,128)(2,1)} fusion(bf16[2048,768]{1,0:T(8,128)(2,1)S(1)} %copy-done, s32[1024]{0:T(1024)S(1)} %broadcast_clamp_fusion), kind=kCustom, calls=%fused_computation | custom fusion | bytes 3149824 | tf_op jit(solution)/shard_map/gather | solution.py:164
  7.7 2.8 %bitcast_select_fusion = bf16[128,8,768]{2,1,0:T(8,128)(2,1)} fusion(bf16[1024,768]{1,0:T(8,128)(2,1)} %gather_fusion, pred[128,8]{1,0:T(8,128)(4,1)S(1)} %iota_compare_fusion), kind=kLoop, calls=%fused_computation.4 | loop fusion | flops 786432 | bytes 3146752 | tf_op jit(solution)/shard_map/jit(_where)/select_n | solution.py:167
  10.5 2.4 %gather_fusion.1 = bf16[8,256,768]{2,1,0:T(8,128)(2,1)} fusion(bf16[8,256,768]{2,1,0:T(8,128)(2,1)S(1)} %bitcast.15, s32[1024]{0:T(1024)S(1)} %pad_clamp_fusion), kind=kCustom, calls=%fused_computation.1 | custom fusion | bytes 6291488 | tf_op jit(solution)/shard_map/gather | solution.py:161
  12.9 4.8 %pad_maximum_fusion = bf16[128,24,768]{2,1,0:T(8,128)(2,1)} fusion(bf16[128,16,768]{2,1,0:T(8,128)(2,1)} %bitcast.16, bf16[128,8,768]{2,1,0:T(8,128)(2,1)} %bitcast_select_fusion), kind=kLoop, calls=%fused_computation.2 | loop fusion | flops 9437184 | bytes 9437184 | tf_op jit(solution)/shard_map/concatenate | solution.py:168
  17.7 0.0 copy-start.3
  17.7 0.0 copy-start.2
  17.7 0.0 copy-start.1
  17.7 11.9 %all-to-all-start = ((bf16[128,24,768]{2,1,0:T(8,128)(2,1)}), bf16[128,24,768]{2,1,0:T(8,128)(2,1)}, u32[]{:S(2)}, u32[]{:S(2)}) async-start(bf16[128,24,768]{2,1,0:T(8,128)(2,1)} %pad_maximum_fusion), calls=%async_computation | async-start | bytes 9437184 | tf_op jit(solution)/shard_map/all_to_all | solution.py:169
  29.6 0.0 copy-done.3
  29.6 0.6 dynamic_slice.7
  32.8 0.0 copy-done.2
  32.9 0.1 copy.11
  32.9 0.7 reshape.71.cols_ref
  33.6 0.0 copy-done.1
  33.6 0.6 reshape.76.bias_ref
  34.2 53.8 %all-to-all-done = bf16[128,24,768]{2,1,0:T(8,128)(2,1)} async-done(((bf16[128,24,768]{2,1,0:T(8,128)(2,1)}), bf16[128,24,768]{2,1,0:T(8,128)(2,1)}, u32[]{:S(2)}, u32[]{:S(2)}) %all-to-all-start) | async-done | bytes 4718624 | tf_op jit(solution)/shard_map/all_to_all | solution.py:169
  88.0 1.3 dynamic-slice_bitcast_fusion.piece_ref
  89.4 35.9 %shard_map.91 = bf16[128,16,768]{2,1,0:T(8,128)(2,1)} custom-call(bf16[16,768]{1,0:T(8,128)(2,1)} %dynamic-slice_bitcast_fusion.piece_ref), custom_call_target="tpu_custom_call" | custom-call | tf_op jit(solution)/shard_map/pallas_call | solution.py:85
  125.3 2.7 %slice_bitcast_fusion.inc_ref = bf16[1024,768]{1,0:T(8,128)(2,1)} fusion(bf16[128,24,768]{2,1,0:T(8,128)(2,1)} %all-to-all-done), kind=kLoop, calls=%fused_computation.3 | loop fusion | bytes 3145728 | tf_op jit(solution)/shard_map/reshape | solution.py:170
  128.0 19.8 %shard_map.92 = bf16[2048,768]{1,0:T(8,128)(2,1)} custom-call(s32[32]{0:T(128)} %reshape.71.cols_ref, bf16[8,4,256,256]{3,2,1,0:T(8,128)(2,1)} %w_ref.1, bf16[8,256,768]{2,1,0:T(8,128)(2,1)} %bitcast.17, bf16[2048,1024]{1,0:T(8,128)(2,1)} %sw_ref.1, bf16[1024,768]{1,0:T(8,128)(2,1)} %slice_bitcast_fusion.inc_ref, bf16[768,768]{1,0:T(8,128)(2,1)} %weight_ref.1, ...), custom_call_target="tpu_custom_call" | custom-call | tf_op jit(solution)/shard_map/pallas_call | solution.py:128
  (2 shorter events, 0.0 us)
Async XLA Ops:
  0.0 2.5 %copy-start = (bf16[2048,768]{1,0:T(8,128)(2,1)S(1)}, bf16[2048,768]{1,0:T(8,128)(2,1)}, u32[]{:S(2)}) copy-start(bf16[2048,768]{1,0:T(8,128)(2,1)} %param.9) | copy-start | bytes 9437188
  17.7 11.9 %copy-start.3 = (s32[8]{0:T(128)S(1)}, s32[8]{0:T(128)}, u32[]{:S(2)}) copy-start(s32[8]{0:T(128)} %param.12) | copy-start | bytes 100
  17.7 15.1 %copy-start.2 = (s32[8,4]{0,1:T(4,128)S(1)}, s32[8,4]{0,1:T(4,128)}, u32[]{:S(2)}) copy-start(s32[8,4]{0,1:T(4,128)} %param.11) | copy-start | bytes 388
  17.7 15.9 %copy-start.1 = (f32[768]{0:T(1024)S(1)}, f32[768]{0:T(1024)}, u32[]{:S(2)}) copy-start(f32[768]{0:T(1024)} %param.17) | copy-start | bytes 9220
  17.7 70.3 %all-to-all-start = ((bf16[128,24,768]{2,1,0:T(8,128)(2,1)}), bf16[128,24,768]{2,1,0:T(8,128)(2,1)}, u32[]{:S(2)}, u32[]{:S(2)}) async-start(bf16[128,24,768]{2,1,0:T(8,128)(2,1)} %pad_maximum_fusion), calls=%async_computation | async-start | bytes 9437184 | tf_op jit(solution)/shard_map/all_to_all | solution.py:169

commit v6 on v5

--- a/solution.py
+++ b/solution.py
@@ -158,14 +158,12 @@
     piece = stripe_count * tile_size // peer_count
     me = lax.axis_index(AXES)
 
-    candidates = local_blocks[dense_ids % block_count]
-    stripe_pieces = candidates.reshape(peer_count, piece, feature_width)
-
-    outgoing = features[rows_out]
-    slot_ids = jnp.arange(slot_count, dtype=jnp.int32)
-    live_slots = slot_ids[None, :] < counts_out[:, None]
-    outgoing = jnp.where(live_slots[:, :, None], outgoing, jnp.zeros((), outgoing.dtype))
-    payload = jnp.concatenate([outgoing, stripe_pieces], axis=1)
+    stripe_rows = jnp.arange(stripe_count * tile_size, dtype=jnp.int32)
+    stripe_rows = (dense_ids % block_count)[stripe_rows // tile_size] * tile_size + stripe_rows % tile_size
+    row_ids = jnp.concatenate([rows_out, stripe_rows.reshape(peer_count, piece)], axis=1)
+    slot_ids = jnp.arange(slot_count + piece, dtype=jnp.int32)
+    live_slots = (slot_ids[None, :] < counts_out[:, None]) | (slot_ids[None, :] >= slot_count)
+    payload = jnp.where(live_slots[:, :, None], features[row_ids], jnp.zeros((), features.dtype))
     arrived = lax.all_to_all(payload, AXES, split_axis=0, concat_axis=0, tiled=True)
     incoming_rows = arrived[:, :slot_count].reshape(peer_count * slot_count, feature_width)
     my_owner = dense_ids[me * piece // tile_size] // block_count

time: 148 us -> 158 us (1.068)
  local copies, waits for them, and re-layouts: 13.8 us -> 20.6 us
  other arithmetic: 9.85 us -> 12.4 us
    gather x2, local copies, waits for them, and re-layouts: 7.63 us -> 14.3 us  [the longest x1 13.6 us: on_device(): features[row_ids]]
    concatenate x1, other arithmetic: 4.81 us -> 0.04 us  [on_device(): jnp.concatenate([rows_out, stripe_rows.reshape(peer_count, piece)], axis=1)]
    gather x2 -> x3, other arithmetic: 0.02 us -> 4.42 us  [the longest x2 4.41 us: on_device(): (dense_ids % block_count)[stripe_rows // tile_size] * tile_size]
    select_n x3, other arithmetic: 4.28 us -> 7.23 us  [the longest x1 5.71 us: on_device(): jnp.where(live_slots[:, :, None], features[row_ids], jnp.zeros((), featur...]
where the time goes in v6:
time: 158 us; the launch traced here: 157 us
  Pallas kernels  55.7 us (35%)
  waiting for transfers between devices  53.8 us (34%)
  local copies, waits for them, and re-layouts  20.6 us (13%)
  other arithmetic  12.4 us (8%)
  starting transfers between devices  11.9 us (8%)
  between operations  2.73 us (2%)
    all_to_all x1, waiting for transfers between devices, on_device(): lax.all_to_all(payload, AXES, split_axis=0, concat_axis=0, tiled=True)  53.8 us
    pallas_call x1, Pallas kernels, gather_pieces(): pl.pallas_call(functools.partial(gather_kernel, group), out_shape=jax.Sha...  35.9 us
    pallas_call x1, Pallas kernels, fused_layer(): pl.pallas_call(functools.partial(layer_kernel, tiles_per), grid_spec=grid...  19.8 us
    gather x1, local copies, waits for them, and re-layouts, on_device(): features[row_ids]  13.6 us
    all_to_all x1, starting transfers between devices, on_device(): lax.all_to_all(payload, AXES, split_axis=0, concat_axis=0, tiled=True)  11.9 us
    select_n x1, other arithmetic, on_device(): jnp.where(live_slots[:, :, None], features[row_ids], jnp.zeros((), featur...  5.71 us
    gather x2, other arithmetic, on_device(): (dense_ids % block_count)[stripe_rows // tile_size] * tile_size  4.41 us
  transfers between devices with their start and end apart: 1, of which 1 were waited for; matrix products, arithmetic and copies ran while one was open for 1% of the time, Pallas kernels for 0%

profile of v6, /device:TPU:1, one launch (start us, length us, event | category | flops | bytes accessed | tf_op | source)
XLA Modules:
  0.0 157.2 jit_solution(10762042147226273386)
XLA Ops:
  0.0 0.0 copy-start
  0.0 0.8 and_select_fusion.1
  0.9 0.7 fusion.5
  1.5 4.4 %compare_select_fusion.2 = s32[2048,1]{0,1:T(1,128)S(1)} fusion(s32[]{:T(128)} %bitcast.3, s32[]{:T(128)} %bitcast.4, s32[]{:T(128)} %bitcast.5, s32[]{:T(128)} %bitcast.6, s32[]{:T(128)} %bitcast.7, s32[]{:T(128)} %bitcast.9, s32[]{:T(128)} %bitcast.8), kind=kLoop, calls=%fused_computation.14 | loop fusion | flops 47104 | bytes 8220 | tf_op jit(solution)/shard_map/gather | solution.py:162
  5.9 0.7 select_multiply_fusion
  6.6 0.1 mul.27
  6.7 0.1 copy.15
  6.8 0.7 compare_select_fusion.1
  7.5 0.1 copy.16
  7.6 0.1 reshape.208
  7.7 0.0 copy-done
  7.7 0.0 copy-start.3
  7.7 13.6 %gather_fusion = bf16[3072,768]{1,0:T(8,128)(2,1)} fusion(bf16[2048,768]{1,0:T(8,128)(2,1)S(1)} %copy-done, s32[3072]{0:T(1024)S(1)} %broadcast_clamp_fusion), kind=kCustom, calls=%fused_computation | custom fusion | bytes 9449472 | tf_op jit(solution)/shard_map/gather | solution.py:166
  21.3 0.0 copy-done.3
  21.3 0.1 fusion.3
  21.4 5.7 %broadcast_select_fusion = bf16[128,24,768]{2,1,0:T(8,128)(2,1)} fusion(bf16[128,24,768]{2,1,0:T(8,128)(2,1)} %bitcast.22, pred[128,24]{1,0:T(8,128)(4,1)S(1)} %fusion.3), kind=kLoop, calls=%fused_computation.1 | loop fusion | flops 2359296 | bytes 9440256 | tf_op jit(solution)/shard_map/jit(_where)/select_n | solution.py:166
  27.1 0.0 copy-start.4
  27.1 0.0 copy-start.2
  27.1 0.0 copy-start.1
  27.1 11.9 %all-to-all-start = ((bf16[128,24,768]{2,1,0:T(8,128)(2,1)}), bf16[128,24,768]{2,1,0:T(8,128)(2,1)}, u32[]{:S(2)}, u32[]{:S(2)}) async-start(bf16[128,24,768]{2,1,0:T(8,128)(2,1)} %broadcast_select_fusion), calls=%async_computation | async-start | bytes 9437184 | tf_op jit(solution)/shard_map/all_to_all | solution.py:167
  39.0 0.0 copy-done.4
  39.1 0.6 dynamic_slice.7
  42.3 0.0 copy-done.2
  42.3 0.1 copy.14
  42.3 0.7 reshape.187.cols_ref
  43.0 0.0 copy-done.1
  43.0 0.6 reshape.190.bias_ref
  43.6 53.8 %all-to-all-done = bf16[128,24,768]{2,1,0:T(8,128)(2,1)} async-done(((bf16[128,24,768]{2,1,0:T(8,128)(2,1)}), bf16[128,24,768]{2,1,0:T(8,128)(2,1)}, u32[]{:S(2)}, u32[]{:S(2)}) %all-to-all-start) | async-done | bytes 4718624 | tf_op jit(solution)/shard_map/all_to_all | solution.py:167
  97.4 1.3 dynamic-slice_bitcast_fusion.piece_ref
  98.8 35.9 %shard_map.91 = bf16[128,16,768]{2,1,0:T(8,128)(2,1)} custom-call(bf16[16,768]{1,0:T(8,128)(2,1)} %dynamic-slice_bitcast_fusion.piece_ref), custom_call_target="tpu_custom_call" | custom-call | tf_op jit(solution)/shard_map/pallas_call | solution.py:85
  134.7 2.7 %slice_bitcast_fusion.inc_ref = bf16[1024,768]{1,0:T(8,128)(2,1)} fusion(bf16[128,24,768]{2,1,0:T(8,128)(2,1)} %all-to-all-done), kind=kLoop, calls=%fused_computation.2 | loop fusion | bytes 3145728 | tf_op jit(solution)/shard_map/reshape | solution.py:168
  137.4 19.8 %shard_map.92 = bf16[2048,768]{1,0:T(8,128)(2,1)} custom-call(s32[32]{0:T(128)} %reshape.187.cols_ref, bf16[8,4,256,256]{3,2,1,0:T(8,128)(2,1)} %w_ref.1, bf16[8,256,768]{2,1,0:T(8,128)(2,1)} %bitcast.23, bf16[2048,1024]{1,0:T(8,128)(2,1)} %sw_ref.1, bf16[1024,768]{1,0:T(8,128)(2,1)} %slice_bitcast_fusion.inc_ref, bf16[768,768]{1,0:T(8,128)(2,1)} %weight_ref.1, ...), custom_call_target="tpu_custom_call" | custom-call | tf_op jit(solution)/shard_map/pallas_call | solution.py:128
  (4 shorter events, 0.1 us)
Async XLA Ops:
  0.0 7.7 %copy-start = (bf16[2048,768]{1,0:T(8,128)(2,1)S(1)}, bf16[2048,768]{1,0:T(8,128)(2,1)}, u32[]{:S(2)}) copy-start(bf16[2048,768]{1,0:T(8,128)(2,1)} %param.9) | copy-start | bytes 9437188
  7.7 13.6 %copy-start.3 = (s32[1,128]{1,0:T(1,128)S(1)}, s32[1,128]{1,0:T(1,128)}, u32[]{:S(2)}) copy-start(s32[1,128]{1,0:T(1,128)} %param.15) | copy-start | bytes 1540
  27.1 11.9 %copy-start.4 = (s32[8]{0:T(128)S(1)}, s32[8]{0:T(128)}, u32[]{:S(2)}) copy-start(s32[8]{0:T(128)} %param.12) | copy-start | bytes 100
  27.1 15.1 %copy-start.2 = (s32[8,4]{0,1:T(4,128)S(1)}, s32[8,4]{0,1:T(4,128)}, u32[]{:S(2)}) copy-start(s32[8,4]{0,1:T(4,128)} %param.11) | copy-start | bytes 388
  27.1 15.9 %copy-start.1 = (f32[768]{0:T(1024)S(1)}, f32[768]{0:T(1024)}, u32[]{:S(2)}) copy-start(f32[768]{0:T(1024)} %param.17) | copy-start | bytes 9220
  27.1 70.3 %all-to-all-start = ((bf16[128,24,768]{2,1,0:T(8,128)(2,1)}), bf16[128,24,768]{2,1,0:T(8,128)(2,1)}, u32[]{:S(2)}, u32[]{:S(2)}) async-start(bf16[128,24,768]{2,1,0:T(8,128)(2,1)} %broadcast_select_fusion), calls=%async_computation | async-start | bytes 9437184 | tf_op jit(solution)/shard_map/all_to_all | solution.py:167

commit v7 on v5

--- a/solution.py
+++ b/solution.py
@@ -161,15 +161,16 @@
     candidates = local_blocks[dense_ids % block_count]
     stripe_pieces = candidates.reshape(peer_count, piece, feature_width)
 
+    stripe_arrived = lax.all_to_all(stripe_pieces, AXES, split_axis=0, concat_axis=0, tiled=True)
+    my_owner = dense_ids[me * piece // tile_size] // block_count
+    my_piece = lax.dynamic_index_in_dim(stripe_arrived, my_owner, 0, keepdims=False)
+
     outgoing = features[rows_out]
     slot_ids = jnp.arange(slot_count, dtype=jnp.int32)
     live_slots = slot_ids[None, :] < counts_out[:, None]
     outgoing = jnp.where(live_slots[:, :, None], outgoing, jnp.zeros((), outgoing.dtype))
-    payload = jnp.concatenate([outgoing, stripe_pieces], axis=1)
-    arrived = lax.all_to_all(payload, AXES, split_axis=0, concat_axis=0, tiled=True)
-    incoming_rows = arrived[:, :slot_count].reshape(peer_count * slot_count, feature_width)
-    my_owner = dense_ids[me * piece // tile_size] // block_count
-    my_piece = lax.dynamic_index_in_dim(arrived, my_owner, 0, keepdims=False)[slot_count:]
+    arrived = lax.all_to_all(outgoing, AXES, split_axis=0, concat_axis=0, tiled=True)
+    incoming_rows = arrived.reshape(peer_count * slot_count, feature_width)
     dense_bands = gather_pieces(my_piece, peer_count, group).reshape(
         stripe_count, tile_size, feature_width
     )

time: 148 us -> 134 us (0.905)
  waiting for transfers between devices: 53.8 us -> 33 us
  Pallas kernels: 55.7 us -> 65 us
  other arithmetic: 9.85 us -> 3.71 us
  starting transfers between devices: 11.9 us -> 16.5 us
  local copies, waits for them, and re-layouts: 13.8 us -> 12.2 us
    all_to_all x1 -> x2, waiting for transfers between devices: 53.8 us -> 33 us  [the longest x1 33 us: on_device(): lax.all_to_all(stripe_pieces, AXES, split_axis=0, concat_axis=0, tiled=True)]
    pallas_call x1, Pallas kernels: 35.9 us -> 45.2 us  [gather_pieces(): pl.pallas_call(functools.partial(gather_kernel, group), out_shape=jax.Sha...]
    concatenate x1 -> x0, other arithmetic: 4.81 us -> none  [on_device(): payload = jnp.concatenate([outgoing, stripe_pieces], axis=1)]
    all_to_all x1 -> x2, starting transfers between devices: 11.9 us -> 16.5 us  [the longest x1 11.9 us: on_device(): lax.all_to_all(stripe_pieces, AXES, split_axis=0, concat_axis=0, tiled=True)]
    reshape x1 -> x0, local copies, waits for them, and re-layouts: 2.73 us -> none  [on_device(): arrived[:, :slot_count].reshape(peer_count * slot_count, feature_width)]
  transfers between devices with their start and end apart: 1 -> 2, of which waited for: 1 -> 1; matrix products, arithmetic and copies ran while one was open for 1% -> 9% of each run, Pallas kernels for 0% -> 34%
where the time goes in v7:
time: 134 us; the launch traced here: 133 us
  Pallas kernels  65 us (49%)
  waiting for transfers between devices  33 us (25%)
  starting transfers between devices  16.5 us (12%)
  local copies, waits for them, and re-layouts  12.2 us (9%)
  other arithmetic  3.71 us (3%)
  between operations  2.75 us (2%)
    pallas_call x1, Pallas kernels, gather_pieces(): pl.pallas_call(functools.partial(gather_kernel, group), out_shape=jax.Sha...  45.2 us
    all_to_all x1, waiting for transfers between devices, on_device(): lax.all_to_all(stripe_pieces, AXES, split_axis=0, concat_axis=0, tiled=True)  33 us
    pallas_call x1, Pallas kernels, fused_layer(): pl.pallas_call(functools.partial(layer_kernel, tiles_per), grid_spec=grid...  19.8 us
    all_to_all x1, starting transfers between devices, on_device(): lax.all_to_all(stripe_pieces, AXES, split_axis=0, concat_axis=0, tiled=True)  11.9 us
    gather x1, local copies, waits for them, and re-layouts, on_device(): outgoing = features[rows_out]  5.26 us
    all_to_all x1, starting transfers between devices, on_device(): lax.all_to_all(outgoing, AXES, split_axis=0, concat_axis=0, tiled=True)  4.65 us
    select_n x1, other arithmetic, on_device(): jnp.where(live_slots[:, :, None], outgoing, jnp.zeros((), outgoing.dtype))  2.79 us
  transfers between devices with their start and end apart: 2, of which 1 were waited for; matrix products, arithmetic and copies ran while one was open for 9% of the time, Pallas kernels for 34%

profile of v7, /device:TPU:1, one launch (start us, length us, event | category | flops | bytes accessed | tf_op | source)
XLA Modules:
  0.0 133.2 jit_solution(14230211119019814692)
XLA Ops:
  0.0 0.0 copy-start
  0.0 0.8 compare_select_fusion.1
  0.8 1.1 copy-done
  1.9 2.4 %gather_fusion = bf16[8,256,768]{2,1,0:T(8,128)(2,1)} fusion(bf16[8,256,768]{2,1,0:T(8,128)(2,1)S(1)} %bitcast.14, s32[1024]{0:T(1024)S(1)} %pad_clamp_fusion), kind=kCustom, calls=%fused_computation | custom fusion | bytes 6291488 | tf_op jit(solution)/shard_map/gather | solution.py:161
  4.3 0.0 copy-start.2
  4.3 11.9 %all-to-all-start = ((bf16[128,16,768]{2,1,0:T(8,128)(2,1)}), bf16[128,16,768]{2,1,0:T(8,128)(2,1)}, u32[]{:S(2)}, u32[]{:S(2)}) async-start(bf16[128,16,768]{2,1,0:T(8,128)(2,1)} %bitcast.15), calls=%async_computation | async-start | bytes 6291456 | tf_op jit(solution)/shard_map/all_to_all | solution.py:164
  16.2 0.0 copy-done.2
  16.2 0.1 copy.12
  16.4 0.1 reshape.86
  16.5 0.0 copy-start.4
  16.5 5.3 %gather_fusion.1 = bf16[1024,768]{1,0:T(8,128)(2,1)} fusion(bf16[2048,768]{1,0:T(8,128)(2,1)S(1)} %copy-done, s32[1024]{0:T(1024)S(1)} %broadcast_clamp_fusion), kind=kCustom, calls=%fused_computation.1 | custom fusion | bytes 3149824 | tf_op jit(solution)/shard_map/gather | solution.py:168
  21.7 0.0 copy-done.4
  21.7 0.1 iota_compare_fusion
  21.8 0.0 copy-start.5
  21.8 0.0 copy-start.3
  21.8 0.0 copy-start.1
  21.9 2.8 %bitcast_select_fusion = bf16[128,8,768]{2,1,0:T(8,128)(2,1)} fusion(bf16[1024,768]{1,0:T(8,128)(2,1)} %gather_fusion.1, pred[128,8]{1,0:T(8,128)(4,1)S(1)} %iota_compare_fusion), kind=kLoop, calls=%fused_computation.2 | loop fusion | flops 786432 | bytes 3146752 | tf_op jit(solution)/shard_map/jit(_where)/select_n | solution.py:171
  24.6 33.0 %all-to-all-done = bf16[128,16,768]{2,1,0:T(8,128)(2,1)} async-done(((bf16[128,16,768]{2,1,0:T(8,128)(2,1)}), bf16[128,16,768]{2,1,0:T(8,128)(2,1)}, u32[]{:S(2)}, u32[]{:S(2)}) %all-to-all-start) | async-done | bytes 3145760 | tf_op jit(solution)/shard_map/all_to_all | solution.py:164
  57.7 4.6 %all-to-all-start.1 = ((bf16[128,8,768]{2,1,0:T(8,128)(2,1)}), bf16[128,8,768]{2,1,0:T(8,128)(2,1)}, u32[]{:S(2)}, u32[]{:S(2)}) async-start(bf16[128,8,768]{2,1,0:T(8,128)(2,1)} %bitcast_select_fusion), calls=%async_computation.1 | async-start | bytes 3145728 | tf_op jit(solution)/shard_map/all_to_all | solution.py:172
  62.4 0.0 copy-done.5
  62.4 0.6 dynamic_slice.7
  65.6 0.0 copy-done.3
  65.6 0.1 copy.11
  65.6 0.6 reshape.70.cols_ref
  66.3 0.0 copy-done.1
  66.3 0.6 reshape.75.bias_ref
  66.8 1.3 %dynamic-slice_bitcast_fusion.piece_ref = bf16[16,768]{1,0:T(8,128)(2,1)} fusion(bf16[128,16,768]{2,1,0:T(8,128)(2,1)} %all-to-all-done, s32[]{:T(128)S(6)} %select_n.43), kind=kLoop, calls=%fused_computation.4 | loop fusion | bytes 49156 | tf_op jit(solution)/shard_map/jit(dynamic_index_in_dim)/squeeze | solution.py:166
  68.2 45.2 %shard_map.91 = bf16[128,16,768]{2,1,0:T(8,128)(2,1)} custom-call(bf16[16,768]{1,0:T(8,128)(2,1)} %dynamic-slice_bitcast_fusion.piece_ref), custom_call_target="tpu_custom_call" | custom-call | tf_op jit(solution)/shard_map/pallas_call | solution.py:85
  113.4 0.0 all-to-all-done.1
  113.4 19.8 %shard_map.92 = bf16[2048,768]{1,0:T(8,128)(2,1)} custom-call(s32[32]{0:T(128)} %reshape.70.cols_ref, bf16[8,4,256,256]{3,2,1,0:T(8,128)(2,1)} %w_ref.1, bf16[8,256,768]{2,1,0:T(8,128)(2,1)} %bitcast.16, bf16[2048,1024]{1,0:T(8,128)(2,1)} %sw_ref.1, bf16[1024,768]{1,0:T(8,128)(2,1)} %bitcast.8.inc_ref, bf16[768,768]{1,0:T(8,128)(2,1)} %weight_ref.1, ...), custom_call_target="tpu_custom_call" | custom-call | tf_op jit(solution)/shard_map/pallas_call | solution.py:128
  (3 shorter events, 0.0 us)
Async XLA Ops:
  0.0 1.9 %copy-start = (bf16[2048,768]{1,0:T(8,128)(2,1)S(1)}, bf16[2048,768]{1,0:T(8,128)(2,1)}, u32[]{:S(2)}) copy-start(bf16[2048,768]{1,0:T(8,128)(2,1)} %param.9) | copy-start | bytes 9437188
  4.3 11.9 %copy-start.2 = (s32[1,128,8]{1,2,0:T(8,128)S(1)}, s32[1,128,8]{1,2,0:T(8,128)}, u32[]{:S(2)}) copy-start(s32[1,128,8]{1,2,0:T(8,128)} %param.14) | copy-start | bytes 12292
  4.3 53.4 %all-to-all-start = ((bf16[128,16,768]{2,1,0:T(8,128)(2,1)}), bf16[128,16,768]{2,1,0:T(8,128)(2,1)}, u32[]{:S(2)}, u32[]{:S(2)}) async-start(bf16[128,16,768]{2,1,0:T(8,128)(2,1)} %bitcast.15), calls=%async_computation | async-start | bytes 6291456 | tf_op jit(solution)/shard_map/all_to_all | solution.py:164
  16.5 5.3 %copy-start.4 = (s32[1,128]{1,0:T(1,128)S(1)}, s32[1,128]{1,0:T(1,128)}, u32[]{:S(2)}) copy-start(s32[1,128]{1,0:T(1,128)} %param.15) | copy-start | bytes 1540
  21.8 40.5 %copy-start.5 = (s32[8]{0:T(128)S(1)}, s32[8]{0:T(128)}, u32[]{:S(2)}) copy-start(s32[8]{0:T(128)} %param.12) | copy-start | bytes 100
  21.8 43.7 %copy-start.3 = (s32[8,4]{0,1:T(4,128)S(1)}, s32[8,4]{0,1:T(4,128)}, u32[]{:S(2)}) copy-start(s32[8,4]{0,1:T(4,128)} %param.11) | copy-start | bytes 388
  21.8 44.4 %copy-start.1 = (f32[768]{0:T(1024)S(1)}, f32[768]{0:T(1024)}, u32[]{:S(2)}) copy-start(f32[768]{0:T(1024)} %param.17) | copy-start | bytes 9220
  57.7 55.7 %all-to-all-start.1 = ((bf16[128,8,768]{2,1,0:T(8,128)(2,1)}), bf16[128,8,768]{2,1,0:T(8,128)(2,1)}, u32[]{:S(2)}, u32[]{:S(2)}) async-start(bf16[128,8,768]{2,1,0:T(8,128)(2,1)} %bitcast_select_fusion), calls=%async_computation.1 | async-start | bytes 3145728 | tf_op jit(solution)/shard_map/all_to_all | solution.py:172

commit v8 on v7

--- a/solution.py
+++ b/solution.py
@@ -96,15 +96,17 @@
         compiler_params=pltpu.CompilerParams(collective_id=0, has_side_effects=True),
     )(piece)
 
-def layer_kernel(tiles_per, cols_ref, w_ref, bands_ref, sw_ref, inc_ref, weight_ref, bias_ref, out_ref):
-    block = pl.program_id(0)
-    total = jnp.dot(sw_ref[...], inc_ref[...], preferred_element_type=jnp.float32)
-    for tile_index in range(tiles_per):
-        col = cols_ref[block * tiles_per + tile_index]
-        total = total + jnp.dot(w_ref[0, tile_index], bands_ref[col], preferred_element_type=jnp.float32)
-    aggregate = total.astype(jnp.bfloat16)
-    result = jnp.dot(aggregate, weight_ref[...], preferred_element_type=jnp.float32) + bias_ref[...]
-    out_ref[...] = jnp.maximum(result, 0.0).astype(out_ref.dtype)
+def layer_kernel(tiles_per, tile_size, step_blocks, cols_ref, w_ref, bands_ref, sw_ref, inc_ref, weight_ref, bias_ref, out_ref):
+    step = pl.program_id(0)
+    for half in range(step_blocks):
+        rows = pl.ds(half * tile_size, tile_size)
+        total = jnp.dot(sw_ref[rows], inc_ref[...], preferred_element_type=jnp.float32)
+        for tile_index in range(tiles_per):
+            col = cols_ref[(step * step_blocks + half) * tiles_per + tile_index]
+            total = total + jnp.dot(w_ref[half, tile_index], bands_ref[col], preferred_element_type=jnp.float32)
+        aggregate = total.astype(jnp.bfloat16)
+        result = jnp.dot(aggregate, weight_ref[...], preferred_element_type=jnp.float32) + bias_ref[...]
+        out_ref[rows] = jnp.maximum(result, 0.0).astype(out_ref.dtype)
 
 
 def fused_layer(dense_cols, dense_edge_weights, dense_bands, sparse_w, incoming_rows, weight, bias):
@@ -112,25 +114,25 @@
     stripe_count, _, width = dense_bands.shape
     slots = incoming_rows.shape[0]
     out_width = weight.shape[1]
+    step_blocks = 2 if block_count % 2 == 0 else 1
     grid_spec = pltpu.PrefetchScalarGridSpec(
         num_scalar_prefetch=1,
-        grid=(block_count,),
+        grid=(block_count // step_blocks,),
         in_specs=[
-            pl.BlockSpec((1, tiles_per, tile_size, tile_size), lambda b, cols: (b, 0, 0, 0)),
+            pl.BlockSpec((step_blocks, tiles_per, tile_size, tile_size), lambda b, cols: (b, 0, 0, 0)),
             pl.BlockSpec((stripe_count, tile_size, width), lambda b, cols: (0, 0, 0)),
-            pl.BlockSpec((tile_size, slots), lambda b, cols: (b, 0)),
+            pl.BlockSpec((step_blocks * tile_size, slots), lambda b, cols: (b, 0)),
             pl.BlockSpec((slots, width), lambda b, cols: (0, 0)),
             pl.BlockSpec((width, out_width), lambda b, cols: (0, 0)),
             pl.BlockSpec((1, out_width), lambda b, cols: (0, 0)),
         ],
-        out_specs=pl.BlockSpec((tile_size, out_width), lambda b, cols: (b, 0)),
+        out_specs=pl.BlockSpec((step_blocks * tile_size, out_width), lambda b, cols: (b, 0)),
     )
     return pl.pallas_call(
-        functools.partial(layer_kernel, tiles_per),
+        functools.partial(layer_kernel, tiles_per, tile_size, step_blocks),
         grid_spec=grid_spec,
         out_shape=jax.ShapeDtypeStruct((block_count * tile_size, out_width), jnp.bfloat16),
     )(dense_cols.reshape(-1), dense_edge_weights, dense_bands, sparse_w, incoming_rows, weight, bias.reshape(1, -1))
-
 
 def on_device(
     features,

time: 134 us -> 131 us (0.978)
  Pallas kernels: 65 us -> 62.4 us
    pallas_call x1, Pallas kernels: 19.8 us -> 17.3 us  [fused_layer(): pl.pallas_call(functools.partial(layer_kernel, tiles_per, tile_size, step...]
  transfers between devices with their start and end apart: 2 -> 2, of which waited for: 1 -> 1; matrix products, arithmetic and copies ran while one was open for 9% -> 9% of each run, Pallas kernels for 34% -> 35%
where the time goes in v8:
time: 131 us
  Pallas kernels  62.4 us (48%)
  waiting for transfers between devices  33 us (25%)
  starting transfers between devices  16.5 us (13%)
  local copies, waits for them, and re-layouts  12.2 us (9%)
  other arithmetic  3.71 us (3%)
  between operations  2.75 us (2%)
    pallas_call x1, Pallas kernels, gather_pieces(): pl.pallas_call(functools.partial(gather_kernel, group), out_shape=jax.Sha...  45.2 us
    all_to_all x1, waiting for transfers between devices, on_device(): lax.all_to_all(stripe_pieces, AXES, split_axis=0, concat_axis=0, tiled=True)  33 us
    pallas_call x1, Pallas kernels, fused_layer(): pl.pallas_call(functools.partial(layer_kernel, tiles_per, tile_size, step...  17.3 us
    all_to_all x1, starting transfers between devices, on_device(): lax.all_to_all(stripe_pieces, AXES, split_axis=0, concat_axis=0, tiled=True)  11.9 us
    gather x1, local copies, waits for them, and re-layouts, on_device(): outgoing = features[rows_out]  5.26 us
    all_to_all x1, starting transfers between devices, on_device(): lax.all_to_all(outgoing, AXES, split_axis=0, concat_axis=0, tiled=True)  4.65 us
    select_n x1, other arithmetic, on_device(): jnp.where(live_slots[:, :, None], outgoing, jnp.zeros((), outgoing.dtype))  2.79 us
  transfers between devices with their start and end apart: 2, of which 1 were waited for; matrix products, arithmetic and copies ran while one was open for 9% of the time, Pallas kernels for 35%

profile of v8, /device:TPU:1, one launch (start us, length us, event | category | flops | bytes accessed | tf_op | source)
XLA Modules:
  0.0 130.6 jit_solution(16822900817517657518)
XLA Ops:
  0.0 0.0 copy-start
  0.0 0.8 compare_select_fusion.1
  0.8 1.1 copy-done
  1.9 2.4 %gather_fusion = bf16[8,256,768]{2,1,0:T(8,128)(2,1)} fusion(bf16[8,256,768]{2,1,0:T(8,128)(2,1)S(1)} %bitcast.14, s32[1024]{0:T(1024)S(1)} %pad_clamp_fusion), kind=kCustom, calls=%fused_computation | custom fusion | bytes 6291488 | tf_op jit(solution)/shard_map/gather | solution.py:163
  4.3 0.0 copy-start.2
  4.3 11.9 %all-to-all-start = ((bf16[128,16,768]{2,1,0:T(8,128)(2,1)}), bf16[128,16,768]{2,1,0:T(8,128)(2,1)}, u32[]{:S(2)}, u32[]{:S(2)}) async-start(bf16[128,16,768]{2,1,0:T(8,128)(2,1)} %bitcast.15), calls=%async_computation | async-start | bytes 6291456 | tf_op jit(solution)/shard_map/all_to_all | solution.py:166
  16.2 0.0 copy-done.2
  16.2 0.1 copy.12
  16.4 0.1 reshape.86
  16.5 0.0 copy-start.4
  16.5 5.3 %gather_fusion.1 = bf16[1024,768]{1,0:T(8,128)(2,1)} fusion(bf16[2048,768]{1,0:T(8,128)(2,1)S(1)} %copy-done, s32[1024]{0:T(1024)S(1)} %broadcast_clamp_fusion), kind=kCustom, calls=%fused_computation.1 | custom fusion | bytes 3149824 | tf_op jit(solution)/shard_map/gather | solution.py:170
  21.7 0.0 copy-done.4
  21.7 0.1 iota_compare_fusion
  21.8 0.0 copy-start.5
  21.8 0.0 copy-start.3
  21.8 0.0 copy-start.1
  21.9 2.8 %bitcast_select_fusion = bf16[128,8,768]{2,1,0:T(8,128)(2,1)} fusion(bf16[1024,768]{1,0:T(8,128)(2,1)} %gather_fusion.1, pred[128,8]{1,0:T(8,128)(4,1)S(1)} %iota_compare_fusion), kind=kLoop, calls=%fused_computation.2 | loop fusion | flops 786432 | bytes 3146752 | tf_op jit(solution)/shard_map/jit(_where)/select_n | solution.py:173
  24.6 33.0 %all-to-all-done = bf16[128,16,768]{2,1,0:T(8,128)(2,1)} async-done(((bf16[128,16,768]{2,1,0:T(8,128)(2,1)}), bf16[128,16,768]{2,1,0:T(8,128)(2,1)}, u32[]{:S(2)}, u32[]{:S(2)}) %all-to-all-start) | async-done | bytes 3145760 | tf_op jit(solution)/shard_map/all_to_all | solution.py:166
  57.7 4.6 %all-to-all-start.1 = ((bf16[128,8,768]{2,1,0:T(8,128)(2,1)}), bf16[128,8,768]{2,1,0:T(8,128)(2,1)}, u32[]{:S(2)}, u32[]{:S(2)}) async-start(bf16[128,8,768]{2,1,0:T(8,128)(2,1)} %bitcast_select_fusion), calls=%async_computation.1 | async-start | bytes 3145728 | tf_op jit(solution)/shard_map/all_to_all | solution.py:174
  62.4 0.0 copy-done.5
  62.4 0.6 dynamic_slice.7
  65.6 0.0 copy-done.3
  65.6 0.1 copy.11
  65.6 0.6 reshape.70.cols_ref
  66.3 0.0 copy-done.1
  66.3 0.6 reshape.75.bias_ref
  66.8 1.3 %dynamic-slice_bitcast_fusion.piece_ref = bf16[16,768]{1,0:T(8,128)(2,1)} fusion(bf16[128,16,768]{2,1,0:T(8,128)(2,1)} %all-to-all-done, s32[]{:T(128)S(6)} %select_n.43), kind=kLoop, calls=%fused_computation.4 | loop fusion | bytes 49156 | tf_op jit(solution)/shard_map/jit(dynamic_index_in_dim)/squeeze | solution.py:168
  68.2 45.2 %shard_map.91 = bf16[128,16,768]{2,1,0:T(8,128)(2,1)} custom-call(bf16[16,768]{1,0:T(8,128)(2,1)} %dynamic-slice_bitcast_fusion.piece_ref), custom_call_target="tpu_custom_call" | custom-call | tf_op jit(solution)/shard_map/pallas_call | solution.py:85
  113.4 0.0 all-to-all-done.1
  113.4 17.3 %shard_map.92 = bf16[2048,768]{1,0:T(8,128)(2,1)} custom-call(s32[32]{0:T(128)} %reshape.70.cols_ref, bf16[8,4,256,256]{3,2,1,0:T(8,128)(2,1)} %w_ref.1, bf16[8,256,768]{2,1,0:T(8,128)(2,1)} %bitcast.16, bf16[2048,1024]{1,0:T(8,128)(2,1)} %sw_ref.1, bf16[1024,768]{1,0:T(8,128)(2,1)} %bitcast.8.inc_ref, bf16[768,768]{1,0:T(8,128)(2,1)} %weight_ref.1, ...), custom_call_target="tpu_custom_call" | custom-call | tf_op jit(solution)/shard_map/pallas_call | solution.py:131
  (3 shorter events, 0.0 us)
Async XLA Ops:
  0.0 1.9 %copy-start = (bf16[2048,768]{1,0:T(8,128)(2,1)S(1)}, bf16[2048,768]{1,0:T(8,128)(2,1)}, u32[]{:S(2)}) copy-start(bf16[2048,768]{1,0:T(8,128)(2,1)} %param.9) | copy-start | bytes 9437188
  4.3 11.9 %copy-start.2 = (s32[1,128,8]{1,2,0:T(8,128)S(1)}, s32[1,128,8]{1,2,0:T(8,128)}, u32[]{:S(2)}) copy-start(s32[1,128,8]{1,2,0:T(8,128)} %param.14) | copy-start | bytes 12292
  4.3 53.4 %all-to-all-start = ((bf16[128,16,768]{2,1,0:T(8,128)(2,1)}), bf16[128,16,768]{2,1,0:T(8,128)(2,1)}, u32[]{:S(2)}, u32[]{:S(2)}) async-start(bf16[128,16,768]{2,1,0:T(8,128)(2,1)} %bitcast.15), calls=%async_computation | async-start | bytes 6291456 | tf_op jit(solution)/shard_map/all_to_all | solution.py:166
  16.5 5.3 %copy-start.4 = (s32[1,128]{1,0:T(1,128)S(1)}, s32[1,128]{1,0:T(1,128)}, u32[]{:S(2)}) copy-start(s32[1,128]{1,0:T(1,128)} %param.15) | copy-start | bytes 1540
  21.8 40.5 %copy-start.5 = (s32[8]{0:T(128)S(1)}, s32[8]{0:T(128)}, u32[]{:S(2)}) copy-start(s32[8]{0:T(128)} %param.12) | copy-start | bytes 100
  21.8 43.7 %copy-start.3 = (s32[8,4]{0,1:T(4,128)S(1)}, s32[8,4]{0,1:T(4,128)}, u32[]{:S(2)}) copy-start(s32[8,4]{0,1:T(4,128)} %param.11) | copy-start | bytes 388
  21.8 44.4 %copy-start.1 = (f32[768]{0:T(1024)S(1)}, f32[768]{0:T(1024)}, u32[]{:S(2)}) copy-start(f32[768]{0:T(1024)} %param.17) | copy-start | bytes 9220
  57.7 55.7 %all-to-all-start.1 = ((bf16[128,8,768]{2,1,0:T(8,128)(2,1)}), bf16[128,8,768]{2,1,0:T(8,128)(2,1)}, u32[]{:S(2)}, u32[]{:S(2)}) async-start(bf16[128,8,768]{2,1,0:T(8,128)(2,1)} %bitcast_select_fusion), calls=%async_computation.1 | async-start | bytes 3145728 | tf_op jit(solution)/shard_map/all_to_all | solution.py:174

commit v9 on v8

--- a/solution.py
+++ b/solution.py
@@ -95,6 +95,66 @@
         ],
         compiler_params=pltpu.CompilerParams(collective_id=0, has_side_effects=True),
     )(piece)
+
+def exchange_kernel(group, pay_ref, out_ref, send_sem, recv_sem, local_sem):
+    n = out_ref.shape[0]
+    me = lax.axis_index(AXES)
+    mesh_ids = pl.DeviceIdType.MESH
+
+    def where(k):
+        return (k // group, k % group)
+
+    barrier = pltpu.get_barrier_semaphore()
+
+    def greet(i, carry):
+        peer = lax.rem(me + i, n)
+        pl.semaphore_signal(barrier, inc=1, device_id=where(peer), device_id_type=mesh_ids)
+        return carry
+
+    lax.fori_loop(1, n, greet, 0)
+    pl.semaphore_wait(barrier, n - 1)
+    own = pltpu.make_async_copy(pay_ref.at[me], out_ref.at[me], local_sem)
+    own.start()
+
+    def send(i, carry):
+        peer = lax.rem(me + i, n)
+        pltpu.make_async_remote_copy(
+            src_ref=pay_ref.at[peer], dst_ref=out_ref.at[me], send_sem=send_sem.at[i],
+            recv_sem=recv_sem.at[me], device_id=where(peer), device_id_type=mesh_ids,
+        ).start()
+        return carry
+
+    lax.fori_loop(1, n, send, 0)
+
+    def wait(i, carry):
+        peer = lax.rem(me + i, n)
+        source = lax.rem(me + n - i, n)
+        pltpu.make_async_remote_copy(
+            src_ref=pay_ref.at[peer], dst_ref=out_ref.at[source], send_sem=send_sem.at[i],
+            recv_sem=recv_sem.at[source], device_id=where(peer), device_id_type=mesh_ids,
+        ).wait()
+        return carry
+
+    lax.fori_loop(1, n, wait, 0)
+    own.wait()
+
+
+def exchange_rows(payload, group):
+    n = payload.shape[0]
+    return pl.pallas_call(
+        functools.partial(exchange_kernel, group),
+        out_shape=jax.ShapeDtypeStruct(payload.shape, payload.dtype),
+        in_specs=[pl.BlockSpec(memory_space=pltpu.VMEM)],
+        out_specs=pl.BlockSpec(memory_space=pltpu.VMEM),
+        scratch_shapes=[
+            pltpu.SemaphoreType.DMA((n,)),
+            pltpu.SemaphoreType.DMA((n,)),
+            pltpu.SemaphoreType.DMA,
+        ],
+        cost_estimate=pl.CostEstimate(flops=0, transcendentals=0, bytes_accessed=2 * payload.size * payload.dtype.itemsize),
+        compiler_params=pltpu.CompilerParams(collective_id=1, has_side_effects=True),
+    )(payload)
+
 
 def layer_kernel(tiles_per, tile_size, step_blocks, cols_ref, w_ref, bands_ref, sw_ref, inc_ref, weight_ref, bias_ref, out_ref):
     step = pl.program_id(0)
@@ -171,7 +231,7 @@
     slot_ids = jnp.arange(slot_count, dtype=jnp.int32)
     live_slots = slot_ids[None, :] < counts_out[:, None]
     outgoing = jnp.where(live_slots[:, :, None], outgoing, jnp.zeros((), outgoing.dtype))
-    arrived = lax.all_to_all(outgoing, AXES, split_axis=0, concat_axis=0, tiled=True)
+    arrived = exchange_rows(outgoing, group)
     incoming_rows = arrived.reshape(peer_count * slot_count, feature_width)
     dense_bands = gather_pieces(my_piece, peer_count, group).reshape(
         stripe_count, tile_size, feature_width

time: 131 us -> 138 us (1.053)
  Pallas kernels: 62.4 us -> 107 us
  waiting for transfers between devices: 33 us -> 0.01 us
  starting transfers between devices: 16.5 us -> 11.9 us
    pallas_call x0 -> x1, Pallas kernels: none -> 53.1 us  [exchange_rows(): pl.pallas_call(functools.partial(exchange_kernel, group), out_shape=jax.S...]
    all_to_all x1, waiting for transfers between devices: 33 us -> 0.01 us  [on_device(): lax.all_to_all(stripe_pieces, AXES, split_axis=0, concat_axis=0, tiled=True)]
    pallas_call x1, Pallas kernels: 45.2 us -> 36.5 us  [gather_pieces(): pl.pallas_call(functools.partial(gather_kernel, group), out_shape=jax.Sha...]
    all_to_all x1 -> x0, starting transfers between devices: 4.65 us -> none  [on_device(): lax.all_to_all(outgoing, AXES, split_axis=0, concat_axis=0, tiled=True)]
  transfers between devices with their start and end apart: 2 -> 1, of which waited for: 1 -> 0; matrix products, arithmetic and copies ran while one was open for 9% -> 7% of each run, Pallas kernels for 35% -> 39%
where the time goes in v9:
time: 138 us; the launch traced here: 137 us
  Pallas kernels  107 us (78%)
  local copies, waits for them, and re-layouts  12.2 us (9%)
  starting transfers between devices  11.9 us (9%)
  other arithmetic  3.72 us (3%)
  between operations  2.39 us (2%)
    pallas_call x1, Pallas kernels, exchange_rows(): pl.pallas_call(functools.partial(exchange_kernel, group), out_shape=jax.S...  53.1 us
    pallas_call x1, Pallas kernels, gather_pieces(): pl.pallas_call(functools.partial(gather_kernel, group), out_shape=jax.Sha...  36.5 us
    pallas_call x1, Pallas kernels, fused_layer(): pl.pallas_call(functools.partial(layer_kernel, tiles_per, tile_size, step...  17.3 us
    all_to_all x1, starting transfers between devices, on_device(): lax.all_to_all(stripe_pieces, AXES, split_axis=0, concat_axis=0, tiled=True)  11.9 us
    gather x1, local copies, waits for them, and re-layouts, on_device(): outgoing = features[rows_out]  5.23 us
    select_n x1, other arithmetic, on_device(): jnp.where(live_slots[:, :, None], outgoing, jnp.zeros((), outgoing.dtype))  2.8 us
  transfers between devices with their start and end apart: 1, of which 0 were waited for; matrix products, arithmetic and copies ran while one was open for 7% of the time, Pallas kernels for 39%

profile of v9, /device:TPU:1, one launch (start us, length us, event | category | flops | bytes accessed | tf_op | source)
XLA Modules:
  0.0 137.1 jit_solution(15286453413601994872)
XLA Ops:
  0.0 0.0 copy-start
  0.0 0.8 compare_select_fusion.1
  0.8 1.1 copy-done
  1.9 2.4 %gather_fusion = bf16[8,256,768]{2,1,0:T(8,128)(2,1)} fusion(bf16[8,256,768]{2,1,0:T(8,128)(2,1)S(1)} %bitcast.14, s32[1024]{0:T(1024)S(1)} %pad_clamp_fusion), kind=kCustom, calls=%fused_computation | custom fusion | bytes 6291488 | tf_op jit(solution)/shard_map/gather | solution.py:223
  4.3 0.0 copy-start.5
  4.3 0.0 copy-start.2
  4.3 11.9 %all-to-all-start = ((bf16[128,16,768]{2,1,0:T(8,128)(2,1)}), bf16[128,16,768]{2,1,0:T(8,128)(2,1)}, u32[]{:S(2)}, u32[]{:S(2)}) async-start(bf16[128,16,768]{2,1,0:T(8,128)(2,1)} %bitcast.15), calls=%async_computation | async-start | bytes 6291456 | tf_op jit(solution)/shard_map/all_to_all | solution.py:226
  16.2 0.0 copy-done.5
  16.3 0.6 dynamic_slice.7
  19.1 0.0 copy-done.2
  19.1 0.1 copy.12
  19.2 0.1 reshape.86
  19.3 0.0 copy-start.4
  19.4 5.2 %gather_fusion.1 = bf16[1024,768]{1,0:T(8,128)(2,1)} fusion(bf16[2048,768]{1,0:T(8,128)(2,1)S(1)} %copy-done, s32[1024]{0:T(1024)S(1)} %broadcast_clamp_fusion), kind=kCustom, calls=%fused_computation.1 | custom fusion | bytes 3149824 | tf_op jit(solution)/shard_map/gather | solution.py:230
  24.6 0.0 copy-done.4
  24.6 0.1 iota_compare_fusion
  24.7 0.0 copy-start.3
  24.7 0.0 copy-start.1
  24.7 2.8 %bitcast_select_fusion.pay_ref = bf16[128,8,768]{2,1,0:T(8,128)(2,1)} fusion(bf16[1024,768]{1,0:T(8,128)(2,1)} %gather_fusion.1, pred[128,8]{1,0:T(8,128)(4,1)S(1)} %iota_compare_fusion), kind=kLoop, calls=%fused_computation.2 | loop fusion | flops 786432 | bytes 3146752 | tf_op jit(solution)/shard_map/jit(_where)/select_n | solution.py:233
  27.5 53.1 %shard_map.92 = bf16[128,8,768]{2,1,0:T(8,128)(2,1)} custom-call(bf16[128,8,768]{2,1,0:T(8,128)(2,1)} %bitcast_select_fusion.pay_ref), custom_call_target="tpu_custom_call" | custom-call | bytes 3145728 | tf_op jit(solution)/shard_map/pallas_call | solution.py:144
  80.6 0.0 copy-done.3
  80.7 0.1 copy.11
  80.7 0.7 reshape.70.cols_ref
  81.4 0.0 copy-done.1
  81.4 0.6 reshape.75.bias_ref
  82.0 0.0 all-to-all-done
  82.0 1.3 dynamic-slice_bitcast_fusion.piece_ref
  83.4 36.5 %shard_map.91 = bf16[128,16,768]{2,1,0:T(8,128)(2,1)} custom-call(bf16[16,768]{1,0:T(8,128)(2,1)} %dynamic-slice_bitcast_fusion.piece_ref), custom_call_target="tpu_custom_call" | custom-call | tf_op jit(solution)/shard_map/pallas_call | solution.py:85
  119.9 17.3 %shard_map.93 = bf16[2048,768]{1,0:T(8,128)(2,1)} custom-call(s32[32]{0:T(128)} %reshape.70.cols_ref, bf16[8,4,256,256]{3,2,1,0:T(8,128)(2,1)} %w_ref.1, bf16[8,256,768]{2,1,0:T(8,128)(2,1)} %bitcast.16, bf16[2048,1024]{1,0:T(8,128)(2,1)} %sw_ref.1, bf16[1024,768]{1,0:T(8,128)(2,1)} %bitcast.17, bf16[768,768]{1,0:T(8,128)(2,1)} %weight_ref.1, ...), custom_call_target="tpu_custom_call" | custom-call | tf_op jit(solution)/shard_map/pallas_call | solution.py:191
  (3 shorter events, 0.0 us)
Async XLA Ops:
  0.0 1.9 %copy-start = (bf16[2048,768]{1,0:T(8,128)(2,1)S(1)}, bf16[2048,768]{1,0:T(8,128)(2,1)}, u32[]{:S(2)}) copy-start(bf16[2048,768]{1,0:T(8,128)(2,1)} %param.9) | copy-start | bytes 9437188
  4.3 11.9 %copy-start.5 = (s32[8]{0:T(128)S(1)}, s32[8]{0:T(128)}, u32[]{:S(2)}) copy-start(s32[8]{0:T(128)} %param.12) | copy-start | bytes 100
  4.3 14.8 %copy-start.2 = (s32[1,128,8]{1,2,0:T(8,128)S(1)}, s32[1,128,8]{1,2,0:T(8,128)}, u32[]{:S(2)}) copy-start(s32[1,128,8]{1,2,0:T(8,128)} %param.14) | copy-start | bytes 12292
  4.3 77.7 %all-to-all-start = ((bf16[128,16,768]{2,1,0:T(8,128)(2,1)}), bf16[128,16,768]{2,1,0:T(8,128)(2,1)}, u32[]{:S(2)}, u32[]{:S(2)}) async-start(bf16[128,16,768]{2,1,0:T(8,128)(2,1)} %bitcast.15), calls=%async_computation | async-start | bytes 6291456 | tf_op jit(solution)/shard_map/all_to_all | solution.py:226
  19.3 5.2 %copy-start.4 = (s32[1,128]{1,0:T(1,128)S(1)}, s32[1,128]{1,0:T(1,128)}, u32[]{:S(2)}) copy-start(s32[1,128]{1,0:T(1,128)} %param.15) | copy-start | bytes 1540
  24.7 56.0 %copy-start.3 = (s32[8,4]{0,1:T(4,128)S(1)}, s32[8,4]{0,1:T(4,128)}, u32[]{:S(2)}) copy-start(s32[8,4]{0,1:T(4,128)} %param.11) | copy-start | bytes 388
  24.7 56.7 %copy-start.1 = (f32[768]{0:T(1024)S(1)}, f32[768]{0:T(1024)}, u32[]{:S(2)}) copy-start(f32[768]{0:T(1024)} %param.17) | copy-start | bytes 9220

commit v10 on v8

--- a/solution.py
+++ b/solution.py
@@ -120,11 +120,11 @@
         grid=(block_count // step_blocks,),
         in_specs=[
             pl.BlockSpec((step_blocks, tiles_per, tile_size, tile_size), lambda b, cols: (b, 0, 0, 0)),
-            pl.BlockSpec((stripe_count, tile_size, width), lambda b, cols: (0, 0, 0)),
+            pl.BlockSpec(memory_space=pltpu.VMEM),
             pl.BlockSpec((step_blocks * tile_size, slots), lambda b, cols: (b, 0)),
-            pl.BlockSpec((slots, width), lambda b, cols: (0, 0)),
-            pl.BlockSpec((width, out_width), lambda b, cols: (0, 0)),
-            pl.BlockSpec((1, out_width), lambda b, cols: (0, 0)),
+            pl.BlockSpec(memory_space=pltpu.VMEM),
+            pl.BlockSpec(memory_space=pltpu.VMEM),
+            pl.BlockSpec(memory_space=pltpu.VMEM),
         ],
         out_specs=pl.BlockSpec((step_blocks * tile_size, out_width), lambda b, cols: (b, 0)),
     )

time: 131 us -> 131 us (level)
  no operation moved by 1% of the time
where the time goes in v10:
time: 131 us
  Pallas kernels  62.4 us (48%)
  waiting for transfers between devices  33 us (25%)
  starting transfers between devices  16.5 us (13%)
  local copies, waits for them, and re-layouts  12.2 us (9%)
  other arithmetic  3.71 us (3%)
  between operations  2.75 us (2%)
    pallas_call x1, Pallas kernels, gather_pieces(): pl.pallas_call(functools.partial(gather_kernel, group), out_shape=jax.Sha...  45.2 us
    all_to_all x1, waiting for transfers between devices, on_device(): lax.all_to_all(stripe_pieces, AXES, split_axis=0, concat_axis=0, tiled=True)  33 us
    pallas_call x1, Pallas kernels, fused_layer(): pl.pallas_call(functools.partial(layer_kernel, tiles_per, tile_size, step...  17.3 us
    all_to_all x1, starting transfers between devices, on_device(): lax.all_to_all(stripe_pieces, AXES, split_axis=0, concat_axis=0, tiled=True)  11.9 us
    gather x1, local copies, waits for them, and re-layouts, on_device(): outgoing = features[rows_out]  5.26 us
    all_to_all x1, starting transfers between devices, on_device(): lax.all_to_all(outgoing, AXES, split_axis=0, concat_axis=0, tiled=True)  4.65 us
    select_n x1, other arithmetic, on_device(): jnp.where(live_slots[:, :, None], outgoing, jnp.zeros((), outgoing.dtype))  2.79 us
  transfers between devices with their start and end apart: 2, of which 1 were waited for; matrix products, arithmetic and copies ran while one was open for 9% of the time, Pallas kernels for 35%

profile of v10, /device:TPU:1, one launch (start us, length us, event | category | flops | bytes accessed | tf_op | source)
XLA Modules:
  0.0 130.6 jit_solution(16822900817517657518)
XLA Ops:
  0.0 0.0 copy-start
  0.0 0.8 compare_select_fusion.1
  0.8 1.1 copy-done
  1.9 2.4 %gather_fusion = bf16[8,256,768]{2,1,0:T(8,128)(2,1)} fusion(bf16[8,256,768]{2,1,0:T(8,128)(2,1)S(1)} %bitcast.14, s32[1024]{0:T(1024)S(1)} %pad_clamp_fusion), kind=kCustom, calls=%fused_computation | custom fusion | bytes 6291488 | tf_op jit(solution)/shard_map/gather | solution.py:163
  4.3 0.0 copy-start.2
  4.3 11.9 %all-to-all-start = ((bf16[128,16,768]{2,1,0:T(8,128)(2,1)}), bf16[128,16,768]{2,1,0:T(8,128)(2,1)}, u32[]{:S(2)}, u32[]{:S(2)}) async-start(bf16[128,16,768]{2,1,0:T(8,128)(2,1)} %bitcast.15), calls=%async_computation | async-start | bytes 6291456 | tf_op jit(solution)/shard_map/all_to_all | solution.py:166
  16.2 0.0 copy-done.2
  16.2 0.1 copy.12
  16.4 0.1 reshape.86
  16.5 0.0 copy-start.4
  16.5 5.3 %gather_fusion.1 = bf16[1024,768]{1,0:T(8,128)(2,1)} fusion(bf16[2048,768]{1,0:T(8,128)(2,1)S(1)} %copy-done, s32[1024]{0:T(1024)S(1)} %broadcast_clamp_fusion), kind=kCustom, calls=%fused_computation.1 | custom fusion | bytes 3149824 | tf_op jit(solution)/shard_map/gather | solution.py:170
  21.7 0.0 copy-done.4
  21.7 0.1 iota_compare_fusion
  21.8 0.0 copy-start.5
  21.8 0.0 copy-start.3
  21.8 0.0 copy-start.1
  21.9 2.8 %bitcast_select_fusion = bf16[128,8,768]{2,1,0:T(8,128)(2,1)} fusion(bf16[1024,768]{1,0:T(8,128)(2,1)} %gather_fusion.1, pred[128,8]{1,0:T(8,128)(4,1)S(1)} %iota_compare_fusion), kind=kLoop, calls=%fused_computation.2 | loop fusion | flops 786432 | bytes 3146752 | tf_op jit(solution)/shard_map/jit(_where)/select_n | solution.py:173
  24.6 33.0 %all-to-all-done = bf16[128,16,768]{2,1,0:T(8,128)(2,1)} async-done(((bf16[128,16,768]{2,1,0:T(8,128)(2,1)}), bf16[128,16,768]{2,1,0:T(8,128)(2,1)}, u32[]{:S(2)}, u32[]{:S(2)}) %all-to-all-start) | async-done | bytes 3145760 | tf_op jit(solution)/shard_map/all_to_all | solution.py:166
  57.7 4.6 %all-to-all-start.1 = ((bf16[128,8,768]{2,1,0:T(8,128)(2,1)}), bf16[128,8,768]{2,1,0:T(8,128)(2,1)}, u32[]{:S(2)}, u32[]{:S(2)}) async-start(bf16[128,8,768]{2,1,0:T(8,128)(2,1)} %bitcast_select_fusion), calls=%async_computation.1 | async-start | bytes 3145728 | tf_op jit(solution)/shard_map/all_to_all | solution.py:174
  62.4 0.0 copy-done.5
  62.4 0.6 dynamic_slice.7
  65.6 0.0 copy-done.3
  65.6 0.1 copy.11
  65.6 0.6 reshape.70.cols_ref
  66.3 0.0 copy-done.1
  66.3 0.6 reshape.75.bias_ref
  66.8 1.3 %dynamic-slice_bitcast_fusion.piece_ref = bf16[16,768]{1,0:T(8,128)(2,1)} fusion(bf16[128,16,768]{2,1,0:T(8,128)(2,1)} %all-to-all-done, s32[]{:T(128)S(6)} %select_n.43), kind=kLoop, calls=%fused_computation.4 | loop fusion | bytes 49156 | tf_op jit(solution)/shard_map/jit(dynamic_index_in_dim)/squeeze | solution.py:168
  68.2 45.2 %shard_map.91 = bf16[128,16,768]{2,1,0:T(8,128)(2,1)} custom-call(bf16[16,768]{1,0:T(8,128)(2,1)} %dynamic-slice_bitcast_fusion.piece_ref), custom_call_target="tpu_custom_call" | custom-call | tf_op jit(solution)/shard_map/pallas_call | solution.py:85
  113.4 0.0 all-to-all-done.1
  113.4 17.3 %shard_map.92 = bf16[2048,768]{1,0:T(8,128)(2,1)} custom-call(s32[32]{0:T(128)} %reshape.70.cols_ref, bf16[8,4,256,256]{3,2,1,0:T(8,128)(2,1)} %w_ref.1, bf16[8,256,768]{2,1,0:T(8,128)(2,1)} %bitcast.16, bf16[2048,1024]{1,0:T(8,128)(2,1)} %sw_ref.1, bf16[1024,768]{1,0:T(8,128)(2,1)} %bitcast.8.inc_ref, bf16[768,768]{1,0:T(8,128)(2,1)} %weight_ref.1, ...), custom_call_target="tpu_custom_call" | custom-call | tf_op jit(solution)/shard_map/pallas_call | solution.py:131
  (3 shorter events, 0.0 us)
Async XLA Ops:
  0.0 1.9 %copy-start = (bf16[2048,768]{1,0:T(8,128)(2,1)S(1)}, bf16[2048,768]{1,0:T(8,128)(2,1)}, u32[]{:S(2)}) copy-start(bf16[2048,768]{1,0:T(8,128)(2,1)} %param.9) | copy-start | bytes 9437188
  4.3 11.9 %copy-start.2 = (s32[1,128,8]{1,2,0:T(8,128)S(1)}, s32[1,128,8]{1,2,0:T(8,128)}, u32[]{:S(2)}) copy-start(s32[1,128,8]{1,2,0:T(8,128)} %param.14) | copy-start | bytes 12292
  4.3 53.4 %all-to-all-start = ((bf16[128,16,768]{2,1,0:T(8,128)(2,1)}), bf16[128,16,768]{2,1,0:T(8,128)(2,1)}, u32[]{:S(2)}, u32[]{:S(2)}) async-start(bf16[128,16,768]{2,1,0:T(8,128)(2,1)} %bitcast.15), calls=%async_computation | async-start | bytes 6291456 | tf_op jit(solution)/shard_map/all_to_all | solution.py:166
  16.5 5.3 %copy-start.4 = (s32[1,128]{1,0:T(1,128)S(1)}, s32[1,128]{1,0:T(1,128)}, u32[]{:S(2)}) copy-start(s32[1,128]{1,0:T(1,128)} %param.15) | copy-start | bytes 1540
  21.8 40.5 %copy-start.5 = (s32[8]{0:T(128)S(1)}, s32[8]{0:T(128)}, u32[]{:S(2)}) copy-start(s32[8]{0:T(128)} %param.12) | copy-start | bytes 100
  21.8 43.7 %copy-start.3 = (s32[8,4]{0,1:T(4,128)S(1)}, s32[8,4]{0,1:T(4,128)}, u32[]{:S(2)}) copy-start(s32[8,4]{0,1:T(4,128)} %param.11) | copy-start | bytes 388
  21.8 44.4 %copy-start.1 = (f32[768]{0:T(1024)S(1)}, f32[768]{0:T(1024)}, u32[]{:S(2)}) copy-start(f32[768]{0:T(1024)} %param.17) | copy-start | bytes 9220
  57.7 55.7 %all-to-all-start.1 = ((bf16[128,8,768]{2,1,0:T(8,128)(2,1)}), bf16[128,8,768]{2,1,0:T(8,128)(2,1)}, u32[]{:S(2)}, u32[]{:S(2)}) async-start(bf16[128,8,768]{2,1,0:T(8,128)(2,1)} %bitcast_select_fusion), calls=%async_computation.1 | async-start | bytes 3145728 | tf_op jit(solution)/shard_map/all_to_all | solution.py:174

commit v11 on v8

--- a/solution.py
+++ b/solution.py
@@ -95,6 +95,140 @@
         ],
         compiler_params=pltpu.CompilerParams(collective_id=0, has_side_effects=True),
     )(piece)
+
+def scatter_kernel(group, send_ref, out_ref, send_sem, recv_sem, local_sem):
+    served = send_ref.shape[0]
+    me = lax.axis_index(AXES)
+    core = (me // group) % 2
+    my_chip = (me // (2 * group)) * group + me % group
+    parity = (core + my_chip) % 2
+    mesh_ids = pl.DeviceIdType.MESH
+
+    def device(chip, which_core):
+        return ((chip // group) * 2 + which_core) * group + chip % group
+
+    def where(k):
+        return (k // group, k % group)
+
+    def chip_of(m):
+        return (m // 2) * group + (m % 2) * 2 + parity
+
+    def remote(src, dst, send, recv, k):
+        return pltpu.make_async_remote_copy(
+            src_ref=src, dst_ref=dst, send_sem=send, recv_sem=recv,
+            device_id=where(k), device_id_type=mesh_ids,
+        )
+
+    barrier = pltpu.get_barrier_semaphore()
+
+    def greet(m, carry):
+        peer = device(chip_of(m), core)
+
+        @pl.when(peer != me)
+        def _():
+            pl.semaphore_signal(barrier, inc=1, device_id=where(peer), device_id_type=mesh_ids)
+
+        return carry
+
+    lax.fori_loop(0, served, greet, 0)
+
+    pl.semaphore_wait(barrier, served - 1 + core)
+    slot = my_chip // 2
+
+    def send(m, carry):
+        peer = device(chip_of(m), core)
+
+        @pl.when(peer != me)
+        def _():
+            remote(send_ref.at[m], out_ref.at[slot], send_sem.at[m], recv_sem.at[slot], peer).start()
+
+        @pl.when(peer == me)
+        def _():
+            pltpu.make_async_copy(send_ref.at[m], out_ref.at[slot], local_sem).start()
+
+        return carry
+
+    lax.fori_loop(0, served, send, 0)
+
+    def wait(m, carry):
+        sender = device(2 * m + parity, core)
+        peer = device(chip_of(m), core)
+
+        @pl.when(sender != me)
+        def _():
+            remote(send_ref.at[m], out_ref.at[m], send_sem.at[m], recv_sem.at[m], sender).wait_recv()
+
+        @pl.when(sender == me)
+        def _():
+            pltpu.make_async_copy(send_ref.at[m], out_ref.at[m], local_sem).wait()
+
+        @pl.when(peer != me)
+        def _():
+            remote(send_ref.at[m], out_ref.at[slot], send_sem.at[m], recv_sem.at[slot], peer).wait_send()
+
+        return carry
+
+    lax.fori_loop(0, served, wait, 0)
+
+
+def scatter_pieces(send, group):
+    return pl.pallas_call(
+        functools.partial(scatter_kernel, group),
+        out_shape=jax.ShapeDtypeStruct(send.shape, send.dtype),
+        in_specs=[pl.BlockSpec(memory_space=pltpu.VMEM)],
+        out_specs=pl.BlockSpec(memory_space=pltpu.VMEM),
+        scratch_shapes=[
+            pltpu.SemaphoreType.DMA((send.shape[0],)),
+            pltpu.SemaphoreType.DMA((send.shape[0],)),
+            pltpu.SemaphoreType.DMA,
+        ],
+        compiler_params=pltpu.CompilerParams(collective_id=1, has_side_effects=True),
+    )(send)
+
+
+def broadcast_stripes(local_blocks, dense_ids, n, group):
+    block_count, tile_size, width = local_blocks.shape
+    stripe_count = dense_ids.shape[0]
+    piece = stripe_count * tile_size // n
+    chips = n // 2
+    me = lax.axis_index(AXES)
+    row_count = lax.axis_size("row")
+    core = (me // group) % 2
+    my_chip = (me // (2 * group)) * group + me % group
+    parity = (core + my_chip) % 2
+    partner = me + group * (1 - 2 * core)
+    swap = [(r, r ^ 1) for r in range(row_count)]
+
+    def chip_of_device(k):
+        return (k // (2 * group)) * group + k % group
+
+    owners = dense_ids // block_count
+    candidates = local_blocks[dense_ids % block_count].reshape(
+        chips // group, 2, group // 2, 2, piece, width
+    )
+    mine = lax.dynamic_index_in_dim(candidates, parity, 3, keepdims=False)
+    for_partner = lax.dynamic_index_in_dim(candidates, 1 - parity, 3, keepdims=False)
+    from_partner = lax.ppermute(for_partner, "row", swap)
+    z_part = jnp.arange(chips // group, dtype=jnp.int32)[:, None, None]
+    c_part = jnp.arange(2, dtype=jnp.int32)[None, :, None]
+    g_part = jnp.arange(group // 2, dtype=jnp.int32)[None, None, :]
+    piece_ids = (z_part * 2 + c_part) * group + g_part * 2 + parity
+    use_partner = owners[piece_ids * piece // tile_size] == partner
+    chosen = jnp.where(use_partner[..., None, None], from_partner, mine)
+    outgoing = jnp.transpose(chosen, (0, 2, 1, 3, 4)).reshape(chips // 2, 2 * piece, width)
+    arrived = scatter_pieces(outgoing, group).reshape(chips // 2, 2, piece, width)
+
+    def held(which_core):
+        owner_chip = chip_of_device(owners[(me + group * (which_core - core)) * piece // tile_size])
+        slot = lax.dynamic_index_in_dim(arrived, owner_chip // 2, 0, keepdims=False)
+        return owner_chip % 2 == parity, lax.dynamic_index_in_dim(slot, which_core, 0, keepdims=False)
+
+    _, to_partner = held(1 - core)
+    mine_held, my_rows = held(core)
+    got = lax.ppermute(to_partner, "row", swap)
+    my_piece = jnp.where(mine_held, my_rows, got)
+    return gather_pieces(my_piece, n, group).reshape(stripe_count, tile_size, width)
+
 
 def layer_kernel(tiles_per, tile_size, step_blocks, cols_ref, w_ref, bands_ref, sw_ref, inc_ref, weight_ref, bias_ref, out_ref):
     step = pl.program_id(0)
@@ -160,12 +294,7 @@
     piece = stripe_count * tile_size // peer_count
     me = lax.axis_index(AXES)
 
-    candidates = local_blocks[dense_ids % block_count]
-    stripe_pieces = candidates.reshape(peer_count, piece, feature_width)
-
-    stripe_arrived = lax.all_to_all(stripe_pieces, AXES, split_axis=0, concat_axis=0, tiled=True)
-    my_owner = dense_ids[me * piece // tile_size] // block_count
-    my_piece = lax.dynamic_index_in_dim(stripe_arrived, my_owner, 0, keepdims=False)
+    dense_bands = broadcast_stripes(local_blocks, dense_ids, peer_count, group)
 
     outgoing = features[rows_out]
     slot_ids = jnp.arange(slot_count, dtype=jnp.int32)
@@ -173,9 +302,6 @@
     outgoing = jnp.where(live_slots[:, :, None], outgoing, jnp.zeros((), outgoing.dtype))
     arrived = lax.all_to_all(outgoing, AXES, split_axis=0, concat_axis=0, tiled=True)
     incoming_rows = arrived.reshape(peer_count * slot_count, feature_width)
-    dense_bands = gather_pieces(my_piece, peer_count, group).reshape(
-        stripe_count, tile_size, feature_width
-    )
 
     return fused_layer(dense_cols, dense_edge_weights, dense_bands, sparse_w, incoming_rows, weight, bias)
 

time: 131 us -> 140 us (1.069)
  Pallas kernels: 62.4 us -> 96 us
  waiting for transfers between devices: 33 us -> 0.01 us
  local copies, waits for them, and re-layouts: 12.2 us -> 17.5 us
  other arithmetic: 3.71 us -> 8.5 us
  starting transfers between devices: 16.5 us -> 12.4 us
  between operations: 2.75 us -> 5.42 us
    pallas_call x0 -> x1, Pallas kernels: none -> 37.2 us  [scatter_pieces(): pl.pallas_call(functools.partial(scatter_kernel, group), out_shape=jax.Sh...]
    all_to_all x1 -> x0, waiting for transfers between devices: 33 us -> none  [on_device(): lax.all_to_all(stripe_pieces, AXES, split_axis=0, concat_axis=0, tiled=True)]
    all_to_all x1 -> x0, starting transfers between devices: 11.9 us -> none  [on_device(): lax.all_to_all(stripe_pieces, AXES, split_axis=0, concat_axis=0, tiled=True)]
    all_to_all x1, starting transfers between devices: 4.65 us -> 10.6 us  [on_device(): lax.all_to_all(outgoing, AXES, split_axis=0, concat_axis=0, tiled=True)]
    select_n x1 -> x4, other arithmetic: 0.81 us -> 5.54 us  [the longest x1 3.25 us: broadcast_stripes(): chosen = jnp.where(use_partner[..., None, None], from_partner, mine)]
    pallas_call x1, Pallas kernels: 45.2 us -> 41.6 us  [gather_pieces(): pl.pallas_call(functools.partial(gather_kernel, group), out_shape=jax.Sha...]
    dynamic_slice x1 -> x2, local copies, waits for them, and re-layouts: 0.59 us -> 3.96 us  [the longest x1 3.3 us: broadcast_stripes(): mine = lax.dynamic_index_in_dim(candidates, parity, 3, keepdims=False)]
    ppermute x0 -> x2, starting transfers between devices: none -> 1.79 us  [the longest x1 1.42 us: broadcast_stripes(): from_partner = lax.ppermute(for_partner, 'row', swap)]
  transfers between devices with their start and end apart: 2 -> 3, of which waited for: 1 -> 0; matrix products, arithmetic and copies ran while one was open for 9% -> 12% of each run, Pallas kernels for 35% -> 56%
where the time goes in v11:
time: 140 us
  Pallas kernels  96 us (69%)
  local copies, waits for them, and re-layouts  17.5 us (12%)
  starting transfers between devices  12.4 us (9%)
  other arithmetic  8.5 us (6%)
  between operations  5.42 us (4%)
    pallas_call x1, Pallas kernels, gather_pieces(): pl.pallas_call(functools.partial(gather_kernel, group), out_shape=jax.Sha...  41.6 us
    pallas_call x1, Pallas kernels, scatter_pieces(): pl.pallas_call(functools.partial(scatter_kernel, group), out_shape=jax.Sh...  37.2 us
    pallas_call x1, Pallas kernels, fused_layer(): pl.pallas_call(functools.partial(layer_kernel, tiles_per, tile_size, step...  17.3 us
    all_to_all x1, starting transfers between devices, on_device(): lax.all_to_all(outgoing, AXES, split_axis=0, concat_axis=0, tiled=True)  10.6 us
    gather x1, local copies, waits for them, and re-layouts, on_device(): outgoing = features[rows_out]  5.24 us
    dynamic_slice x1, local copies, waits for them, and re-layouts, broadcast_stripes(): mine = lax.dynamic_index_in_dim(candidates, parity, 3, keepdims=False)  3.3 us
    select_n x1, other arithmetic, broadcast_stripes(): chosen = jnp.where(use_partner[..., None, None], from_partner, mine)  3.25 us
  transfers between devices with their start and end apart: 3, of which 0 were waited for; matrix products, arithmetic and copies ran while one was open for 12% of the time, Pallas kernels for 56%

profile of v11, /device:TPU:1, one launch (start us, length us, event | category | flops | bytes accessed | tf_op | source)
XLA Modules:
  0.0 139.9 jit_solution(6717180558735310471)
XLA Ops:
  0.0 0.8 and_select_fusion.2
  0.8 1.1 copy-done
  1.9 2.4 %gather_fusion.1 = bf16[8,256,768]{2,1,0:T(8,128)(2,1)} fusion(bf16[8,256,768]{2,1,0:T(8,128)(2,1)S(1)} %bitcast.30, s32[1024]{0:T(1024)S(1)} %pad_clamp_fusion), kind=kCustom, calls=%fused_computation.1 | custom fusion | bytes 6291488 | tf_op jit(solution)/shard_map/gather | solution.py:206
  4.3 3.3 %constant_dynamic-slice_fusion = (bf16[16,2,2,1,16,768]{5,4,3,2,1,0:T(8,128)(2,1)}, bf16[16,2,2,1,16,768]{5,4,3,2,1,0:T(8,128)(2,1)S(1)}) fusion(bf16[16,2,2,2,16,768]{5,4,3,2,1,0:T(8,128)(2,1)} %bitcast.31, s32[]{:T(128)S(6)} %select_n.166, s32[]{:T(128)S(6)} %select_n.165), kind=kLoop, calls=%fused_computation.26 | loop fusion | bytes 6291464 | tf_op jit(solution)/shard_map/jit(dynamic_index_in_dim)/dynamic_slice | solution.py:209
  7.6 1.3 copy.25
  9.0 1.4 %collective-permute-start = (bf16[16,2,2,16,768]{4,3,1,2,0:T(8,128)(2,1)}, bf16[16,2,2,16,768]{4,3,1,2,0:T(8,128)(2,1)}, u32[]{:S(2)}, u32[]{:S(2)}) collective-permute-start(bf16[16,2,2,16,768]{4,3,1,2,0:T(8,128)(2,1)} %bitcast.29), channel_id=1, source_target_pairs={{0,4},{4,0},{8,12},{12,8},{16,20},{20,16},{24,28},{28,24},{32,36},... | collective-permute-start | bytes 4718600 | tf_op jit(solution)/shard_map/ppermute | solution.py:211
  10.4 0.1 copy.18
  10.5 0.1 reshape.208
  10.6 0.0 copy-start.4
  10.6 5.2 %gather_fusion.2 = bf16[1024,768]{1,0:T(8,128)(2,1)} fusion(bf16[2048,768]{1,0:T(8,128)(2,1)S(1)} %copy-done, s32[1024]{0:T(1024)S(1)} %broadcast_clamp_fusion), kind=kCustom, calls=%fused_computation.2 | custom fusion | bytes 3149824 | tf_op jit(solution)/shard_map/gather | solution.py:299
  15.8 0.1 iota_compare_fusion
  15.9 2.8 %bitcast_select_fusion = bf16[128,8,768]{2,1,0:T(8,128)(2,1)} fusion(bf16[1024,768]{1,0:T(8,128)(2,1)} %gather_fusion.2, pred[128,8]{1,0:T(8,128)(4,1)S(1)} %iota_compare_fusion), kind=kLoop, calls=%fused_computation.6 | loop fusion | flops 786432 | bytes 3146752 | tf_op jit(solution)/shard_map/jit(_where)/select_n | solution.py:302
  18.7 10.6 %all-to-all-start = ((bf16[128,8,768]{2,1,0:T(8,128)(2,1)}), bf16[128,8,768]{2,1,0:T(8,128)(2,1)}, u32[]{:S(2)}, u32[]{:S(2)}) async-start(bf16[128,8,768]{2,1,0:T(8,128)(2,1)} %bitcast_select_fusion), calls=%async_computation | async-start | bytes 3145728 | tf_op jit(solution)/shard_map/all_to_all | solution.py:303
  29.4 0.7 fusion.1
  32.6 0.1 add_multiply_fusion
  32.7 0.1 compare_select_fusion
  32.8 0.1 reshape.192
  33.0 0.8 gather_fusion
  33.8 0.1 reshape.218
  33.9 0.2 copy.15
  34.1 0.0 collective-permute-done
  34.1 3.2 %fusion = bf16[16,2,2,16,768]{4,3,1,2,0:T(8,128)(2,1)} fusion(bf16[16,2,2,16,768]{4,3,1,2,0:T(8,128)(2,1)} %collective-permute-done, bf16[16,2,2,1,16,768]{5,4,3,2,1,0:T(8,128)(2,1)} %get-tuple-element.5, pred[16,2,2]{1,2,0:T(4,128)(4,1)S(1)} %copy.15), kind=kLoop, calls=%fused_computation.4 | loop fusion | flops 786432 | bytes 4718656 | tf_op jit(solution)/shard_map/jit(_where)/select_n | solution.py:217
  37.4 37.2 %shard_map.91 = bf16[32,32,768]{2,1,0:T(8,128)(2,1)} custom-call(bf16[32,32,768]{2,1,0:T(8,128)(2,1)} %bitcast.33), custom_call_target="tpu_custom_call" | custom-call | tf_op jit(solution)/shard_map/pallas_call | solution.py:175
  74.5 0.7 dynamic-slice_bitcast_fusion
  75.3 0.4 collective-permute-start.1
  78.3 0.1 copy.14
  78.4 0.7 reshape.182.cols_ref
  79.0 0.6 reshape.189.bias_ref
  79.6 0.0 collective-permute-done.1
  79.6 1.4 bitcast_select_fusion.1.piece_ref
  81.0 41.6 %shard_map.92 = bf16[128,16,768]{2,1,0:T(8,128)(2,1)} custom-call(bf16[16,768]{1,0:T(8,128)(2,1)} %bitcast_select_fusion.1.piece_ref), custom_call_target="tpu_custom_call" | custom-call | tf_op jit(solution)/shard_map/pallas_call | solution.py:85
  122.6 17.3 %shard_map.93 = bf16[2048,768]{1,0:T(8,128)(2,1)} custom-call(s32[32]{0:T(128)} %reshape.182.cols_ref, bf16[8,4,256,256]{3,2,1,0:T(8,128)(2,1)} %w_ref.1, bf16[8,256,768]{2,1,0:T(8,128)(2,1)} %bitcast.32, bf16[2048,1024]{1,0:T(8,128)(2,1)} %sw_ref.1, bf16[1024,768]{1,0:T(8,128)(2,1)} %bitcast.15.inc_ref, bf16[768,768]{1,0:T(8,128)(2,1)} %weight_ref.1, ...), custom_call_target="tpu_custom_call" | custom-call | tf_op jit(solution)/shard_map/pallas_call | solution.py:265
  (16 shorter events, 0.1 us)
Async XLA Ops:
  0.0 1.9 %copy-start = (bf16[2048,768]{1,0:T(8,128)(2,1)S(1)}, bf16[2048,768]{1,0:T(8,128)(2,1)}, u32[]{:S(2)}) copy-start(bf16[2048,768]{1,0:T(8,128)(2,1)} %param.9) | copy-start | bytes 9437188
  7.6 2.8 %copy-start.2 = (s32[1,128,8]{1,2,0:T(8,128)S(1)}, s32[1,128,8]{1,2,0:T(8,128)}, u32[]{:S(2)}) copy-start(s32[1,128,8]{1,2,0:T(8,128)} %param.14) | copy-start | bytes 12292
  9.0 25.2 %collective-permute-start = (bf16[16,2,2,16,768]{4,3,1,2,0:T(8,128)(2,1)}, bf16[16,2,2,16,768]{4,3,1,2,0:T(8,128)(2,1)}, u32[]{:S(2)}, u32[]{:S(2)}) collective-permute-start(bf16[16,2,2,16,768]{4,3,1,2,0:T(8,128)(2,1)} %bitcast.29), channel_id=1, source_target_pairs={{0,4},{4,0},{8,12},{12,8},{16,20},{20,16},{24,28},{28,24},{32,36},... | collective-permute-start | bytes 4718600 | tf_op jit(solution)/shard_map/ppermute | solution.py:211
  10.6 5.3 %copy-start.4 = (s32[1,128]{1,0:T(1,128)S(1)}, s32[1,128]{1,0:T(1,128)}, u32[]{:S(2)}) copy-start(s32[1,128]{1,0:T(1,128)} %param.15) | copy-start | bytes 1540
  18.7 103.9 %all-to-all-start = ((bf16[128,8,768]{2,1,0:T(8,128)(2,1)}), bf16[128,8,768]{2,1,0:T(8,128)(2,1)}, u32[]{:S(2)}, u32[]{:S(2)}) async-start(bf16[128,8,768]{2,1,0:T(8,128)(2,1)} %bitcast_select_fusion), calls=%async_computation | async-start | bytes 3145728 | tf_op jit(solution)/shard_map/all_to_all | solution.py:303
  37.4 40.9 %copy-start.3 = (s32[8,4]{0,1:T(4,128)S(1)}, s32[8,4]{0,1:T(4,128)}, u32[]{:S(2)}) copy-start(s32[8,4]{0,1:T(4,128)} %param.11) | copy-start | bytes 388
  37.4 41.7 %copy-start.1 = (f32[768]{0:T(1024)S(1)}, f32[768]{0:T(1024)}, u32[]{:S(2)}) copy-start(f32[768]{0:T(1024)} %param.17) | copy-start | bytes 9220
  75.3 4.3 %collective-permute-start.1 = (bf16[16,768]{1,0:T(8,128)(2,1)S(1)}, bf16[16,768]{1,0:T(8,128)(2,1)S(1)}, u32[]{:S(2)}, u32[]{:S(2)}) collective-permute-start(bf16[16,768]{1,0:T(8,128)(2,1)S(1)} %dynamic-slice_bitcast_fusion), channel_id=1, source_target_pairs={{0,4},{4,0},{8,12},{12,8},{16,20},{20,16},{24,28},{28,24},{32,36},... | collective-permute-start | bytes 73736 | tf_op jit(solution)/shard_map/ppermute | solution.py:228

commit v12 on v10

--- a/solution.py
+++ b/solution.py
@@ -102,7 +102,7 @@
         rows = pl.ds(half * tile_size, tile_size)
         total = jnp.dot(sw_ref[rows], inc_ref[...], preferred_element_type=jnp.float32)
         for tile_index in range(tiles_per):
-            col = cols_ref[(step * step_blocks + half) * tiles_per + tile_index]
+            col = cols_ref[tile_index, step * step_blocks + half]
             total = total + jnp.dot(w_ref[half, tile_index], bands_ref[col], preferred_element_type=jnp.float32)
         aggregate = total.astype(jnp.bfloat16)
         result = jnp.dot(aggregate, weight_ref[...], preferred_element_type=jnp.float32) + bias_ref[...]
@@ -132,7 +132,7 @@
         functools.partial(layer_kernel, tiles_per, tile_size, step_blocks),
         grid_spec=grid_spec,
         out_shape=jax.ShapeDtypeStruct((block_count * tile_size, out_width), jnp.bfloat16),
-    )(dense_cols.reshape(-1), dense_edge_weights, dense_bands, sparse_w, incoming_rows, weight, bias.reshape(1, -1))
+    )(dense_cols.T, dense_edge_weights, dense_bands, sparse_w, incoming_rows, weight, bias)
 
 def on_device(
     features,
@@ -164,8 +164,13 @@
     stripe_pieces = candidates.reshape(peer_count, piece, feature_width)
 
     stripe_arrived = lax.all_to_all(stripe_pieces, AXES, split_axis=0, concat_axis=0, tiled=True)
-    my_owner = dense_ids[me * piece // tile_size] // block_count
-    my_piece = lax.dynamic_index_in_dim(stripe_arrived, my_owner, 0, keepdims=False)
+    stripe_ids = jnp.arange(stripe_count, dtype=jnp.int32)
+    my_owner = jnp.sum(jnp.where(stripe_ids == me * piece // tile_size, dense_ids, 0)) // block_count
+    from_owner = jnp.arange(peer_count, dtype=jnp.int32) == my_owner
+    my_piece = jnp.sum(
+        jnp.where(from_owner[:, None, None], stripe_arrived, jnp.zeros((), stripe_arrived.dtype)).astype(jnp.float32),
+        axis=0,
+    ).astype(stripe_arrived.dtype)
 
     outgoing = features[rows_out]
     slot_ids = jnp.arange(slot_count, dtype=jnp.int32)

time: 131 us -> 131 us (level)
  local copies, waits for them, and re-layouts: 12.2 us -> 8.3 us
  other arithmetic: 3.71 us -> 7.43 us
    reduce_sum x0 -> x2, other arithmetic: none -> 4.55 us  [the longest x1 3.08 us: on_device(): jnp.sum(jnp.where(from_owner[:, None, None], stripe_arrived, jnp.zeros(()...]
    squeeze x1 -> x0, local copies, waits for them, and re-layouts: 1.35 us -> none  [on_device(): lax.dynamic_index_in_dim(stripe_arrived, my_owner, 0, keepdims=False)]
where the time goes in v12:
time: 131 us
  Pallas kernels  62.7 us (48%)
  waiting for transfers between devices  33.1 us (25%)
  starting transfers between devices  16.5 us (13%)
  local copies, waits for them, and re-layouts  8.3 us (6%)
  other arithmetic  7.43 us (6%)
  between operations  2.63 us (2%)
    pallas_call x1, Pallas kernels, gather_pieces(): pl.pallas_call(functools.partial(gather_kernel, group), out_shape=jax.Sha...  45.4 us
    all_to_all x1, waiting for transfers between devices, on_device(): lax.all_to_all(stripe_pieces, AXES, split_axis=0, concat_axis=0, tiled=True)  33.1 us
    pallas_call x1, Pallas kernels, fused_layer(): pl.pallas_call(functools.partial(layer_kernel, tiles_per, tile_size, step...  17.3 us
    all_to_all x1, starting transfers between devices, on_device(): lax.all_to_all(stripe_pieces, AXES, split_axis=0, concat_axis=0, tiled=True)  11.9 us
    gather x1, local copies, waits for them, and re-layouts, on_device(): outgoing = features[rows_out]  5.25 us
    all_to_all x1, starting transfers between devices, on_device(): lax.all_to_all(outgoing, AXES, split_axis=0, concat_axis=0, tiled=True)  4.64 us
    reduce_sum x1, other arithmetic, on_device(): jnp.sum(jnp.where(from_owner[:, None, None], stripe_arrived, jnp.zeros(()...  3.08 us
    select_n x1, other arithmetic, on_device(): jnp.where(live_slots[:, :, None], outgoing, jnp.zeros((), outgoing.dtype))  2.77 us
  transfers between devices with their start and end apart: 2, of which 1 were waited for; matrix products, arithmetic and copies ran while one was open for 9% of the time, Pallas kernels for 35%

profile of v12, /device:TPU:1, one launch (start us, length us, event | category | flops | bytes accessed | tf_op | source)
XLA Modules:
  0.0 130.7 jit_solution(16737967281641795789)
XLA Ops:
  0.0 0.0 copy-start
  0.0 1.5 %fusion = (s32[]{:T(128)}, s32[8]{0:T(128)S(1)}) fusion(s32[8]{0:T(128)} %param.12, s32[]{:T(128)S(6)} %select_n.39), kind=kLoop, calls=%fused_computation.13 | loop fusion | flops 135 | bytes 72 | tf_op jit(solution)/shard_map/reduce_sum | solution.py:168
  1.5 0.4 copy-done
  1.9 2.4 %gather_fusion = bf16[8,256,768]{2,1,0:T(8,128)(2,1)} fusion(bf16[8,256,768]{2,1,0:T(8,128)(2,1)S(1)} %bitcast.12, s32[1024]{0:T(1024)S(1)} %pad_clamp_fusion), kind=kCustom, calls=%fused_computation | custom fusion | bytes 6291488 | tf_op jit(solution)/shard_map/gather | solution.py:163
  4.3 0.0 copy-start.1
  4.3 11.9 %all-to-all-start = ((bf16[128,16,768]{2,1,0:T(8,128)(2,1)}), bf16[128,16,768]{2,1,0:T(8,128)(2,1)}, u32[]{:S(2)}, u32[]{:S(2)}) async-start(bf16[128,16,768]{2,1,0:T(8,128)(2,1)} %bitcast.14), calls=%async_computation | async-start | bytes 6291456 | tf_op jit(solution)/shard_map/all_to_all | solution.py:166
  16.2 0.0 copy-done.1
  16.2 0.1 copy.10
  16.4 0.1 reshape.82
  16.5 0.0 copy-start.2
  16.5 5.3 %gather_fusion.1 = bf16[1024,768]{1,0:T(8,128)(2,1)} fusion(bf16[2048,768]{1,0:T(8,128)(2,1)S(1)} %copy-done, s32[1024]{0:T(1024)S(1)} %broadcast_clamp_fusion), kind=kCustom, calls=%fused_computation.1 | custom fusion | bytes 3149824 | tf_op jit(solution)/shard_map/gather | solution.py:175
  21.7 0.0 copy-done.2
  21.7 0.1 iota_compare_fusion
  21.8 2.8 %bitcast_select_fusion = bf16[128,8,768]{2,1,0:T(8,128)(2,1)} fusion(bf16[1024,768]{1,0:T(8,128)(2,1)} %gather_fusion.1, pred[128,8]{1,0:T(8,128)(4,1)S(1)} %iota_compare_fusion), kind=kLoop, calls=%fused_computation.3 | loop fusion | flops 786432 | bytes 3146752 | tf_op jit(solution)/shard_map/jit(_where)/select_n | solution.py:178
  24.6 33.1 %all-to-all-done = bf16[128,16,768]{2,1,0:T(8,128)(2,1)} async-done(((bf16[128,16,768]{2,1,0:T(8,128)(2,1)}), bf16[128,16,768]{2,1,0:T(8,128)(2,1)}, u32[]{:S(2)}, u32[]{:S(2)}) %all-to-all-start) | async-done | bytes 3145760 | tf_op jit(solution)/shard_map/all_to_all | solution.py:166
  57.7 4.6 %all-to-all-start.1 = ((bf16[128,8,768]{2,1,0:T(8,128)(2,1)}), bf16[128,8,768]{2,1,0:T(8,128)(2,1)}, u32[]{:S(2)}, u32[]{:S(2)}) async-start(bf16[128,8,768]{2,1,0:T(8,128)(2,1)} %bitcast_select_fusion), calls=%async_computation.1 | async-start | bytes 3145728 | tf_op jit(solution)/shard_map/all_to_all | solution.py:179
  64.9 3.1 %select_reduce_fusion.piece_ref = bf16[16,768]{1,0:T(8,128)(2,1)} fusion(bf16[128,16,768]{2,1,0:T(8,128)(2,1)} %all-to-all-done, pred[128]{0:T(512)(128)(4,1)S(1)} %iota_compare_fusion.1), kind=kLoop, calls=%fused_computation.2 | loop fusion | flops 3133440 | bytes 3170432 | tf_op jit(solution)/shard_map/reduce_sum | solution.py:170
  68.0 45.4 %shard_map.91 = bf16[128,16,768]{2,1,0:T(8,128)(2,1)} custom-call(bf16[16,768]{1,0:T(8,128)(2,1)} %select_reduce_fusion.piece_ref), custom_call_target="tpu_custom_call" | custom-call | tf_op jit(solution)/shard_map/pallas_call | solution.py:85
  113.4 0.0 all-to-all-done.1
  113.4 17.3 %shard_map.92 = bf16[2048,768]{1,0:T(8,128)(2,1)} custom-call(s32[4,8]{1,0:T(4,128)} %bitcast.15, bf16[8,4,256,256]{3,2,1,0:T(8,128)(2,1)} %w_ref.1, bf16[8,256,768]{2,1,0:T(8,128)(2,1)} %bitcast.13, bf16[2048,1024]{1,0:T(8,128)(2,1)} %sw_ref.1, bf16[1024,768]{1,0:T(8,128)(2,1)} %bitcast.7.inc_ref, bf16[768,768]{1,0:T(8,128)(2,1)} %weight_ref.1, f32[768]{0:T(1024)} %bias_ref.1), custom_call_target="tpu_custom_call" | custom-call | tf_op jit(solution)/shard_map/pallas_call | solution.py:131
  (4 shorter events, 0.0 us)
Async XLA Ops:
  0.0 1.9 %copy-start = (bf16[2048,768]{1,0:T(8,128)(2,1)S(1)}, bf16[2048,768]{1,0:T(8,128)(2,1)}, u32[]{:S(2)}) copy-start(bf16[2048,768]{1,0:T(8,128)(2,1)} %param.9) | copy-start | bytes 9437188
  4.3 11.9 %copy-start.1 = (s32[1,128,8]{1,2,0:T(8,128)S(1)}, s32[1,128,8]{1,2,0:T(8,128)}, u32[]{:S(2)}) copy-start(s32[1,128,8]{1,2,0:T(8,128)} %param.14) | copy-start | bytes 12292
  4.3 53.4 %all-to-all-start = ((bf16[128,16,768]{2,1,0:T(8,128)(2,1)}), bf16[128,16,768]{2,1,0:T(8,128)(2,1)}, u32[]{:S(2)}, u32[]{:S(2)}) async-start(bf16[128,16,768]{2,1,0:T(8,128)(2,1)} %bitcast.14), calls=%async_computation | async-start | bytes 6291456 | tf_op jit(solution)/shard_map/all_to_all | solution.py:166
  16.5 5.3 %copy-start.2 = (s32[1,128]{1,0:T(1,128)S(1)}, s32[1,128]{1,0:T(1,128)}, u32[]{:S(2)}) copy-start(s32[1,128]{1,0:T(1,128)} %param.15) | copy-start | bytes 1540
  57.7 55.7 %all-to-all-start.1 = ((bf16[128,8,768]{2,1,0:T(8,128)(2,1)}), bf16[128,8,768]{2,1,0:T(8,128)(2,1)}, u32[]{:S(2)}, u32[]{:S(2)}) async-start(bf16[128,8,768]{2,1,0:T(8,128)(2,1)} %bitcast_select_fusion), calls=%async_computation.1 | async-start | bytes 3145728 | tf_op jit(solution)/shard_map/all_to_all | solution.py:179

commit v13 on v10

--- a/solution.py
+++ b/solution.py
@@ -95,6 +95,81 @@
         ],
         compiler_params=pltpu.CompilerParams(collective_id=0, has_side_effects=True),
     )(piece)
+
+def dimgather_kernel(group, piece_ref, out_ref, s1, r1, s2, r2, s3, r3, s4, r4, local_sem):
+    Z, X, C, Y = out_ref.shape[:4]
+    me = lax.axis_index(AXES)
+    row = me // group
+    y = me % group
+    core = row % 2
+    x = (row // 2) % X
+    z = row // (2 * X)
+    MESH = pl.DeviceIdType.MESH
+    def did(zz, xx, cc, yy):
+        return ((zz * X + xx) * 2 + cc, yy)
+    def rc(src, dst, ss, rs, dev):
+        return pltpu.make_async_remote_copy(src_ref=src, dst_ref=dst, send_sem=ss, recv_sem=rs, device_id=dev, device_id_type=MESH)
+    barrier = pltpu.get_barrier_semaphore()
+    peers = [did(z, x, core, (y + d) % Y) for d in range(1, Y)] + [did(z, (x + d) % X, core, y) for d in range(1, X)] \
+        + [did((z + d) % Z, x, core, y) for d in range(1, Z)] + [did(z, x, 1 - core, y)]
+    for p in peers:
+        pl.semaphore_signal(barrier, inc=1, device_id=p, device_id_type=MESH)
+    pl.semaphore_wait(barrier, len(peers))
+    own = pltpu.make_async_copy(piece_ref, out_ref.at[z, x, core, y], local_sem)
+    own.start()
+    partner = did(z, x, 1 - core, y)
+    for d in range(1, Y):
+        rc(piece_ref, out_ref.at[z, x, core, y], s1.at[d], r1.at[y], did(z, x, core, (y + d) % Y)).start()
+    for d in range(1, Y):
+        ys = (y + Y - d) % Y
+        rc(piece_ref, out_ref.at[z, x, core, ys], s1.at[d], r1.at[ys], did(z, x, core, ys)).wait_recv()
+    own.wait()
+    for d in range(1, X):
+        rc(out_ref.at[z, x, core], out_ref.at[z, x, core], s2.at[d], r2.at[x], did(z, (x + d) % X, core, y)).start()
+    rc(out_ref.at[z, x, core], out_ref.at[z, x, core], s4.at[z * X + x], r4.at[z * X + x], partner).start()
+    for d in range(1, X):
+        xs = (x + X - d) % X
+        rc(out_ref.at[z, xs, core], out_ref.at[z, xs, core], s2.at[d], r2.at[xs], did(z, xs, core, y)).wait_recv()
+        rc(out_ref.at[z, xs, core], out_ref.at[z, xs, core], s4.at[z * X + xs], r4.at[z * X + xs], partner).start()
+    for d in range(1, Z):
+        for xx in range(X):
+            rc(out_ref.at[z, xx, core], out_ref.at[z, xx, core], s3.at[d * X + xx], r3.at[z * X + xx], did((z + d) % Z, x, core, y)).start()
+    for d in range(1, Z):
+        zs = (z + Z - d) % Z
+        for xx in range(X):
+            rc(out_ref.at[zs, xx, core], out_ref.at[zs, xx, core], s3.at[d * X + xx], r3.at[zs * X + xx], did(zs, x, core, y)).wait_recv()
+            rc(out_ref.at[zs, xx, core], out_ref.at[zs, xx, core], s4.at[zs * X + xx], r4.at[zs * X + xx], partner).start()
+    for zz in range(Z):
+        for xx in range(X):
+            rc(out_ref.at[zz, xx, 1 - core], out_ref.at[zz, xx, 1 - core], s4.at[zz * X + xx], r4.at[zz * X + xx], partner).wait_recv()
+    for d in range(1, Y):
+        rc(piece_ref, out_ref.at[z, x, core, y], s1.at[d], r1.at[y], did(z, x, core, (y + d) % Y)).wait_send()
+    for d in range(1, X):
+        rc(out_ref.at[z, x, core], out_ref.at[z, x, core], s2.at[d], r2.at[x], did(z, (x + d) % X, core, y)).wait_send()
+    for d in range(1, Z):
+        for xx in range(X):
+            rc(out_ref.at[z, xx, core], out_ref.at[z, xx, core], s3.at[d * X + xx], r3.at[z * X + xx], did((z + d) % Z, x, core, y)).wait_send()
+    for zz in range(Z):
+        for xx in range(X):
+            rc(out_ref.at[zz, xx, core], out_ref.at[zz, xx, core], s4.at[zz * X + xx], r4.at[zz * X + xx], partner).wait_send()
+
+def dim_gather(piece, row_count, group):
+    rows, width = piece.shape
+    across = 4 if (row_count // 2) % 4 == 0 else 1
+    depth = row_count // 2 // across
+    sem = pltpu.SemaphoreType.DMA
+    return pl.pallas_call(
+        functools.partial(dimgather_kernel, group),
+        out_shape=jax.ShapeDtypeStruct((depth, across, 2, group, rows, width), piece.dtype),
+        in_specs=[pl.BlockSpec(memory_space=pltpu.VMEM)],
+        out_specs=pl.BlockSpec(memory_space=pltpu.VMEM),
+        scratch_shapes=[
+            sem((group,)), sem((group,)), sem((across,)), sem((across,)),
+            sem((depth * across,)), sem((depth * across,)), sem((depth * across,)), sem((depth * across,)), sem,
+        ],
+        compiler_params=pltpu.CompilerParams(collective_id=0, has_side_effects=True),
+    )(piece)
+
 
 def layer_kernel(tiles_per, tile_size, step_blocks, cols_ref, w_ref, bands_ref, sw_ref, inc_ref, weight_ref, bias_ref, out_ref):
     step = pl.program_id(0)
@@ -173,7 +248,7 @@
     outgoing = jnp.where(live_slots[:, :, None], outgoing, jnp.zeros((), outgoing.dtype))
     arrived = lax.all_to_all(outgoing, AXES, split_axis=0, concat_axis=0, tiled=True)
     incoming_rows = arrived.reshape(peer_count * slot_count, feature_width)
-    dense_bands = gather_pieces(my_piece, peer_count, group).reshape(
+    dense_bands = dim_gather(my_piece, lax.axis_size("row"), group).reshape(
         stripe_count, tile_size, feature_width
     )
 

time: 131 us -> 134 us (1.023)
  Pallas kernels: 62.4 us -> 65.3 us
    pallas_call x1, Pallas kernels: 45.2 us -> 48 us  [dim_gather(): pl.pallas_call(functools.partial(dimgather_kernel, group), out_shape=jax....]
  transfers between devices with their start and end apart: 2 -> 2, of which waited for: 1 -> 1; matrix products, arithmetic and copies ran while one was open for 9% -> 9% of each run, Pallas kernels for 35% -> 36%
where the time goes in v13:
time: 134 us
  Pallas kernels  65.3 us (49%)
  waiting for transfers between devices  33 us (25%)
  starting transfers between devices  16.5 us (12%)
  local copies, waits for them, and re-layouts  12.2 us (9%)
  other arithmetic  3.71 us (3%)
  between operations  2.75 us (2%)
    pallas_call x1, Pallas kernels, dim_gather(): pl.pallas_call(functools.partial(dimgather_kernel, group), out_shape=jax....  48 us
    all_to_all x1, waiting for transfers between devices, on_device(): lax.all_to_all(stripe_pieces, AXES, split_axis=0, concat_axis=0, tiled=True)  33 us
    pallas_call x1, Pallas kernels, fused_layer(): pl.pallas_call(functools.partial(layer_kernel, tiles_per, tile_size, step...  17.3 us
    all_to_all x1, starting transfers between devices, on_device(): lax.all_to_all(stripe_pieces, AXES, split_axis=0, concat_axis=0, tiled=True)  11.9 us
    gather x1, local copies, waits for them, and re-layouts, on_device(): outgoing = features[rows_out]  5.26 us
    all_to_all x1, starting transfers between devices, on_device(): lax.all_to_all(outgoing, AXES, split_axis=0, concat_axis=0, tiled=True)  4.65 us
    select_n x1, other arithmetic, on_device(): jnp.where(live_slots[:, :, None], outgoing, jnp.zeros((), outgoing.dtype))  2.79 us
  transfers between devices with their start and end apart: 2, of which 1 were waited for; matrix products, arithmetic and copies ran while one was open for 9% of the time, Pallas kernels for 36%

profile of v13, /device:TPU:1, one launch (start us, length us, event | category | flops | bytes accessed | tf_op | source)
XLA Modules:
  0.0 133.5 jit_solution(4742815770616294808)
XLA Ops:
  0.0 0.0 copy-start
  0.0 0.8 compare_select_fusion.1
  0.8 1.1 copy-done
  1.9 2.4 %gather_fusion = bf16[8,256,768]{2,1,0:T(8,128)(2,1)} fusion(bf16[8,256,768]{2,1,0:T(8,128)(2,1)S(1)} %bitcast.14, s32[1024]{0:T(1024)S(1)} %pad_clamp_fusion), kind=kCustom, calls=%fused_computation | custom fusion | bytes 6291488 | tf_op jit(solution)/shard_map/gather | solution.py:238
  4.3 0.0 copy-start.2
  4.3 11.9 %all-to-all-start = ((bf16[128,16,768]{2,1,0:T(8,128)(2,1)}), bf16[128,16,768]{2,1,0:T(8,128)(2,1)}, u32[]{:S(2)}, u32[]{:S(2)}) async-start(bf16[128,16,768]{2,1,0:T(8,128)(2,1)} %bitcast.15), calls=%async_computation | async-start | bytes 6291456 | tf_op jit(solution)/shard_map/all_to_all | solution.py:241
  16.2 0.0 copy-done.2
  16.2 0.1 copy.12
  16.4 0.1 reshape.86
  16.5 0.0 copy-start.4
  16.5 5.3 %gather_fusion.1 = bf16[1024,768]{1,0:T(8,128)(2,1)} fusion(bf16[2048,768]{1,0:T(8,128)(2,1)S(1)} %copy-done, s32[1024]{0:T(1024)S(1)} %broadcast_clamp_fusion), kind=kCustom, calls=%fused_computation.1 | custom fusion | bytes 3149824 | tf_op jit(solution)/shard_map/gather | solution.py:245
  21.7 0.0 copy-done.4
  21.7 0.1 iota_compare_fusion
  21.8 0.0 copy-start.5
  21.8 0.0 copy-start.3
  21.8 0.0 copy-start.1
  21.9 2.8 %bitcast_select_fusion = bf16[128,8,768]{2,1,0:T(8,128)(2,1)} fusion(bf16[1024,768]{1,0:T(8,128)(2,1)} %gather_fusion.1, pred[128,8]{1,0:T(8,128)(4,1)S(1)} %iota_compare_fusion), kind=kLoop, calls=%fused_computation.2 | loop fusion | flops 786432 | bytes 3146752 | tf_op jit(solution)/shard_map/jit(_where)/select_n | solution.py:248
  24.6 33.0 %all-to-all-done = bf16[128,16,768]{2,1,0:T(8,128)(2,1)} async-done(((bf16[128,16,768]{2,1,0:T(8,128)(2,1)}), bf16[128,16,768]{2,1,0:T(8,128)(2,1)}, u32[]{:S(2)}, u32[]{:S(2)}) %all-to-all-start) | async-done | bytes 3145760 | tf_op jit(solution)/shard_map/all_to_all | solution.py:241
  57.7 4.6 %all-to-all-start.1 = ((bf16[128,8,768]{2,1,0:T(8,128)(2,1)}), bf16[128,8,768]{2,1,0:T(8,128)(2,1)}, u32[]{:S(2)}, u32[]{:S(2)}) async-start(bf16[128,8,768]{2,1,0:T(8,128)(2,1)} %bitcast_select_fusion), calls=%async_computation.1 | async-start | bytes 3145728 | tf_op jit(solution)/shard_map/all_to_all | solution.py:249
  62.4 0.0 copy-done.5
  62.4 0.6 dynamic_slice.7
  65.6 0.0 copy-done.3
  65.6 0.1 copy.11
  65.6 0.6 reshape.70.cols_ref
  66.3 0.0 copy-done.1
  66.3 0.6 reshape.75.bias_ref
  66.8 1.3 %dynamic-slice_bitcast_fusion.piece_ref = bf16[16,768]{1,0:T(8,128)(2,1)} fusion(bf16[128,16,768]{2,1,0:T(8,128)(2,1)} %all-to-all-done, s32[]{:T(128)S(6)} %select_n.43), kind=kLoop, calls=%fused_computation.4 | loop fusion | bytes 49156 | tf_op jit(solution)/shard_map/jit(dynamic_index_in_dim)/squeeze | solution.py:243
  68.2 48.0 %shard_map.91 = bf16[4,4,2,4,16,768]{5,4,3,2,1,0:T(8,128)(2,1)} custom-call(bf16[16,768]{1,0:T(8,128)(2,1)} %dynamic-slice_bitcast_fusion.piece_ref), custom_call_target="tpu_custom_call" | custom-call | tf_op jit(solution)/shard_map/pallas_call | solution.py:161
  116.2 0.0 all-to-all-done.1
  116.2 17.3 %shard_map.92 = bf16[2048,768]{1,0:T(8,128)(2,1)} custom-call(s32[32]{0:T(128)} %reshape.70.cols_ref, bf16[8,4,256,256]{3,2,1,0:T(8,128)(2,1)} %w_ref.1, bf16[8,256,768]{2,1,0:T(8,128)(2,1)} %bitcast.16, bf16[2048,1024]{1,0:T(8,128)(2,1)} %sw_ref.1, bf16[1024,768]{1,0:T(8,128)(2,1)} %bitcast.8.inc_ref, bf16[768,768]{1,0:T(8,128)(2,1)} %weight_ref.1, ...), custom_call_target="tpu_custom_call" | custom-call | tf_op jit(solution)/shard_map/pallas_call | solution.py:206
  (3 shorter events, 0.0 us)
Async XLA Ops:
  0.0 1.9 %copy-start = (bf16[2048,768]{1,0:T(8,128)(2,1)S(1)}, bf16[2048,768]{1,0:T(8,128)(2,1)}, u32[]{:S(2)}) copy-start(bf16[2048,768]{1,0:T(8,128)(2,1)} %param.9) | copy-start | bytes 9437188
  4.3 11.9 %copy-start.2 = (s32[1,128,8]{1,2,0:T(8,128)S(1)}, s32[1,128,8]{1,2,0:T(8,128)}, u32[]{:S(2)}) copy-start(s32[1,128,8]{1,2,0:T(8,128)} %param.14) | copy-start | bytes 12292
  4.3 53.4 %all-to-all-start = ((bf16[128,16,768]{2,1,0:T(8,128)(2,1)}), bf16[128,16,768]{2,1,0:T(8,128)(2,1)}, u32[]{:S(2)}, u32[]{:S(2)}) async-start(bf16[128,16,768]{2,1,0:T(8,128)(2,1)} %bitcast.15), calls=%async_computation | async-start | bytes 6291456 | tf_op jit(solution)/shard_map/all_to_all | solution.py:241
  16.5 5.3 %copy-start.4 = (s32[1,128]{1,0:T(1,128)S(1)}, s32[1,128]{1,0:T(1,128)}, u32[]{:S(2)}) copy-start(s32[1,128]{1,0:T(1,128)} %param.15) | copy-start | bytes 1540
  21.8 40.5 %copy-start.5 = (s32[8]{0:T(128)S(1)}, s32[8]{0:T(128)}, u32[]{:S(2)}) copy-start(s32[8]{0:T(128)} %param.12) | copy-start | bytes 100
  21.8 43.7 %copy-start.3 = (s32[8,4]{0,1:T(4,128)S(1)}, s32[8,4]{0,1:T(4,128)}, u32[]{:S(2)}) copy-start(s32[8,4]{0,1:T(4,128)} %param.11) | copy-start | bytes 388
  21.8 44.4 %copy-start.1 = (f32[768]{0:T(1024)S(1)}, f32[768]{0:T(1024)}, u32[]{:S(2)}) copy-start(f32[768]{0:T(1024)} %param.17) | copy-start | bytes 9220
  57.7 58.6 %all-to-all-start.1 = ((bf16[128,8,768]{2,1,0:T(8,128)(2,1)}), bf16[128,8,768]{2,1,0:T(8,128)(2,1)}, u32[]{:S(2)}, u32[]{:S(2)}) async-start(bf16[128,8,768]{2,1,0:T(8,128)(2,1)} %bitcast_select_fusion), calls=%async_computation.1 | async-start | bytes 3145728 | tf_op jit(solution)/shard_map/all_to_all | solution.py:249

commit v14 on v10

--- a/solution.py
+++ b/solution.py
@@ -102,7 +102,7 @@
         rows = pl.ds(half * tile_size, tile_size)
         total = jnp.dot(sw_ref[rows], inc_ref[...], preferred_element_type=jnp.float32)
         for tile_index in range(tiles_per):
-            col = cols_ref[(step * step_blocks + half) * tiles_per + tile_index]
+            col = cols_ref[tile_index, step * step_blocks + half]
             total = total + jnp.dot(w_ref[half, tile_index], bands_ref[col], preferred_element_type=jnp.float32)
         aggregate = total.astype(jnp.bfloat16)
         result = jnp.dot(aggregate, weight_ref[...], preferred_element_type=jnp.float32) + bias_ref[...]
@@ -132,7 +132,7 @@
         functools.partial(layer_kernel, tiles_per, tile_size, step_blocks),
         grid_spec=grid_spec,
         out_shape=jax.ShapeDtypeStruct((block_count * tile_size, out_width), jnp.bfloat16),
-    )(dense_cols.reshape(-1), dense_edge_weights, dense_bands, sparse_w, incoming_rows, weight, bias.reshape(1, -1))
+    )(dense_cols.T, dense_edge_weights, dense_bands, sparse_w, incoming_rows, weight, bias)
 
 def on_device(
     features,

time: 131 us -> 131 us (level)
  transfers between devices with their start and end apart: 2 -> 2, of which waited for: 1 -> 1; matrix products, arithmetic and copies ran while one was open for 9% -> 8% of each run, Pallas kernels for 35% -> 36%
where the time goes in v14:
time: 131 us
  Pallas kernels  63.7 us (49%)
  waiting for transfers between devices  33.1 us (25%)
  starting transfers between devices  16.5 us (13%)
  local copies, waits for them, and re-layouts  10.9 us (8%)
  other arithmetic  3.69 us (3%)
  between operations  2.72 us (2%)
    pallas_call x1, Pallas kernels, gather_pieces(): pl.pallas_call(functools.partial(gather_kernel, group), out_shape=jax.Sha...  46.4 us
    all_to_all x1, waiting for transfers between devices, on_device(): lax.all_to_all(stripe_pieces, AXES, split_axis=0, concat_axis=0, tiled=True)  33.1 us
    pallas_call x1, Pallas kernels, fused_layer(): pl.pallas_call(functools.partial(layer_kernel, tiles_per, tile_size, step...  17.3 us
    all_to_all x1, starting transfers between devices, on_device(): lax.all_to_all(stripe_pieces, AXES, split_axis=0, concat_axis=0, tiled=True)  11.9 us
    gather x1, local copies, waits for them, and re-layouts, on_device(): outgoing = features[rows_out]  5.24 us
    all_to_all x1, starting transfers between devices, on_device(): lax.all_to_all(outgoing, AXES, split_axis=0, concat_axis=0, tiled=True)  4.65 us
    select_n x1, other arithmetic, on_device(): jnp.where(live_slots[:, :, None], outgoing, jnp.zeros((), outgoing.dtype))  2.78 us
  transfers between devices with their start and end apart: 2, of which 1 were waited for; matrix products, arithmetic and copies ran while one was open for 8% of the time, Pallas kernels for 36%

profile of v14, /device:TPU:1, one launch (start us, length us, event | category | flops | bytes accessed | tf_op | source)
XLA Modules:
  0.0 130.6 jit_solution(10941439809006781273)
XLA Ops:
  0.0 0.0 copy-start
  0.0 0.8 compare_select_fusion.1
  0.8 1.1 copy-done
  1.9 2.4 %gather_fusion = bf16[8,256,768]{2,1,0:T(8,128)(2,1)} fusion(bf16[8,256,768]{2,1,0:T(8,128)(2,1)S(1)} %bitcast.15, s32[1024]{0:T(1024)S(1)} %pad_clamp_fusion), kind=kCustom, calls=%fused_computation | custom fusion | bytes 6291488 | tf_op jit(solution)/shard_map/gather | solution.py:163
  4.3 0.0 copy-start.1
  4.3 11.9 %all-to-all-start = ((bf16[128,16,768]{2,1,0:T(8,128)(2,1)}), bf16[128,16,768]{2,1,0:T(8,128)(2,1)}, u32[]{:S(2)}, u32[]{:S(2)}) async-start(bf16[128,16,768]{2,1,0:T(8,128)(2,1)} %bitcast.17), calls=%async_computation | async-start | bytes 6291456 | tf_op jit(solution)/shard_map/all_to_all | solution.py:166
  16.2 0.0 copy-done.1
  16.2 0.1 copy.10
  16.4 0.1 reshape.78
  16.5 0.0 copy-start.2
  16.5 5.2 %gather_fusion.1 = bf16[1024,768]{1,0:T(8,128)(2,1)} fusion(bf16[2048,768]{1,0:T(8,128)(2,1)S(1)} %copy-done, s32[1024]{0:T(1024)S(1)} %broadcast_clamp_fusion), kind=kCustom, calls=%fused_computation.1 | custom fusion | bytes 3149824 | tf_op jit(solution)/shard_map/gather | solution.py:170
  21.7 0.0 copy-done.2
  21.7 0.1 iota_compare_fusion
  21.8 0.0 copy-start.3
  21.8 2.8 %bitcast_select_fusion = bf16[128,8,768]{2,1,0:T(8,128)(2,1)} fusion(bf16[1024,768]{1,0:T(8,128)(2,1)} %gather_fusion.1, pred[128,8]{1,0:T(8,128)(4,1)S(1)} %iota_compare_fusion), kind=kLoop, calls=%fused_computation.2 | loop fusion | flops 786432 | bytes 3146752 | tf_op jit(solution)/shard_map/jit(_where)/select_n | solution.py:173
  24.6 33.1 %all-to-all-done = bf16[128,16,768]{2,1,0:T(8,128)(2,1)} async-done(((bf16[128,16,768]{2,1,0:T(8,128)(2,1)}), bf16[128,16,768]{2,1,0:T(8,128)(2,1)}, u32[]{:S(2)}, u32[]{:S(2)}) %all-to-all-start) | async-done | bytes 3145760 | tf_op jit(solution)/shard_map/all_to_all | solution.py:166
  57.7 4.6 %all-to-all-start.1 = ((bf16[128,8,768]{2,1,0:T(8,128)(2,1)}), bf16[128,8,768]{2,1,0:T(8,128)(2,1)}, u32[]{:S(2)}, u32[]{:S(2)}) async-start(bf16[128,8,768]{2,1,0:T(8,128)(2,1)} %bitcast_select_fusion), calls=%async_computation.1 | async-start | bytes 3145728 | tf_op jit(solution)/shard_map/all_to_all | solution.py:174
  62.4 0.0 copy-done.3
  62.4 0.6 dynamic_slice.7
  65.6 1.4 %dynamic-slice_bitcast_fusion.piece_ref = bf16[16,768]{1,0:T(8,128)(2,1)} fusion(bf16[128,16,768]{2,1,0:T(8,128)(2,1)} %all-to-all-done, s32[]{:T(128)S(6)} %select_n.43), kind=kLoop, calls=%fused_computation.4 | loop fusion | bytes 49156 | tf_op jit(solution)/shard_map/jit(dynamic_index_in_dim)/squeeze | solution.py:168
  66.9 46.4 %shard_map.91 = bf16[128,16,768]{2,1,0:T(8,128)(2,1)} custom-call(bf16[16,768]{1,0:T(8,128)(2,1)} %dynamic-slice_bitcast_fusion.piece_ref), custom_call_target="tpu_custom_call" | custom-call | tf_op jit(solution)/shard_map/pallas_call | solution.py:85
  113.3 0.0 all-to-all-done.1
  113.3 17.3 %shard_map.92 = bf16[2048,768]{1,0:T(8,128)(2,1)} custom-call(s32[4,8]{1,0:T(4,128)} %bitcast.18, bf16[8,4,256,256]{3,2,1,0:T(8,128)(2,1)} %w_ref.1, bf16[8,256,768]{2,1,0:T(8,128)(2,1)} %bitcast.16, bf16[2048,1024]{1,0:T(8,128)(2,1)} %sw_ref.1, bf16[1024,768]{1,0:T(8,128)(2,1)} %bitcast.9.inc_ref, bf16[768,768]{1,0:T(8,128)(2,1)} %weight_ref.1, f32[768]{0:T(1024)} %bias_ref.1), custom_call_target="tpu_custom_call" | custom-call | tf_op jit(solution)/shard_map/pallas_call | solution.py:131
  (3 shorter events, 0.0 us)
Async XLA Ops:
  0.0 1.9 %copy-start = (bf16[2048,768]{1,0:T(8,128)(2,1)S(1)}, bf16[2048,768]{1,0:T(8,128)(2,1)}, u32[]{:S(2)}) copy-start(bf16[2048,768]{1,0:T(8,128)(2,1)} %param.9) | copy-start | bytes 9437188
  4.3 11.9 %copy-start.1 = (s32[1,128,8]{1,2,0:T(8,128)S(1)}, s32[1,128,8]{1,2,0:T(8,128)}, u32[]{:S(2)}) copy-start(s32[1,128,8]{1,2,0:T(8,128)} %param.14) | copy-start | bytes 12292
  4.3 53.4 %all-to-all-start = ((bf16[128,16,768]{2,1,0:T(8,128)(2,1)}), bf16[128,16,768]{2,1,0:T(8,128)(2,1)}, u32[]{:S(2)}, u32[]{:S(2)}) async-start(bf16[128,16,768]{2,1,0:T(8,128)(2,1)} %bitcast.17), calls=%async_computation | async-start | bytes 6291456 | tf_op jit(solution)/shard_map/all_to_all | solution.py:166
  16.5 5.3 %copy-start.2 = (s32[1,128]{1,0:T(1,128)S(1)}, s32[1,128]{1,0:T(1,128)}, u32[]{:S(2)}) copy-start(s32[1,128]{1,0:T(1,128)} %param.15) | copy-start | bytes 1540
  21.8 40.6 %copy-start.3 = (s32[8]{0:T(128)S(1)}, s32[8]{0:T(128)}, u32[]{:S(2)}) copy-start(s32[8]{0:T(128)} %param.12) | copy-start | bytes 100
  57.7 55.6 %all-to-all-start.1 = ((bf16[128,8,768]{2,1,0:T(8,128)(2,1)}), bf16[128,8,768]{2,1,0:T(8,128)(2,1)}, u32[]{:S(2)}, u32[]{:S(2)}) async-start(bf16[128,8,768]{2,1,0:T(8,128)(2,1)} %bitcast_select_fusion), calls=%async_computation.1 | async-start | bytes 3145728 | tf_op jit(solution)/shard_map/all_to_all | solution.py:174
